TPU v7x, 32 devices: a whole 2x2x4 slice. The times are simulated.
32 devices in a mesh: ep: 8 (over y, x, core), tp: 4 (over z).
Axes of the slice: x: 2, y: 2, z: 4, core: 2. Of those that a mesh axis runs over, the one named last changes fastest.
Arguments:
- layer_in: bfloat16 [2048, 2048], P('ep', 'tp'), may hold values from -6 to 6
- token_order: int32 [2048], replicated, may hold values from 0 to 2047, as said below
- seq_lengths: int32 [16, 3], P('ep'), may hold values from 1 to 64, 128 in all within a row
- routes: int32 [2048, 8], P('ep'), may hold values from 0 to 15, all different within a row; in each aligned block of 128 rows (0 to 127, 128 to 255, ...) at most 80 rows name the same one
- route_weights: float32 [2048, 8], P('ep'), may hold values from 0.25 to 0.75
- w_query: bfloat16 [2048, 4096], P('ep', 'tp'), may hold values from -0.125 to 0.125
- w_key: bfloat16 [2048, 512], P('ep', 'tp'), may hold values from -0.125 to 0.125
- w_value: bfloat16 [2048, 512], P('ep', 'tp'), may hold values from -0.125 to 0.125
- w_out: bfloat16 [2048, 4096], P('ep', 'tp'), may hold values from -0.5 to 0.5
- norm_attn: bfloat16 [2048], P('ep'), may hold values from 0.5 to 1.5
- norm_moe: bfloat16 [2048], P('ep'), may hold values from 0.5 to 1.5
- query_gain: bfloat16 [128], P('ep'), may hold values from 1 to 1.796875
- key_gain: bfloat16 [128], P('ep'), may hold values from 1 to 1.796875
- w_gate: bfloat16 [16, 768, 2048], P('ep', 'tp'), may hold values from -0.125 to 0.125
- w_up: bfloat16 [16, 768, 2048], P('ep', 'tp'), may hold values from -0.125 to 0.125
- w_down: bfloat16 [16, 768, 2048], P('ep', 'tp'), may hold values from -0.3125 to 0.3125
- grad_out: bfloat16 [2048, 2048], P('ep', 'tp'), may hold values from -6 to 6
Outputs:
- layer_out: bfloat16 [2048, 2048], P('ep', 'tp')
- grad_layer_in: float32 [2048, 2048], P('ep', 'tp')
- grad_w_query: float32 [2048, 4096], P('ep', 'tp')
- grad_w_key: float32 [2048, 512], P('ep', 'tp')
- grad_w_value: float32 [2048, 512], P('ep', 'tp')
- grad_w_out: float32 [2048, 4096], P('ep', 'tp')
- grad_norm_attn: float32 [2048], P('ep')
- grad_norm_moe: float32 [2048], P('ep')
- grad_query_gain: float32 [128], P('ep')
- grad_key_gain: float32 [128], P('ep')
- grad_w_gate: float32 [16, 768, 2048], P('ep', 'tp')
- grad_w_up: float32 [16, 768, 2048], P('ep', 'tp')
- grad_w_down: float32 [16, 768, 2048], P('ep', 'tp')
Inputs may be any that keep to these rules, and one draw needn't show every extreme that they name: `token_order`: each row number appears once. Of the 256 dealt rows of one index of ep, exactly 32 are rows of each index of ep. `seq_lengths`: row b holds the lengths of the 3 sequences of block b of 128 dealt rows, in order; they sum to 128, and the longest is 64. `routes`: each row names 8 different experts. Within each aligned block of 128 dealt rows (one micro-batch of one index of ep) no expert is named by more than 80 rows; in some blocks one is named by exactly 80.
All inputs are finite; a program needn't handle non-finite values.
Results may differ from a plain program's by a relative error of at most 0.023.
Values may be sent and summed in bfloat16 or wider, within the bound.
A program may use at most 256 MiB of HBM per device.

v0:
```python
import jax
import jax.numpy as jnp
from jax import lax
from jax.sharding import PartitionSpec as P

HEAD_DIM = 128
MICRO = 2


epsilon = 1e-06
rope_base = 1000000.0


def positions_of(lengths, row_count):
    offsets = jnp.arange(row_count, dtype=jnp.int32)
    seq_ends = jnp.cumsum(lengths)
    segment = jnp.sum((offsets[:, None] >= seq_ends[None, :]).astype(jnp.int32), axis=1)
    starts = seq_ends - lengths
    in_segment = segment[:, None] == jnp.arange(lengths.shape[0], dtype=jnp.int32)[None, :]
    position = offsets - jnp.sum(jnp.where(in_segment, starts[None, :], 0), axis=1)
    return (segment, position)


def rope_tables(position, half_dim):
    frequency = rope_base ** (-jnp.arange(half_dim, dtype=jnp.float32) / half_dim)
    angles = position.astype(jnp.float32)[:, None] * frequency[None, :]
    return (jnp.cos(angles)[:, None, :], jnp.sin(angles)[:, None, :])


def rotate(values, cosine, sine_table):
    half_dim = values.shape[-1] // 2
    first_half = values[..., :half_dim]
    second_half = values[..., half_dim:]
    return jnp.concatenate(
        [
            first_half * cosine - second_half * sine_table,
            second_half * cosine + first_half * sine_table,
        ],
        axis=-1,
    )


def rotate_back(incoming, cosine, sine_table):
    half_dim = incoming.shape[-1] // 2
    first_half = incoming[..., :half_dim]
    second_half = incoming[..., half_dim:]
    return jnp.concatenate(
        [
            first_half * cosine + second_half * sine_table,
            second_half * cosine - first_half * sine_table,
        ],
        axis=-1,
    )


def slot_tables(routes, experts, capacity, top_count):
    flat_routes = routes.reshape(-1)
    route_count = flat_routes.shape[0]
    onehot = (flat_routes[:, None] == jnp.arange(experts, dtype=jnp.int32)[None, :]).astype(
        jnp.float32
    )
    counter = jnp.arange(route_count, dtype=jnp.int32)
    earlier = (counter[None, :] < counter[:, None]).astype(jnp.float32)
    before = jnp.dot(earlier, onehot, preferred_element_type=jnp.float32)
    slot_index = jnp.sum(before * onehot, axis=1).astype(jnp.int32)
    target = flat_routes * capacity + slot_index
    token_of = counter // top_count
    source = jnp.zeros((experts * capacity,), jnp.int32).at[target].set(token_of)
    return (target, source)


def deal_tables(token_order, ep_count, ep_index, rows_dev):
    per_pair = rows_dev // ep_count
    order_grid = token_order.reshape(ep_count, rows_dev)
    source_grid = order_grid // rows_dev
    mine = (source_grid == ep_index).astype(jnp.int32)
    rank_mine = jnp.cumsum(mine, axis=1) - mine
    slot_rank = jnp.where(mine == 1, rank_mine, per_pair)
    dest_index = jnp.broadcast_to(
        jnp.arange(ep_count, dtype=jnp.int32)[:, None], (ep_count, rows_dev)
    )
    local_row = order_grid - ep_index * rows_dev
    send_table = (
        jnp.zeros((ep_count, per_pair), jnp.int32)
        .at[dest_index, slot_rank]
        .set(local_row, mode="drop")
        .reshape(-1)
    )
    my_order = lax.dynamic_slice_in_dim(token_order, ep_index * rows_dev, rows_dev, 0)
    my_source = my_order // rows_dev
    onehot = (my_source[:, None] == jnp.arange(ep_count, dtype=jnp.int32)[None, :]).astype(
        jnp.int32
    )
    before = jnp.cumsum(onehot, axis=0) - onehot
    my_rank = jnp.sum(before * onehot, axis=1)
    recv_index = my_source * per_pair + my_rank
    return (send_table, recv_index)


def inverse_rms(values):
    return lax.rsqrt(jnp.mean(values * values, axis=-1, keepdims=True) + epsilon)


def norm_back(grad_unit, unit_values, inverse):
    return inverse * (
        grad_unit - unit_values * jnp.mean(grad_unit * unit_values, axis=-1, keepdims=True)
    )


def contract_rows(left_rows, right_rows):
    return lax.dot_general(
        left_rows, right_rows, (((0,), (0,)), ((), ())), preferred_element_type=jnp.float32
    )


def times_transposed(left_rows, right_matrix):
    return lax.dot_general(
        left_rows, right_matrix, (((1,), (1,)), ((), ())), preferred_element_type=jnp.float32
    )


def fetch_weights(w_query, w_key, w_value, w_out, norm_attn, norm_moe, query_gain, key_gain):
    return (
        lax.all_gather(w_query, "ep", axis=0, tiled=True),
        lax.all_gather(w_key, "ep", axis=0, tiled=True),
        lax.all_gather(w_value, "ep", axis=0, tiled=True),
        lax.all_gather(w_out, "ep", axis=0, tiled=True),
        lax.all_gather(norm_attn, "ep", axis=0, tiled=True),
        lax.all_gather(norm_moe, "ep", axis=0, tiled=True),
        lax.all_gather(query_gain, "ep", axis=0, tiled=True),
        lax.all_gather(key_gain, "ep", axis=0, tiled=True),
    )


def to_owner(routed):
    return lax.all_to_all(routed, "ep", split_axis=0, concat_axis=0, tiled=True)


def owner_total(partial_value):
    return lax.psum_scatter(partial_value, "tp", scatter_dimension=3, tiled=True).astype(
        jnp.bfloat16
    )


def to_anchor(results):
    return lax.all_to_all(results, "ep", split_axis=0, concat_axis=0, tiled=True)


def on_device(
    layer_in,
    token_order,
    seq_lengths,
    routes,
    route_weights,
    w_query,
    w_key,
    w_value,
    w_out,
    norm_attn,
    norm_moe,
    query_gain,
    key_gain,
    w_gate,
    w_up,
    w_down,
    grad_out,
):
    ep_count = lax.axis_size("ep")
    tp_count = lax.axis_size("tp")
    tp_index = lax.axis_index("tp")
    ep_index = lax.axis_index("ep")
    local_experts = w_gate.shape[0]
    experts = local_experts * ep_count
    rows_dev = layer_in.shape[0]
    micro_rows = rows_dev // MICRO
    top_count = routes.shape[1]
    capacity = 5 * micro_rows * top_count // (4 * experts)
    share_width = layer_in.shape[1]
    model_width = share_width * tp_count
    score_scale = HEAD_DIM ** (-0.5)
    per_pair = rows_dev // ep_count
    send_table, recv_index = deal_tables(token_order, ep_count, ep_index, rows_dev)
    send_in = jnp.take(layer_in, send_table, axis=0).reshape(ep_count, per_pair, share_width)
    send_grad = jnp.take(grad_out, send_table, axis=0).reshape(ep_count, per_pair, share_width)
    got_in, got_grad = (
        lax.all_to_all(send_in, "ep", split_axis=0, concat_axis=0, tiled=True),
        lax.all_to_all(send_grad, "ep", split_axis=0, concat_axis=0, tiled=True),
    )
    dealt_in = jnp.take(got_in.reshape(rows_dev, share_width), recv_index, axis=0)
    dealt_grad = jnp.take(got_grad.reshape(rows_dev, share_width), recv_index, axis=0)
    acc_query = jnp.zeros((model_width, w_query.shape[1]), jnp.float32)
    acc_key = jnp.zeros((model_width, w_key.shape[1]), jnp.float32)
    acc_value = jnp.zeros((model_width, w_value.shape[1]), jnp.float32)
    acc_out = jnp.zeros((model_width, w_out.shape[1]), jnp.float32)
    acc_norm_attn = jnp.zeros((model_width,), jnp.float32)
    acc_norm_moe = jnp.zeros((model_width,), jnp.float32)
    acc_query_gain = jnp.zeros((HEAD_DIM,), jnp.float32)
    acc_key_gain = jnp.zeros((HEAD_DIM,), jnp.float32)
    acc_gate = jnp.zeros(w_gate.shape, jnp.float32)
    acc_up = jnp.zeros(w_up.shape, jnp.float32)
    acc_down = jnp.zeros(w_down.shape, jnp.float32)
    outputs = []
    input_grads = []
    for micro_step in range(MICRO):
        gathered = fetch_weights(
            w_query, w_key, w_value, w_out, norm_attn, norm_moe, query_gain, key_gain
        )
        full_query, full_key, full_value, full_out, gain_attn, gain_moe, gain_query, gain_key = (
            gathered
        )
        gain_attn = gain_attn.astype(jnp.float32)
        gain_moe = gain_moe.astype(jnp.float32)
        gain_query = gain_query.astype(jnp.float32)
        gain_key = gain_key.astype(jnp.float32)
        heads_here = full_query.shape[1] // HEAD_DIM
        kv_here = full_key.shape[1] // HEAD_DIM
        group_size = heads_here // kv_here
        row_start = micro_step * micro_rows
        layer_rows = dealt_in[row_start : row_start + micro_rows]
        grad_rows = dealt_grad[row_start : row_start + micro_rows]
        route_rows = routes[row_start : row_start + micro_rows]
        weight_rows = route_weights[row_start : row_start + micro_rows]
        layer_full, grad_full = (
            lax.all_gather(layer_rows, "tp", axis=1, tiled=True),
            lax.all_gather(grad_rows, "tp", axis=1, tiled=True),
        )
        segment, position = positions_of(seq_lengths[micro_step], micro_rows)
        cosine, sine_table = rope_tables(position, HEAD_DIM // 2)
        layer_float = layer_full.astype(jnp.float32)
        inverse_one = inverse_rms(layer_float)
        unit_one = layer_float * inverse_one
        normed = (unit_one * gain_attn).astype(jnp.bfloat16)
        query_proj = jnp.dot(normed, full_query, preferred_element_type=jnp.float32).reshape(
            micro_rows, heads_here, HEAD_DIM
        )
        key_proj = jnp.dot(normed, full_key, preferred_element_type=jnp.float32).reshape(
            micro_rows, kv_here, HEAD_DIM
        )
        value_proj = jnp.dot(normed, full_value, preferred_element_type=jnp.float32).reshape(
            micro_rows, kv_here, HEAD_DIM
        )
        inverse_query = inverse_rms(query_proj)
        unit_query = query_proj * inverse_query
        inverse_key = inverse_rms(key_proj)
        unit_key = key_proj * inverse_key
        queries = (
            rotate(unit_query * gain_query, cosine, sine_table)
            .astype(jnp.bfloat16)
            .reshape(micro_rows, kv_here, group_size, HEAD_DIM)
        )
        key_rows = rotate(unit_key * gain_key, cosine, sine_table).astype(jnp.bfloat16)
        values = value_proj.astype(jnp.bfloat16)
        scores = (
            jnp.einsum("qkgd,tkd->kgqt", queries, key_rows, preferred_element_type=jnp.float32)
            * score_scale
        )
        offsets = jnp.arange(micro_rows, dtype=jnp.int32)
        allowed = (segment[:, None] == segment[None, :]) & (offsets[None, :] <= offsets[:, None])
        scores = jnp.where(allowed, scores, -1e30)
        row_peak = jnp.max(scores, axis=-1, keepdims=True)
        exponent = jnp.exp(scores - row_peak)
        attn_probs = exponent / jnp.sum(exponent, axis=-1, keepdims=True)
        probs_low = attn_probs.astype(jnp.bfloat16)
        context = jnp.einsum(
            "kgqt,tkd->qkgd", probs_low, values, preferred_element_type=jnp.float32
        )
        context_low = context.reshape(micro_rows, heads_here * HEAD_DIM).astype(jnp.bfloat16)
        attn_part = times_transposed(context_low, full_out)
        attn_out = lax.psum(attn_part, "tp")
        hidden = layer_float + attn_out
        inverse_two = inverse_rms(hidden)
        unit_two = hidden * inverse_two
        moe_in = (unit_two * gain_moe).astype(jnp.bfloat16)
        target, source = slot_tables(route_rows, experts, capacity, top_count)
        route_scale = (
            jnp.zeros((experts * capacity,), jnp.float32).at[target].set(weight_rows.reshape(-1))
        )
        sending = jnp.take(moe_in, source, axis=0).reshape(
            ep_count, local_experts, capacity, model_width
        )
        arrived = to_owner(sending)
        gate_pre = jnp.einsum("secd,efd->secf", arrived, w_gate, preferred_element_type=jnp.float32)
        up_pre = jnp.einsum("secd,efd->secf", arrived, w_up, preferred_element_type=jnp.float32)
        sigmoid_gate = jax.nn.sigmoid(gate_pre)
        silu_gate = gate_pre * sigmoid_gate
        active = (silu_gate * up_pre).astype(jnp.bfloat16)
        down_part = jnp.einsum("secf,efd->secd", active, w_down, preferred_element_type=jnp.float32)
        expert_rows = owner_total(down_part)
        returned = to_anchor(expert_rows).reshape(experts * capacity, share_width)
        picked = (
            jnp.take(returned, target, axis=0)
            .reshape(micro_rows, top_count, share_width)
            .astype(jnp.float32)
        )
        mixed = jnp.sum(weight_rows[:, :, None] * picked, axis=1)
        hidden_share = lax.dynamic_slice_in_dim(hidden, tp_index * share_width, share_width, 1)
        outputs.append((hidden_share + mixed).astype(jnp.bfloat16))
        grad_float = grad_full.astype(jnp.float32)
        grad_sending = (
            jnp.take(grad_full, source, axis=0).astype(jnp.float32) * route_scale[:, None]
        ).astype(jnp.bfloat16)
        grad_arrived = to_owner(
            grad_sending.reshape(ep_count, local_experts, capacity, model_width)
        )
        grad_active = jnp.einsum(
            "secd,efd->secf", grad_arrived, w_down, preferred_element_type=jnp.float32
        )
        acc_down = acc_down + jnp.einsum(
            "secf,secd->efd", active, grad_arrived, preferred_element_type=jnp.float32
        )
        grad_up_pre = (grad_active * silu_gate).astype(jnp.bfloat16)
        grad_gate_pre = (
            grad_active * up_pre * sigmoid_gate * (1.0 + gate_pre * (1.0 - sigmoid_gate))
        ).astype(jnp.bfloat16)
        acc_gate = acc_gate + jnp.einsum(
            "secf,secd->efd", grad_gate_pre, arrived, preferred_element_type=jnp.float32
        )
        acc_up = acc_up + jnp.einsum(
            "secf,secd->efd", grad_up_pre, arrived, preferred_element_type=jnp.float32
        )
        grad_partial = jnp.einsum(
            "secf,efd->secd", grad_gate_pre, w_gate, preferred_element_type=jnp.float32
        ) + jnp.einsum("secf,efd->secd", grad_up_pre, w_up, preferred_element_type=jnp.float32)
        grad_rows_out = owner_total(grad_partial)
        grad_back = to_anchor(grad_rows_out).reshape(experts * capacity, share_width)
        grad_moe_share = jnp.sum(
            jnp.take(grad_back, target, axis=0)
            .reshape(micro_rows, top_count, share_width)
            .astype(jnp.float32),
            axis=1,
        )
        grad_moe_in = lax.all_gather(grad_moe_share, "tp", axis=1, tiled=True)
        acc_norm_moe = acc_norm_moe + jnp.sum(grad_moe_in * unit_two, axis=0)
        grad_hidden = grad_float + norm_back(grad_moe_in * gain_moe, unit_two, inverse_two)
        grad_attn = grad_hidden.astype(jnp.bfloat16)
        acc_out = acc_out + contract_rows(grad_attn, context_low)
        grad_context = (
            jnp.dot(grad_attn, full_out, preferred_element_type=jnp.float32)
            .astype(jnp.bfloat16)
            .reshape(micro_rows, kv_here, group_size, HEAD_DIM)
        )
        grad_probs = jnp.einsum(
            "qkgd,tkd->kgqt", grad_context, values, preferred_element_type=jnp.float32
        )
        prob_delta = jnp.sum(attn_probs * grad_probs, axis=-1, keepdims=True)
        grad_scores = (attn_probs * (grad_probs - prob_delta)).astype(jnp.bfloat16)
        grad_queries = (
            jnp.einsum(
                "kgqt,tkd->qkgd", grad_scores, key_rows, preferred_element_type=jnp.float32
            ).reshape(micro_rows, heads_here, HEAD_DIM)
            * score_scale
        )
        grad_keys = (
            jnp.einsum("kgqt,qkgd->tkd", grad_scores, queries, preferred_element_type=jnp.float32)
            * score_scale
        )
        grad_values = jnp.einsum(
            "kgqt,qkgd->tkd", probs_low, grad_context, preferred_element_type=jnp.float32
        )
        grad_unit_query = rotate_back(grad_queries, cosine, sine_table)
        grad_unit_key = rotate_back(grad_keys, cosine, sine_table)
        query_gain_part = jnp.sum(grad_unit_query * unit_query, axis=(0, 1))
        key_gain_part = jnp.sum(grad_unit_key * unit_key, axis=(0, 1))
        grad_query_proj = (
            norm_back(grad_unit_query * gain_query, unit_query, inverse_query)
            .reshape(micro_rows, heads_here * HEAD_DIM)
            .astype(jnp.bfloat16)
        )
        grad_key_proj = (
            norm_back(grad_unit_key * gain_key, unit_key, inverse_key)
            .reshape(micro_rows, kv_here * HEAD_DIM)
            .astype(jnp.bfloat16)
        )
        grad_value_proj = grad_values.reshape(micro_rows, kv_here * HEAD_DIM).astype(jnp.bfloat16)
        acc_query = acc_query + contract_rows(normed, grad_query_proj)
        acc_key = acc_key + contract_rows(normed, grad_key_proj)
        acc_value = acc_value + contract_rows(normed, grad_value_proj)
        normed_part = (
            times_transposed(grad_query_proj, full_query)
            + times_transposed(grad_key_proj, full_key)
            + times_transposed(grad_value_proj, full_value)
        )
        grad_normed, query_gain_sum, key_gain_sum = (
            lax.psum(normed_part.astype(jnp.bfloat16), "tp").astype(jnp.float32),
            lax.psum(query_gain_part.astype(jnp.bfloat16), "tp").astype(jnp.float32),
            lax.psum(key_gain_part.astype(jnp.bfloat16), "tp").astype(jnp.float32),
        )
        acc_query_gain = acc_query_gain + query_gain_sum
        acc_key_gain = acc_key_gain + key_gain_sum
        acc_norm_attn = acc_norm_attn + jnp.sum(grad_normed * unit_one, axis=0)
        grad_layer = grad_hidden + norm_back(grad_normed * gain_attn, unit_one, inverse_one)
        input_grads.append(
            lax.dynamic_slice_in_dim(grad_layer, tp_index * share_width, share_width, 1)
        )
    summed = (
        lax.psum_scatter(
            acc_query.astype(jnp.bfloat16), "ep", scatter_dimension=0, tiled=True
        ).astype(jnp.float32),
        lax.psum_scatter(
            acc_key.astype(jnp.bfloat16), "ep", scatter_dimension=0, tiled=True
        ).astype(jnp.float32),
        lax.psum_scatter(
            acc_value.astype(jnp.bfloat16), "ep", scatter_dimension=0, tiled=True
        ).astype(jnp.float32),
        lax.psum_scatter(
            acc_out.astype(jnp.bfloat16), "ep", scatter_dimension=0, tiled=True
        ).astype(jnp.float32),
        lax.psum_scatter(
            acc_norm_attn.astype(jnp.bfloat16), "ep", scatter_dimension=0, tiled=True
        ).astype(jnp.float32),
        lax.psum_scatter(
            acc_norm_moe.astype(jnp.bfloat16), "ep", scatter_dimension=0, tiled=True
        ).astype(jnp.float32),
        lax.psum_scatter(
            acc_query_gain.astype(jnp.bfloat16), "ep", scatter_dimension=0, tiled=True
        ).astype(jnp.float32),
        lax.psum_scatter(
            acc_key_gain.astype(jnp.bfloat16), "ep", scatter_dimension=0, tiled=True
        ).astype(jnp.float32),
    )
    layer_dealt = jnp.concatenate(outputs, axis=0).astype(jnp.float32)
    grad_dealt = jnp.concatenate(input_grads, axis=0)
    back_table = (
        jnp.zeros((rows_dev,), jnp.int32).at[recv_index].set(jnp.arange(rows_dev, dtype=jnp.int32))
    )
    send_out = jnp.take(layer_dealt, back_table, axis=0).reshape(ep_count, per_pair, share_width)
    send_back = jnp.take(grad_dealt, back_table, axis=0).reshape(ep_count, per_pair, share_width)
    home_out, home_grad = (
        lax.all_to_all(
            send_out.astype(jnp.bfloat16), "ep", split_axis=0, concat_axis=0, tiled=True
        ).astype(send_out.dtype),
        lax.all_to_all(
            send_back.astype(jnp.bfloat16), "ep", split_axis=0, concat_axis=0, tiled=True
        ).astype(send_back.dtype),
    )
    home_table = (
        jnp.zeros((rows_dev,), jnp.int32).at[send_table].set(jnp.arange(rows_dev, dtype=jnp.int32))
    )
    layer_out = jnp.take(home_out.reshape(rows_dev, share_width), home_table, axis=0).astype(
        jnp.bfloat16
    )
    grad_layer_in = jnp.take(home_grad.reshape(rows_dev, share_width), home_table, axis=0)
    return (
        layer_out,
        grad_layer_in,
        summed[0],
        summed[1],
        summed[2],
        summed[3],
        summed[4],
        summed[5],
        summed[6],
        summed[7],
        acc_gate,
        acc_up,
        acc_down,
    )


def solution(mesh):
    return jax.shard_map(
        on_device,
        mesh=mesh,
        in_specs=(
            P("ep", "tp"),
            P(),
            P("ep", None),
            P("ep", None),
            P("ep", None),
            P("ep", "tp"),
            P("ep", "tp"),
            P("ep", "tp"),
            P("ep", "tp"),
            P("ep"),
            P("ep"),
            P("ep"),
            P("ep"),
            P("ep", "tp", None),
            P("ep", "tp", None),
            P("ep", "tp", None),
            P("ep", "tp"),
        ),
        out_specs=(
            P("ep", "tp"),
            P("ep", "tp"),
            P("ep", "tp"),
            P("ep", "tp"),
            P("ep", "tp"),
            P("ep", "tp"),
            P("ep"),
            P("ep"),
            P("ep"),
            P("ep"),
            P("ep", "tp", None),
            P("ep", "tp", None),
            P("ep", "tp", None),
        ),
        check_vma=False,
    )
```

profile of v0, /device:TPU:0, one launch (start us, length us, event | category | flops | bytes accessed | tf_op | source)
XLA Modules:
  0.0 1614.2 jit_solution(9810889341020071675)
XLA Ops:
  12.5 8.0 scatter_custom_fusion.6
  39.2 12.8 all_gather.53
  53.4 10.3 all_gather.52
  64.4 8.5 all-gather
  74.7 14.0 all-reduce.8
  106.7 15.4 all_gather.60
  122.1 6.2 gather_fusion.10
  128.3 6.2 multiply_convert_fusion.1
  139.3 16.9 %all_gather.59 = bf16[128,2048]{1,0:T(8,128)(2,1)S(1)} all-gather(bf16[128,512]{1,0:T(8,128)(2,1)S(1)} %get-tuple-element.82), channel_id=1, replica_groups=mesh['ep'=8,'tp'=4] {'tp'}, dimensions={1}, use_global_device_ids=true | all-gather | bytes 655360 | tf_op jit(solution)/shard_map/all_gather | solution.py:224
  156.4 16.0 all_gather.50
  206.0 9.5 all-gather.1
  215.4 77.4 %all-reduce.14.cloned.1.call-done = (f32[128,2048]{1,0:T(8,128)}, f32[128,2048]{1,0:T(8,128)}) async-done(((f32[128,2048]{1,0:T(8,128)}, f32[128,2048]{1,0:T(8,128)}), (f32[128,2048]{1,0:T(8,128)}, f32[128,2048]{1,0:T(8,128)})) %all-reduce.14.cloned.1.call-update) | async-done | bytes 2097168 | tf_op jit(solution)/shard_map/psum | solution.py:269
  295.4 6.2 gather_fusion.2
  301.6 5.4 broadcast_select_fusion.1
  311.7 5.6 fusion.72
  317.3 54.7 %all-to-all-done.1 = bf16[8,2,80,2048]{3,2,1,0:T(8,128)(2,1)} async-done(((bf16[8,2,80,2048]{3,2,1,0:T(8,128)(2,1)}), bf16[8,2,80,2048]{3,2,1,0:T(8,128)(2,1)}, u32[]{:S(2)}, u32[]{:S(2)}) %all-to-all-start.1) | async-done | bytes 5242912 | tf_op jit(solution)/shard_map/all_to_all | solution.py:136
  382.9 5.4 add_bitcast_fusion.1
  388.5 7.1 convolution_bitcast_fusion.1
  395.6 168.4 %reduce-scatter.13.cloned.1.call-done = f32[8,2,80,512]{3,2,0,1:T(8,128)} async-done(((f32[8,2,80,2048]{3,2,0,1:T(8,128)}), f32[8,2,80,512]{3,2,0,1:T(8,128)}) %reduce-scatter.13.cloned.1.call-update) | async-done | bytes 2621456 | tf_op jit(solution)/shard_map/reduce_scatter | solution.py:140
  582.4 23.3 %all_gather.62 = bf16[128,2048]{1,0:T(8,128)(2,1)S(1)} all-gather(bf16[128,512]{1,0:T(8,128)(2,1)S(1)} %copy-done.75), channel_id=1, replica_groups=mesh['ep'=8,'tp'=4] {'tp'}, dimensions={1}, use_global_device_ids=true | all-gather | bytes 655360 | tf_op jit(solution)/shard_map/all_gather | solution.py:225
  605.7 6.1 gather_fusion.12
  611.8 142.0 %reduce-scatter.9.cloned.1.call-done = f32[8,2,80,512]{3,2,0,1:T(8,128)} async-done(((f32[8,2,80,2048]{3,2,0,1:T(8,128)}), f32[8,2,80,512]{3,2,0,1:T(8,128)}) %reduce-scatter.9.cloned.1.call-update) | async-done | bytes 2621456 | tf_op jit(solution)/shard_map/reduce_scatter | solution.py:140
  761.2 6.1 multiply_convert_fusion
  767.2 12.1 all-to-all-done.2
  784.3 6.6 gather_fusion.11
  790.9 6.6 gather_fusion.3
  803.6 27.2 %all-gather.11.cloned.1.call-done = f32[128,2048]{1,0:T(8,128)} async-done(((f32[128,512]{1,0:T(8,128)}), f32[128,2048]{1,0:T(8,128)}) %all-gather.11.cloned.1.call-update) | async-done | bytes 1048592 | tf_op jit(solution)/shard_map/all_gather | solution.py:332
  836.5 6.1 gather_fusion.4
  852.8 5.6 fusion.77
  858.3 54.5 %all-to-all-done.3 = bf16[8,2,80,2048]{3,2,1,0:T(8,128)(2,1)} async-done(((bf16[8,2,80,2048]{3,2,1,0:T(8,128)(2,1)}), bf16[8,2,80,2048]{3,2,1,0:T(8,128)(2,1)}, u32[]{:S(2)}, u32[]{:S(2)}) %all-to-all-start.3) | async-done | bytes 5242912 | tf_op jit(solution)/shard_map/all_to_all | solution.py:136
  923.8 5.4 add_bitcast_fusion
  929.3 7.2 convolution_bitcast_fusion
  936.6 168.5 %reduce-scatter.15.cloned.1.call-done = f32[8,2,80,512]{3,2,0,1:T(8,128)} async-done(((f32[8,2,80,2048]{3,2,0,1:T(8,128)}), f32[8,2,80,512]{3,2,0,1:T(8,128)}) %reduce-scatter.15.cloned.1.call-update) | async-done | bytes 2621456 | tf_op jit(solution)/shard_map/reduce_scatter | solution.py:140
  1112.5 174.0 %reduce-scatter.11.cloned.1.call-done = f32[8,2,80,512]{3,2,0,1:T(8,128)} async-done(((f32[8,2,80,2048]{3,2,0,1:T(8,128)}), f32[8,2,80,512]{3,2,0,1:T(8,128)}) %reduce-scatter.11.cloned.1.call-update) | async-done | bytes 2621456 | tf_op jit(solution)/shard_map/reduce_scatter | solution.py:140
  1303.4 6.6 gather_fusion.13
  1312.2 6.7 gather_fusion.5
  1329.4 20.6 %all-gather.13.cloned.1.call-done = f32[128,2048]{1,0:T(8,128)} async-done(((f32[128,512]{1,0:T(8,128)}), f32[128,2048]{1,0:T(8,128)}) %all-gather.13.cloned.1.call-update) | async-done | bytes 1048592 | tf_op jit(solution)/shard_map/all_gather | solution.py:332
  1405.1 5.8 fusion.10
  1411.0 5.7 fusion.12
  1426.7 5.8 bitcast_add_fusion.1
  1432.5 5.7 bitcast_add_fusion.2
  1438.3 5.8 bitcast_add_fusion
  1446.3 10.7 all-reduce.9
  1460.1 34.2 %all-reduce.16.cloned.1.call-done = (bf16[128,2048]{1,0:T(8,128)(2,1)}, bf16[128,2048]{1,0:T(8,128)(2,1)}) async-done(((bf16[128,2048]{1,0:T(8,128)(2,1)}, bf16[128,2048]{1,0:T(8,128)(2,1)}), (bf16[128,2048]{1,0:T(8,128)(2,1)}, bf16[128,2048]{1,0:T(8,128)(2,1)})) %all-reduce.16.cloned.1.call-update) | async-done | bytes 1048592 | tf_op jit(solution)/shard_map/psum | solution.py:384
  1504.3 14.9 all-reduce.7
  1526.2 9.0 all-to-all-done.5
  1538.1 12.8 reduce-scatter.23.cloned.1.call-done
  1553.0 52.3 %reduce-scatter.17.cloned.1.call-done = bf16[256,1024]{1,0:T(8,128)(2,1)} async-done(((bf16[2048,1024]{1,0:T(8,128)(2,1)}), bf16[256,1024]{1,0:T(8,128)(2,1)}) %reduce-scatter.17.cloned.1.call-update) | async-done | bytes 524304 | tf_op jit(solution)/shard_map/reduce_scatter | solution.py:396
  (637 shorter events, 293.2 us)
Async XLA Ops:
  7.2 369.5 %copy-start = (bf16[2,192,2048]{2,1,0:T(8,128)(2,1)S(1)}, bf16[2,192,2048]{2,1,0:T(8,128)(2,1)}, u32[]{:S(2)}) copy-start(bf16[2,192,2048]{2,1,0:T(8,128)(2,1)} %param.39) | copy-start | bytes 4718596
  7.2 170.2 %all-gather.7.cloned.1.call-start = ((), (), s32[]{:S(2)}) async-start(), calls=%async_computation.20 | async-start | bytes 4718592 | tf_op jit(solution)/shard_map/all_gather | solution.py:124
  23.6 50.8 %copy-start.164 = (bf16[16]{0:T(256)(128)(2,1)S(1)}, bf16[16]{0:T(256)(128)(2,1)}, u32[]{:S(2)}) copy-start(bf16[16]{0:T(256)(128)(2,1)} %param.36) | copy-start | bytes 100
  25.7 68.8 %all-to-all-start = ((bf16[8,32,512]{2,1,0:T(8,128)(2,1)}), bf16[8,32,512]{2,1,0:T(8,128)(2,1)S(1)}, u32[]{:S(2)}, u32[]{:S(2)}) async-start(bf16[8,32,512]{2,1,0:T(8,128)(2,1)} %bitcast.7), calls=%async_computation | async-start | bytes 524288 | tf_op jit(solution)/shard_map/all_to_all | solution.py:186
  30.9 167.7 %all-gather.9.cloned.1.call-start = ((), (), s32[]{:S(2)}) async-start(), calls=%async_computation.21 | async-start | bytes 4718592 | tf_op jit(solution)/shard_map/all_gather | solution.py:127
  32.5 62.0 %copy-start.109 = (s32[1024]{0:T(1024)}, s32[1024]{0:T(1024)S(1)}, u32[]{:S(2)}) copy-start(s32[1024]{0:T(1024)S(1)} %eq.152) | copy-start | bytes 12292
  38.2 90.1 %copy-start.128 = (pred[1280]{0:T(1024)(128)(4,1)}, pred[1280]{0:T(1024)(128)(4,1)S(1)}, u32[]{:S(2)}) copy-start(pred[1280]{0:T(1024)(128)(4,1)S(1)} %compare_and_fusion.1) | copy-start | bytes 3844
  53.3 52.6 %copy-start.140 = (f32[128]{0:T(128)}, f32[128]{0:T(128)S(1)}, u32[]{:S(2)}) copy-start(f32[128]{0:T(128)S(1)} %subtract_convert_fusion.2) | copy-start | bytes 1540
  53.4 52.6 %copy-start.142 = (f32[128]{0:T(128)}, f32[128]{0:T(128)S(1)}, u32[]{:S(2)}) copy-start(f32[128]{0:T(128)S(1)} %subtract_convert_fusion.3) | copy-start | bytes 1540
  63.7 64.6 %copy-start.92 = (s32[2048]{0:T(1024)}, s32[2048]{0:T(1024)S(1)}, u32[]{:S(2)}) copy-start(s32[2048]{0:T(1024)S(1)} %pad_clamp_fusion.1) | copy-start | bytes 24580
  64.4 63.9 %copy-start.144 = (f32[64]{0:T(128)}, f32[64]{0:T(128)S(1)}, u32[]{:S(2)}) copy-start(f32[64]{0:T(128)S(1)} %multiply_power_fusion) | copy-start | bytes 772
  72.9 112.3 %copy-start.54 = (f32[8,1,256]{2,1,0:T(1,128)}, f32[8,1,256]{2,1,0:T(1,128)S(1)}, u32[]{:S(2)}) copy-start(f32[8,1,256]{2,1,0:T(1,128)S(1)} %convert_element_type.512) | copy-start | bytes 24580
  88.8 87.7 %copy-start.137 = (f32[128]{0:T(128)}, f32[128]{0:T(128)S(1)}, u32[]{:S(2)}) copy-start(f32[128]{0:T(128)S(1)} %convert_element_type.405) | copy-start | bytes 1540
  94.5 10.3 all-to-all-start.6
  98.9 95.6 %copy-start.68 = (f32[128,64]{1,0:T(8,128)}, f32[128,64]{1,0:T(8,128)S(1)}, u32[]{:S(2)}) copy-start(f32[128,64]{1,0:T(8,128)S(1)} %get-tuple-element.126) | copy-start | bytes 98308
  98.9 95.6 %copy-start.70 = (f32[128,64]{1,0:T(8,128)}, f32[128,64]{1,0:T(8,128)S(1)}, u32[]{:S(2)}) copy-start(f32[128,64]{1,0:T(8,128)S(1)} %get-tuple-element.127) | copy-start | bytes 98308
  134.5 172.6 %all-to-all-start.7 = ((bf16[8,2,80,2048]{3,2,1,0:T(8,128)(2,1)}), bf16[8,2,80,2048]{3,2,1,0:T(8,128)(2,1)}, u32[]{:S(2)}, u32[]{:S(2)}) async-start(bf16[8,2,80,2048]{3,2,1,0:T(8,128)(2,1)} %bitcast.453), calls=%async_computation.9 | async-start | bytes 10485760 | tf_op jit(solution)/shard_map/all_to_all | solution.py:136
  139.1 153.7 %all-reduce.14.cloned.1.call-start = ((), (), s32[]{:S(2)}) async-start(), calls=%async_computation.32 | async-start | bytes 4194304 | tf_op jit(solution)/shard_map/psum | solution.py:269
  156.2 645.1 %copy-start.5 = (bf16[128,2048]{1,0:T(8,128)(2,1)}, bf16[128,2048]{1,0:T(8,128)(2,1)S(1)}, u32[]{:S(2)}) copy-start(bf16[128,2048]{1,0:T(8,128)(2,1)S(1)} %all_gather.59) | copy-start | bytes 1572868
  172.4 120.5 %copy-start.3 = (bf16[128,2048]{1,0:T(8,128)(2,1)}, bf16[128,2048]{1,0:T(8,128)(2,1)S(1)}, u32[]{:S(2)}) copy-start(bf16[128,2048]{1,0:T(8,128)(2,1)S(1)} %all_gather.50) | copy-start | bytes 1572868
  205.9 89.5 %copy-start.93 = (s32[2048]{0:T(1024)S(1)}, s32[2048]{0:T(1024)}, u32[]{:S(2)}) copy-start(s32[2048]{0:T(1024)} %copy-done.92) | copy-start | bytes 24580
  307.0 65.0 %all-to-all-start.1 = ((bf16[8,2,80,2048]{3,2,1,0:T(8,128)(2,1)}), bf16[8,2,80,2048]{3,2,1,0:T(8,128)(2,1)}, u32[]{:S(2)}, u32[]{:S(2)}) async-start(bf16[8,2,80,2048]{3,2,1,0:T(8,128)(2,1)} %bitcast.455), calls=%async_computation.1 | async-start | bytes 10485760 | tf_op jit(solution)/shard_map/all_to_all | solution.py:136
  311.7 252.3 %reduce-scatter.13.cloned.1.call-start = ((), (), s32[]{:S(2)}) async-start(), calls=%async_computation.24 | async-start | bytes 13107200 | tf_op jit(solution)/shard_map/reduce_scatter | solution.py:140
  388.4 365.4 %reduce-scatter.9.cloned.1.call-start = ((), (), s32[]{:S(2)}) async-start(), calls=%async_computation.22 | async-start | bytes 13107200 | tf_op jit(solution)/shard_map/reduce_scatter | solution.py:140
  395.6 176.2 %copy-start.133 = (s32[128,8]{0,1:T(8,128)S(1)}, s32[128,8]{0,1:T(8,128)}, u32[]{:S(2)}) copy-start(s32[128,8]{0,1:T(8,128)} %get-tuple-element.102) | copy-start | bytes 12292
  567.2 189.7 %all-to-all-start.8 = ((bf16[8,2,80,512]{3,2,1,0:T(8,128)(2,1)}), bf16[8,2,80,512]{3,2,1,0:T(8,128)(2,1)}, u32[]{:S(2)}, u32[]{:S(2)}) async-start(bf16[8,2,80,512]{3,2,1,0:T(8,128)(2,1)} %copy.299), calls=%async_computation.11 | async-start | bytes 2621440 | tf_op jit(solution)/shard_map/all_to_all | solution.py:146
  756.9 22.5 %all-to-all-start.2 = ((bf16[8,2,80,512]{3,2,1,0:T(8,128)(2,1)}), bf16[8,2,80,512]{3,2,1,0:T(8,128)(2,1)}, u32[]{:S(2)}, u32[]{:S(2)}) async-start(bf16[8,2,80,512]{3,2,1,0:T(8,128)(2,1)} %copy.285), calls=%async_computation.3 | async-start | bytes 2621440 | tf_op jit(solution)/shard_map/all_to_all | solution.py:146
  779.4 68.5 %all-to-all-start.9 = ((bf16[8,2,80,2048]{3,2,1,0:T(8,128)(2,1)}), bf16[8,2,80,2048]{3,2,1,0:T(8,128)(2,1)}, u32[]{:S(2)}, u32[]{:S(2)}) async-start(bf16[8,2,80,2048]{3,2,1,0:T(8,128)(2,1)} %bitcast.454), calls=%async_computation.12 | async-start | bytes 10485760 | tf_op jit(solution)/shard_map/all_to_all | solution.py:136
  784.2 46.7 %all-gather.11.cloned.1.call-start = ((), (), s32[]{:S(2)}) async-start(), calls=%async_computation.25 | async-start | bytes 1310720 | tf_op jit(solution)/shard_map/all_gather | solution.py:332
  847.9 65.0 %all-to-all-start.3 = ((bf16[8,2,80,2048]{3,2,1,0:T(8,128)(2,1)}), bf16[8,2,80,2048]{3,2,1,0:T(8,128)(2,1)}, u32[]{:S(2)}, u32[]{:S(2)}) async-start(bf16[8,2,80,2048]{3,2,1,0:T(8,128)(2,1)} %bitcast.456), calls=%async_computation.4 | async-start | bytes 10485760 | tf_op jit(solution)/shard_map/all_to_all | solution.py:136
  852.6 252.5 %reduce-scatter.15.cloned.1.call-start = ((), (), s32[]{:S(2)}) async-start(), calls=%async_computation.26 | async-start | bytes 13107200 | tf_op jit(solution)/shard_map/reduce_scatter | solution.py:140
  929.3 357.3 %reduce-scatter.11.cloned.1.call-start = ((), (), s32[]{:S(2)}) async-start(), calls=%async_computation.23 | async-start | bytes 13107200 | tf_op jit(solution)/shard_map/reduce_scatter | solution.py:140
  1108.2 181.5 %all-to-all-start.10 = ((bf16[8,2,80,512]{3,2,1,0:T(8,128)(2,1)}), bf16[8,2,80,512]{3,2,1,0:T(8,128)(2,1)}, u32[]{:S(2)}, u32[]{:S(2)}) async-start(bf16[8,2,80,512]{3,2,1,0:T(8,128)(2,1)} %copy.311), calls=%async_computation.14 | async-start | bytes 2621440 | tf_op jit(solution)/shard_map/all_to_all | solution.py:146
  1112.5 181.8 %copy-start.148 = (f32[128]{0:T(128)S(1)}, f32[128]{0:T(128)}, u32[]{:S(2)}) copy-start(f32[128]{0:T(128)} %convert_element_type.407) | copy-start | bytes 1540
  1112.5 182.4 %copy-start.112 = (s32[1024]{0:T(1024)S(1)}, s32[1024]{0:T(1024)}, u32[]{:S(2)}) copy-start(s32[1024]{0:T(1024)} %copy-done.111) | copy-start | bytes 12292
  1112.5 182.4 %copy-start.116 = (f32[1024]{0:T(1024)S(1)}, f32[1024]{0:T(1024)}, u32[]{:S(2)}) copy-start(f32[1024]{0:T(1024)} %copy-done.115) | copy-start | bytes 12292
  1112.5 182.4 %copy-start.103 = (f32[128,8]{0,1:T(8,128)S(1)}, f32[128,8]{0,1:T(8,128)}, u32[]{:S(2)}) copy-start(f32[128,8]{0,1:T(8,128)} %copy-done.102) | copy-start | bytes 12292
  1112.5 183.1 %copy-start.101 = (f32[128,8]{0,1:T(8,128)S(1)}, f32[128,8]{0,1:T(8,128)}, u32[]{:S(2)}) copy-start(f32[128,8]{0,1:T(8,128)} %copy-done.100) | copy-start | bytes 12292
  1112.5 183.8 %copy-start.39 = (bf16[8,128,128]{1,2,0:T(8,128)(2,1)S(1)}, bf16[8,128,128]{1,2,0:T(8,128)(2,1)}, u32[]{:S(2)}) copy-start(bf16[8,128,128]{1,2,0:T(8,128)(2,1)} %copy-done.38) | copy-start | bytes 786436
  1289.7 22.5 %all-to-all-start.4 = ((bf16[8,2,80,512]{3,2,1,0:T(8,128)(2,1)}), bf16[8,2,80,512]{3,2,1,0:T(8,128)(2,1)}, u32[]{:S(2)}, u32[]{:S(2)}) async-start(bf16[8,2,80,512]{3,2,1,0:T(8,128)(2,1)} %copy.296), calls=%async_computation.6 | async-start | bytes 2621440 | tf_op jit(solution)/shard_map/all_to_all | solution.py:146
  1294.0 56.1 %all-gather.13.cloned.1.call-start = ((), (), s32[]{:S(2)}) async-start(), calls=%async_computation.27 | async-start | bytes 1310720 | tf_op jit(solution)/shard_map/all_gather | solution.py:332
  1322.7 134.4 %reduce-scatter.21.cloned.1.call-start = ((), (), s32[]{:S(2)}) async-start(), calls=%async_computation.30 | async-start | bytes 589824 | tf_op jit(solution)/shard_map/reduce_scatter | solution.py:402
  1368.3 90.3 %reduce-scatter.19.cloned.1.call-start = ((), (), s32[]{:S(2)}) async-start(), calls=%async_computation.29 | async-start | bytes 589824 | tf_op jit(solution)/shard_map/reduce_scatter | solution.py:399
  1380.5 113.9 %all-reduce.16.cloned.1.call-start = ((), (), s32[]{:S(2)}) async-start(), calls=%async_computation.33 | async-start | bytes 2097152 | tf_op jit(solution)/shard_map/psum | solution.py:384
  1391.2 159.7 %reduce-scatter.23.cloned.1.call-start = ((), (), s32[]{:S(2)}) async-start(), calls=%async_computation.31 | async-start | bytes 4718592 | tf_op jit(solution)/shard_map/reduce_scatter | solution.py:405
  1397.3 208.1 %reduce-scatter.17.cloned.1.call-start = ((), (), s32[]{:S(2)}) async-start(), calls=%async_computation.28 | async-start | bytes 4718592 | tf_op jit(solution)/shard_map/reduce_scatter | solution.py:396
  1500.6 21.0 %all-to-all-start.11 = ((bf16[8,32,512]{2,1,0:T(8,128)(2,1)}), bf16[8,32,512]{2,1,0:T(8,128)(2,1)S(1)}, u32[]{:S(2)}, u32[]{:S(2)}) async-start(bf16[8,32,512]{2,1,0:T(8,128)(2,1)} %bitcast.125), calls=%async_computation.15 | async-start | bytes 524288 | tf_op jit(solution)/shard_map/all_to_all | solution.py:432
  1521.6 13.6 all-to-all-start.5
  (146 other events, 1312.7 us)
Sparse Core Ops, SparseCore 0:
  9.9 41.6 all-gather.6
  53.5 36.3 all-gather.8
  206.1 86.7 all-reduce.13
  388.5 175.4 reduce-scatter.12
  566.2 187.5 reduce-scatter.8
  801.4 29.4 all-gather.10
  929.4 175.6 reduce-scatter.14
  1107.4 179.0 reduce-scatter.10
  1322.8 27.2 all-gather.12
  1368.5 33.5 reduce-scatter.20
  1405.1 34.1 reduce-scatter.18
  1442.1 52.1 all-reduce.15
  1497.7 53.1 reduce-scatter.22
  1554.1 51.1 reduce-scatter.16
where the time goes:
time: 1630 us; the launch traced here: 1610 us
  waiting for transfers between devices  1020 us (63%)
  matrix products  152 us (9%)
  blocking collectives  152 us (9%)
  local copies, waits for them, and re-layouts  120 us (7%)
  other arithmetic  102 us (6%)
  starting transfers between devices  53.4 us (3%)
  between operations  19 us (1%)
    reduce_scatter x4, waiting for transfers between devices, owner_total(): lax.psum_scatter(partial_value, 'tp', scatter_dimension=3, tiled=True)  653 us
    all_to_all x4, waiting for transfers between devices, to_owner(): return lax.all_to_all(routed, 'ep', split_axis=0, concat_axis=0, tiled=True)  109 us
    psum x1, waiting for transfers between devices, on_device(): attn_out = lax.psum(attn_part, 'tp')  77.4 us
    reduce_scatter x1, waiting for transfers between devices, on_device(): lax.psum_scatter(acc_query.astype(jnp.bfloat16), 'ep', scatter_dimension=...  52.3 us
    all_gather x2, waiting for transfers between devices, on_device(): grad_moe_in = lax.all_gather(grad_moe_share, 'tp', axis=1, tiled=True)  47.9 us
    all_gather x2, blocking collectives, on_device(): lax.all_gather(grad_rows, 'tp', axis=1, tiled=True)  38.6 us
    psum x1, waiting for transfers between devices, on_device(): lax.psum(normed_part.astype(jnp.bfloat16), 'tp').astype(jnp.float32)  34.2 us
    all_gather x2, blocking collectives, on_device(): lax.all_gather(layer_rows, 'tp', axis=1, tiled=True)  32.9 us
  transfers between devices with their start and end apart: 26, of which 16 were waited for; matrix products, arithmetic and copies ran while one was open for 19% of the time, Pallas kernels for 0%

commit v1 on v0

v1 whole, which is shorter than its diff:
```python
import jax
import jax.numpy as jnp
from jax import lax
from jax.sharding import PartitionSpec as P

HEAD_DIM = 128
MICRO = 2
F32 = jnp.float32
BF16 = jnp.bfloat16

epsilon = 1e-06
rope_base = 1000000.0


def positions_of(lengths, row_count):
    offsets = jnp.arange(row_count, dtype=jnp.int32)
    seq_ends = jnp.cumsum(lengths)
    segment = jnp.sum((offsets[:, None] >= seq_ends[None, :]).astype(jnp.int32), axis=1)
    starts = seq_ends - lengths
    in_segment = segment[:, None] == jnp.arange(lengths.shape[0], dtype=jnp.int32)[None, :]
    position = offsets - jnp.sum(jnp.where(in_segment, starts[None, :], 0), axis=1)
    return (segment, position)


def rope_tables(position, half_dim):
    frequency = rope_base ** (-jnp.arange(half_dim, dtype=F32) / half_dim)
    angles = position.astype(F32)[:, None] * frequency[None, :]
    return (jnp.cos(angles)[:, None, :], jnp.sin(angles)[:, None, :])


def rotate(values, cosine, sine_table):
    half_dim = values.shape[-1] // 2
    first_half = values[..., :half_dim]
    second_half = values[..., half_dim:]
    return jnp.concatenate(
        [
            first_half * cosine - second_half * sine_table,
            second_half * cosine + first_half * sine_table,
        ],
        axis=-1,
    )


def rotate_back(incoming, cosine, sine_table):
    return rotate(incoming, cosine, -sine_table)


def deal_matrices(token_order, ep_index, rows_dev, ep_count):
    per_pair = rows_dev // ep_count
    rows = jnp.arange(rows_dev, dtype=jnp.int32)
    home = ep_index * rows_dev + rows
    at = jnp.arange(token_order.shape[0], dtype=jnp.int32)
    place = jnp.sum(jnp.where(token_order[None, :] == home[:, None], at[None, :], 0), axis=1)
    dest = place // rows_dev
    rank = jnp.sum(
        ((dest[:, None] == dest[None, :]) & (place[None, :] < place[:, None])).astype(jnp.int32),
        axis=1,
    )
    send_slot = dest * per_pair + rank
    send = (send_slot[None, :] == rows[:, None]).astype(BF16)
    mine = lax.dynamic_slice_in_dim(token_order, ep_index * rows_dev, rows_dev, 0)
    source = mine // rows_dev
    my_rank = jnp.sum(
        ((source[:, None] == source[None, :]) & (rows[None, :] < rows[:, None])).astype(jnp.int32),
        axis=1,
    )
    recv_slot = source * per_pair + my_rank
    recv = (recv_slot[:, None] == rows[None, :]).astype(BF16)
    return (send, recv)


def inverse_rms(values):
    return lax.rsqrt(jnp.mean(values * values, axis=-1, keepdims=True) + epsilon)


def norm_back(grad_unit, unit_values, inverse):
    return inverse * (
        grad_unit - unit_values * jnp.mean(grad_unit * unit_values, axis=-1, keepdims=True)
    )


def dot_nn(left, right):
    return jnp.dot(left, right, preferred_element_type=F32)


def dot_tn(left_rows, right_rows):
    return lax.dot_general(
        left_rows, right_rows, (((0,), (0,)), ((), ())), preferred_element_type=F32
    )


def dot_nt(left_rows, right_matrix):
    return lax.dot_general(
        left_rows, right_matrix, (((1,), (1,)), ((), ())), preferred_element_type=F32
    )


def permute_rows(matrix, rows):
    return dot_nn(matrix, rows).astype(BF16)


def exchange(rows, ep_count):
    split = rows.reshape(ep_count, rows.shape[0] // ep_count, rows.shape[1])
    moved = lax.all_to_all(split, "ep", split_axis=0, concat_axis=0, tiled=True)
    return moved.reshape(rows.shape)


def on_device(
    layer_in,
    token_order,
    seq_lengths,
    routes,
    route_weights,
    w_query,
    w_key,
    w_value,
    w_out,
    norm_attn,
    norm_moe,
    query_gain,
    key_gain,
    w_gate,
    w_up,
    w_down,
    grad_out,
):
    ep_count = lax.axis_size("ep")
    tp_count = lax.axis_size("tp")
    tp_index = lax.axis_index("tp")
    ep_index = lax.axis_index("ep")
    local_experts, hidden_here, model_width = w_gate.shape
    experts = local_experts * ep_count
    rows_dev = layer_in.shape[0]
    micro_rows = rows_dev // MICRO
    share_width = layer_in.shape[1]
    score_scale = HEAD_DIM ** (-0.5)

    send, recv = deal_matrices(token_order, ep_index, rows_dev, ep_count)
    both = jnp.concatenate([layer_in, grad_out], axis=1)
    got = permute_rows(recv, exchange(permute_rows(send, both), ep_count))
    layer_full = lax.all_gather(got[:, :share_width], "tp", axis=1, tiled=True)
    grad_full = lax.all_gather(got[:, share_width:], "tp", axis=1, tiled=True)

    q_width, kv_width = w_query.shape[1], w_key.shape[1]
    packed = jnp.concatenate([w_query, w_out, w_key, w_value], axis=1)
    packed = lax.all_gather(packed, "ep", axis=0, tiled=True)
    full_query = packed[:, :q_width]
    full_out = packed[:, q_width : 2 * q_width]
    full_kv = packed[:, 2 * q_width :]
    gains = jnp.concatenate([norm_attn, norm_moe, query_gain, key_gain]).reshape(1, -1)
    gains = lax.all_gather(gains, "ep", axis=0, tiled=True).astype(F32)
    part = norm_attn.shape[0]
    head_part = query_gain.shape[0]
    gain_attn = gains[:, :part].reshape(-1)
    gain_moe = gains[:, part : 2 * part].reshape(-1)
    gain_query = gains[:, 2 * part : 2 * part + head_part].reshape(-1)
    gain_key = gains[:, 2 * part + head_part :].reshape(-1)

    expert_ids = jnp.arange(experts, dtype=jnp.int32)
    dense = jnp.sum(
        jnp.where(routes[:, :, None] == expert_ids[None, None, :], route_weights[:, :, None], 0.0),
        axis=1,
    )
    scale_all = lax.all_gather(dense, "ep", axis=0, tiled=True)
    scale = lax.dynamic_slice_in_dim(scale_all, ep_index * local_experts, local_experts, 1)
    all_grad = lax.all_gather(grad_full, "ep", axis=0, tiled=True)

    heads_here = q_width // HEAD_DIM
    kv_here = kv_width // HEAD_DIM
    group_size = heads_here // kv_here
    segment, position = jax.vmap(positions_of, in_axes=(0, None))(seq_lengths, micro_rows)
    cosine, sine_table = rope_tables(position.reshape(-1), HEAD_DIM // 2)
    layer_float = layer_full.astype(F32)
    inverse_one = inverse_rms(layer_float)
    unit_one = layer_float * inverse_one
    normed = (unit_one * gain_attn).astype(BF16)
    query_proj = dot_nn(normed, full_query).reshape(rows_dev, heads_here, HEAD_DIM)
    kv_proj = dot_nn(normed, full_kv)
    key_proj = kv_proj[:, :kv_width].reshape(rows_dev, kv_here, HEAD_DIM)
    value_proj = kv_proj[:, kv_width:].reshape(rows_dev, kv_here, HEAD_DIM)
    inverse_query = inverse_rms(query_proj)
    unit_query = query_proj * inverse_query
    inverse_key = inverse_rms(key_proj)
    unit_key = key_proj * inverse_key
    queries = (
        rotate(unit_query * gain_query, cosine, sine_table)
        .astype(BF16)
        .reshape(MICRO, micro_rows, kv_here, group_size, HEAD_DIM)
    )
    key_rows = (
        rotate(unit_key * gain_key, cosine, sine_table)
        .astype(BF16)
        .reshape(MICRO, micro_rows, kv_here, HEAD_DIM)
    )
    values = value_proj.astype(BF16).reshape(MICRO, micro_rows, kv_here, HEAD_DIM)
    scores = (
        jnp.einsum("mqkgd,mtkd->mkgqt", queries, key_rows, preferred_element_type=F32)
        * score_scale
    )
    offsets = jnp.arange(micro_rows, dtype=jnp.int32)
    allowed = (segment[:, :, None] == segment[:, None, :]) & (
        offsets[None, None, :] <= offsets[None, :, None]
    )
    scores = jnp.where(allowed[:, None, None], scores, -1e30)
    row_peak = jnp.max(scores, axis=-1, keepdims=True)
    exponent = jnp.exp(scores - row_peak)
    attn_probs = exponent / jnp.sum(exponent, axis=-1, keepdims=True)
    probs_low = attn_probs.astype(BF16)
    context = jnp.einsum("mkgqt,mtkd->mqkgd", probs_low, values, preferred_element_type=F32)
    context_low = context.reshape(rows_dev, heads_here * HEAD_DIM).astype(BF16)
    attn_part = dot_nt(context_low, full_out)
    attn_out = lax.psum(attn_part.astype(BF16), "tp").astype(F32)
    hidden = layer_float + attn_out
    inverse_two = inverse_rms(hidden)
    unit_two = hidden * inverse_two
    moe_in = (unit_two * gain_moe).astype(BF16)

    all_in = lax.all_gather(moe_in, "ep", axis=0, tiled=True)
    flat = local_experts * hidden_here
    gate_matrix = w_gate.reshape(flat, model_width)
    up_matrix = w_up.reshape(flat, model_width)
    down_matrix = w_down.reshape(flat, model_width)
    row_scale = jnp.repeat(scale, hidden_here, axis=1)
    gate_pre = dot_nt(all_in, gate_matrix)
    up_pre = dot_nt(all_in, up_matrix)
    grad_active = dot_nt(all_grad, down_matrix) * row_scale
    sigmoid_gate = jax.nn.sigmoid(gate_pre)
    silu_gate = gate_pre * sigmoid_gate
    active = (silu_gate * up_pre * row_scale).astype(BF16)
    grad_up_pre = (grad_active * silu_gate).astype(BF16)
    grad_gate_pre = (
        grad_active * up_pre * sigmoid_gate * (1.0 + gate_pre * (1.0 - sigmoid_gate))
    ).astype(BF16)
    grad_partial = dot_nn(grad_gate_pre, gate_matrix) + dot_nn(grad_up_pre, up_matrix)
    grad_partial = lax.psum_scatter(
        grad_partial.astype(BF16), "ep", scatter_dimension=0, tiled=True
    )
    grad_share = lax.psum_scatter(grad_partial, "tp", scatter_dimension=1, tiled=True)
    out_partial = dot_nn(active, down_matrix)
    out_partial = lax.psum_scatter(out_partial.astype(BF16), "ep", scatter_dimension=0, tiled=True)
    mixed = lax.psum_scatter(out_partial, "tp", scatter_dimension=1, tiled=True)
    hidden_share = lax.dynamic_slice_in_dim(hidden, tp_index * share_width, share_width, 1)
    layer_dealt = (hidden_share + mixed.astype(F32)).astype(BF16)
    grad_w_down = dot_tn(active, all_grad).reshape(w_down.shape)
    grad_w_gate = dot_tn(grad_gate_pre, all_in).reshape(w_gate.shape)
    grad_w_up = dot_tn(grad_up_pre, all_in).reshape(w_up.shape)

    grad_float = grad_full.astype(F32)
    grad_moe_in = lax.all_gather(grad_share, "tp", axis=1, tiled=True).astype(F32)
    norm_moe_part = jnp.sum(grad_moe_in * unit_two, axis=0)
    grad_hidden = grad_float + norm_back(grad_moe_in * gain_moe, unit_two, inverse_two)
    grad_attn = grad_hidden.astype(BF16)
    grad_w_out = dot_tn(grad_attn, context_low)
    grad_context = (
        dot_nn(grad_attn, full_out)
        .astype(BF16)
        .reshape(MICRO, micro_rows, kv_here, group_size, HEAD_DIM)
    )
    grad_probs = jnp.einsum("mqkgd,mtkd->mkgqt", grad_context, values, preferred_element_type=F32)
    prob_delta = jnp.sum(attn_probs * grad_probs, axis=-1, keepdims=True)
    grad_scores = (attn_probs * (grad_probs - prob_delta)).astype(BF16)
    grad_queries = (
        jnp.einsum("mkgqt,mtkd->mqkgd", grad_scores, key_rows, preferred_element_type=F32).reshape(
            rows_dev, heads_here, HEAD_DIM
        )
        * score_scale
    )
    grad_keys = (
        jnp.einsum("mkgqt,mqkgd->mtkd", grad_scores, queries, preferred_element_type=F32).reshape(
            rows_dev, kv_here, HEAD_DIM
        )
        * score_scale
    )
    grad_values = jnp.einsum(
        "mkgqt,mqkgd->mtkd", probs_low, grad_context, preferred_element_type=F32
    )
    grad_unit_query = rotate_back(grad_queries, cosine, sine_table)
    grad_unit_key = rotate_back(grad_keys, cosine, sine_table)
    query_gain_part = jnp.sum(grad_unit_query * unit_query, axis=(0, 1))
    key_gain_part = jnp.sum(grad_unit_key * unit_key, axis=(0, 1))
    grad_query_proj = (
        norm_back(grad_unit_query * gain_query, unit_query, inverse_query)
        .reshape(rows_dev, heads_here * HEAD_DIM)
        .astype(BF16)
    )
    grad_key_proj = (
        norm_back(grad_unit_key * gain_key, unit_key, inverse_key)
        .reshape(rows_dev, kv_width)
        .astype(BF16)
    )
    grad_value_proj = grad_values.reshape(rows_dev, kv_width).astype(BF16)
    grad_kv_proj = jnp.concatenate([grad_key_proj, grad_value_proj], axis=1)
    normed_part = dot_nt(grad_query_proj, full_query) + dot_nt(grad_kv_proj, full_kv)
    grad_normed = lax.psum_scatter(
        normed_part.astype(BF16), "tp", scatter_dimension=1, tiled=True
    ).astype(F32)
    grad_packed = jnp.concatenate(
        [
            dot_tn(normed, grad_query_proj).astype(BF16),
            grad_w_out.astype(BF16),
            dot_tn(normed, grad_kv_proj).astype(BF16),
        ],
        axis=1,
    )
    grad_packed = lax.psum_scatter(grad_packed, "ep", scatter_dimension=0, tiled=True).astype(F32)

    start = tp_index * share_width
    gain_share = lax.dynamic_slice_in_dim(gain_attn, start, share_width, 0)
    unit_share = lax.dynamic_slice_in_dim(unit_one, start, share_width, 1)
    hidden_grad_share = lax.dynamic_slice_in_dim(grad_hidden, start, share_width, 1)
    scaled = grad_normed * gain_share
    row_mean = lax.psum(jnp.sum(scaled * unit_share, axis=1), "tp") / model_width
    grad_layer = hidden_grad_share + inverse_one * (scaled - unit_share * row_mean[:, None])
    norm_attn_part = lax.dynamic_update_slice_in_dim(
        jnp.zeros((model_width,), F32), jnp.sum(grad_normed * unit_share, axis=0), start, 0
    )
    small = jnp.concatenate(
        [norm_attn_part, norm_moe_part / tp_count, query_gain_part, key_gain_part]
    )
    small = lax.psum(small, ("ep", "tp"))
    grad_norm_attn = lax.dynamic_slice_in_dim(small, ep_index * part, part, 0)
    grad_norm_moe = lax.dynamic_slice_in_dim(small, model_width + ep_index * part, part, 0)
    grad_query_gain = lax.dynamic_slice_in_dim(
        small, 2 * model_width + ep_index * head_part, head_part, 0
    )
    grad_key_gain = lax.dynamic_slice_in_dim(
        small, 2 * model_width + HEAD_DIM + ep_index * head_part, head_part, 0
    )

    back = jnp.concatenate([layer_dealt, grad_layer.astype(BF16)], axis=1)
    home = exchange(dot_tn(recv, back).astype(BF16), ep_count)
    home = dot_tn(send, home)
    return (
        home[:, :share_width].astype(BF16),
        home[:, share_width:],
        grad_packed[:, :q_width],
        grad_packed[:, 2 * q_width : 2 * q_width + kv_width],
        grad_packed[:, 2 * q_width + kv_width :],
        grad_packed[:, q_width : 2 * q_width],
        grad_norm_attn,
        grad_norm_moe,
        grad_query_gain,
        grad_key_gain,
        grad_w_gate,
        grad_w_up,
        grad_w_down,
    )


def solution(mesh):
    return jax.shard_map(
        on_device,
        mesh=mesh,
        in_specs=(
            P("ep", "tp"),
            P(),
            P("ep", None),
            P("ep", None),
            P("ep", None),
            P("ep", "tp"),
            P("ep", "tp"),
            P("ep", "tp"),
            P("ep", "tp"),
            P("ep"),
            P("ep"),
            P("ep"),
            P("ep"),
            P("ep", "tp", None),
            P("ep", "tp", None),
            P("ep", "tp", None),
            P("ep", "tp"),
        ),
        out_specs=(
            P("ep", "tp"),
            P("ep", "tp"),
            P("ep", "tp"),
            P("ep", "tp"),
            P("ep", "tp"),
            P("ep", "tp"),
            P("ep"),
            P("ep"),
            P("ep"),
            P("ep"),
            P("ep", "tp", None),
            P("ep", "tp", None),
            P("ep", "tp", None),
        ),
        check_vma=False,
    )
```

time: 1630 us -> 734 us (0.45)
  waiting for transfers between devices: 1020 us -> 399 us
  local copies, waits for them, and re-layouts: 120 us -> 37.7 us
  blocking collectives: 152 us -> 91.8 us
  other arithmetic: 102 us -> 46.4 us
  starting transfers between devices: 53.4 us -> 9.33 us
  matrix products: 152 us -> 125 us
    reduce_scatter x8 -> x6, waiting for transfers between devices: 718 us -> 168 us  [the longest x1 71.6 us: on_device(): lax.psum_scatter(grad_partial.astype(BF16), 'ep', scatter_dimension=0, ti...]
    all_to_all x12 -> x2, waiting for transfers between devices: 137 us -> 7.94 us  [exchange(): moved = lax.all_to_all(split, 'ep', split_axis=0, concat_axis=0, tiled=True)]
    all_gather x4 -> x6, waiting for transfers between devices: 47.9 us -> 170 us  [the longest x1 56.6 us: on_device(): packed = lax.all_gather(packed, 'ep', axis=0, tiled=True)]
    all_gather x8 -> x1, blocking collectives: 113 us -> 10 us  [on_device(): scale_all = lax.all_gather(dense, 'ep', axis=0, tiled=True)]
    gather x16 -> x0, local copies, waits for them, and re-layouts: 61.2 us -> none  [the longest x2 13.3 us: on_device(): jnp.take(returned, target, axis=0)]
    psum x2 -> x1, waiting for transfers between devices: 112 us -> 52.7 us  [on_device(): attn_out = lax.psum(attn_part.astype(BF16), 'tp').astype(F32)]
    psum x1 -> x2, blocking collectives: 10.7 us -> 58.2 us  [the longest x1 47.9 us: on_device(): small = lax.psum(small, ('ep', 'tp'))]
    all_to_all x12 -> x2, starting transfers between devices: 52.1 us -> 8.81 us  [exchange(): moved = lax.all_to_all(split, 'ep', split_axis=0, concat_axis=0, tiled=True)]
  transfers between devices with their start and end apart: 26 -> 15, of which waited for: 16 -> 11; matrix products, arithmetic and copies ran while one was open for 19% -> 19% of each run, Pallas kernels for 0% -> 0%
where the time goes in v1:
time: 734 us; the launch traced here: 725 us
  waiting for transfers between devices  399 us (54%)
  matrix products  125 us (17%)
  blocking collectives  91.8 us (13%)
  other arithmetic  46.4 us (6%)
  local copies, waits for them, and re-layouts  37.7 us (5%)
  between operations  16 us (2%)
  starting transfers between devices  9.33 us (1%)
    reduce_scatter x1, waiting for transfers between devices, on_device(): lax.psum_scatter(grad_partial.astype(BF16), 'ep', scatter_dimension=0, ti...  71.6 us
    reduce_scatter x1, waiting for transfers between devices, on_device(): lax.psum_scatter(out_partial.astype(BF16), 'ep', scatter_dimension=0, til...  71.1 us
    all_gather x1, waiting for transfers between devices, on_device(): packed = lax.all_gather(packed, 'ep', axis=0, tiled=True)  56.6 us
    dot_general x8, matrix products, dot_nn(): return jnp.dot(left, right, preferred_element_type=F32)  52.9 us
    psum x1, waiting for transfers between devices, on_device(): attn_out = lax.psum(attn_part.astype(BF16), 'tp').astype(F32)  52.7 us
    psum x1, blocking collectives, on_device(): small = lax.psum(small, ('ep', 'tp'))  47.9 us
    all_gather x1, waiting for transfers between devices, on_device(): all_in = lax.all_gather(moe_in, 'ep', axis=0, tiled=True)  45.1 us
    dot_general x6, matrix products, dot_nt(): lax.dot_general(left_rows, right_matrix, (((1,), (1,)), ((), ())), prefer...  40.5 us
  transfers between devices with their start and end apart: 15, of which 11 were waited for; matrix products, arithmetic and copies ran while one was open for 19% of the time, Pallas kernels for 0%

profile of v1, /device:TPU:0, one launch (start us, length us, event | category | flops | bytes accessed | tf_op | source)
XLA Modules:
  0.0 725.2 jit_solution(13505523342195663563)
XLA Ops:
  9.2 2.2 convolution_convert_fusion.7
  11.5 5.2 all-to-all-start
  18.4 7.9 %all-to-all-done = bf16[8,32,1024]{2,1,0:T(8,128)(2,1)S(1)} async-done(((bf16[8,32,1024]{2,1,0:T(8,128)(2,1)}), bf16[8,32,1024]{2,1,0:T(8,128)(2,1)S(1)}, u32[]{:S(2)}, u32[]{:S(2)}) %all-to-all-start) | async-done | bytes 524320 | tf_op jit(solution)/shard_map/all_to_all | solution.py:104
  30.8 23.5 %all-reduce = bf16[4352]{0:T(1024)(128)(2,1)S(1)} all-reduce(bf16[4352]{0:T(1024)(128)(2,1)S(1)} %dynamic-update-slice), channel_id=2, replica_groups=mesh['ep'=8,'tp'=4] {'ep'}, use_global_device_ids=true, to_apply=%add | all-reduce | flops 4352 | bytes 17408
  57.5 1.6 fusion.19
  59.1 56.6 %all-gather.10.cloned.1.call-done = bf16[2048,2304]{1,0:T(8,128)(2,1)} async-done(((bf16[256,2304]{1,0:T(8,128)(2,1)}), bf16[2048,2304]{1,0:T(8,128)(2,1)}) %all-gather.10.cloned.1.call-update) | async-done | bytes 9437200 | tf_op jit(solution)/shard_map/all_gather | solution.py:146
  115.7 2.2 fusion.39
  118.0 3.5 fusion.6
  126.7 2.0 subtract_convert_fusion
  133.0 2.1 copy.80
  135.1 4.6 fusion.10
  139.8 6.0 all-gather.14.cloned.1.call-done
  147.2 52.7 %all-reduce.3.cloned.1.call-done = bf16[256,2048]{1,0:T(8,128)(2,1)} async-done(((bf16[256,2048]{1,0:T(8,128)(2,1)}), bf16[256,2048]{1,0:T(8,128)(2,1)}) %all-reduce.3.cloned.1.call-update) | async-done | bytes 1048592 | tf_op jit(solution)/shard_map/psum | solution.py:212
  200.0 3.8 convert_add_fusion
  204.4 1.5 multiply_convert_fusion.3
  206.7 10.0 %all_gather.28 = f32[2048,16]{0,1:T(8,128)S(1)} all-gather(f32[256,16]{0,1:T(8,128)S(1)} %select_reduce_fusion.1), channel_id=1, replica_groups=mesh['ep'=8,'tp'=4] {'ep'}, dimensions={0}, use_global_device_ids=true | all-gather | bytes 147456 | tf_op jit(solution)/shard_map/all_gather | solution.py:164
  216.7 2.0 broadcast_in_dim.56
  218.8 3.5 copy.81
  222.3 33.1 %all-gather.16.cloned.1.call-done = bf16[2048,2048]{1,0:T(8,128)(2,1)} async-done(((bf16[256,2048]{1,0:T(8,128)(2,1)}), bf16[2048,2048]{1,0:T(8,128)(2,1)}) %all-gather.16.cloned.1.call-update) | async-done | bytes 8388624 | tf_op jit(solution)/shard_map/all_gather | solution.py:166
  255.5 11.0 %convolution_multiply_fusion = f32[2048,384]{1,0:T(8,128)} fusion(f32[2048,384]{1,0:T(8,128)} %copy.81, bf16[2048,2048]{1,0:T(8,128)(2,1)} %all-gather.16.cloned.1.call-done, bf16[384,2048]{1,0:T(8,128)(2,1)} %bitcast.201), kind=kOutput, calls=%fused_computation.21 | convolution fusion | flops 3222011904 | bytes 16252928 | tf_op jit(solution)/shard_map/dot_general | solution.py:93
  266.4 45.1 %all-gather.12.cloned.1.call-done = bf16[2048,2048]{1,0:T(8,128)(2,1)} async-done(((bf16[256,2048]{1,0:T(8,128)(2,1)}), bf16[2048,2048]{1,0:T(8,128)(2,1)}) %all-gather.12.cloned.1.call-update) | async-done | bytes 8388624 | tf_op jit(solution)/shard_map/all_gather | solution.py:218
  311.5 10.2 %fusion.104 = f32[2048,384]{1,0:T(8,128)} fusion(bf16[2048,2048]{1,0:T(8,128)(2,1)} %all-gather.12.cloned.1.call-done, bf16[384,2048]{1,0:T(8,128)(2,1)} %bitcast.184), kind=kOutput, calls=%fused_computation.204 | convolution fusion | flops 3221225472 | bytes 13107200 | tf_op jit(solution)/shard_map/dot_general | solution.py:93
  321.7 8.5 %multiply_convert_fusion.2 = (bf16[2048,384]{1,0:T(8,128)(2,1)}, bf16[2048,384]{1,0:T(8,128)(2,1)S(1)}, bf16[2048,384]{1,0:T(8,128)(2,1)S(1)}) fusion(f32[2048,384]{1,0:T(8,128)S(1)} %copy-done.24, f32[2048,384]{1,0:T(8,128)} %fusion.104, f32[2048,384]{1,0:T(8,128)S(1)} %copy-done.75, bf16[2048,2048]{1,0:T(8,128)(2,1)S(1)} %copy-done.2, ...), kind=kOutput, calls=%fused_computation.15 | convolution fusion | flops 3233808384 | bytes 24117248 | tf_op jit(solution)/shard_map/dot_general | solution.py:93
  330.2 22.1 %fusion.105 = f32[2048,2048]{1,0:T(8,128)} fusion(bf16[2048,384]{1,0:T(8,128)(2,1)S(1)} %get-tuple-element.61, bf16[384,2048]{1,0:T(8,128)(2,1)S(1)} %bitcast.185), kind=kOutput, calls=%fused_computation.205 | convolution fusion | flops 3221225472 | bytes 19922944 | tf_op jit(solution)/shard_map/dot_general | solution.py:83
  352.3 10.2 %add_convert_fusion = bf16[2048,2048]{1,0:T(8,128)(2,1)} fusion(f32[2048,2048]{1,0:T(8,128)} %fusion.105, bf16[2048,384]{1,0:T(8,128)(2,1)S(1)} %get-tuple-element.62, bf16[384,2048]{1,0:T(8,128)(2,1)S(1)} %bitcast.162), kind=kOutput, calls=%fused_computation | convolution fusion | flops 3229614080 | bytes 28311552 | tf_op jit(solution)/shard_map/dot_general | solution.py:83
  362.6 71.6 %reduce-scatter.11.cloned.1.call-done = bf16[256,2048]{1,0:T(8,128)(2,1)} async-done(((bf16[2048,2048]{1,0:T(8,128)(2,1)}), bf16[256,2048]{1,0:T(8,128)(2,1)}) %reduce-scatter.11.cloned.1.call-update) | async-done | bytes 1048592 | tf_op jit(solution)/shard_map/reduce_scatter | solution.py:235
  434.3 8.1 %convolution_convert_fusion = bf16[2048,2048]{1,0:T(8,128)(2,1)} fusion(bf16[2048,384]{1,0:T(8,128)(2,1)S(1)} %copy-done.25, bf16[384,2048]{1,0:T(8,128)(2,1)} %bitcast.202), kind=kOutput, calls=%fused_computation.2 | convolution fusion | flops 3225419776 | bytes 11534336 | tf_op jit(solution)/shard_map/dot_general | solution.py:83
  442.5 21.3 %reduce-scatter.13.cloned.1.call-done = bf16[256,512]{1,0:T(8,128)(2,1)} async-done(((bf16[256,2048]{1,0:T(8,128)(2,1)}), bf16[256,512]{1,0:T(8,128)(2,1)}) %reduce-scatter.13.cloned.1.call-update) | async-done | bytes 262160 | tf_op jit(solution)/shard_map/reduce_scatter | solution.py:238
  466.2 71.1 %reduce-scatter.7.cloned.1.call-done = bf16[256,2048]{1,0:T(8,128)(2,1)} async-done(((bf16[2048,2048]{1,0:T(8,128)(2,1)}), bf16[256,2048]{1,0:T(8,128)(2,1)}) %reduce-scatter.7.cloned.1.call-update) | async-done | bytes 1048592 | tf_op jit(solution)/shard_map/reduce_scatter | solution.py:240
  537.4 29.4 %all-gather.18.cloned.1.call-done = bf16[256,2048]{1,0:T(8,128)(2,1)} async-done(((bf16[256,512]{1,0:T(8,128)(2,1)}), bf16[256,2048]{1,0:T(8,128)(2,1)}) %all-gather.18.cloned.1.call-update) | async-done | bytes 1048592 | tf_op jit(solution)/shard_map/all_gather | solution.py:249
  566.7 2.9 fusion.18
  570.7 4.3 fusion.26
  584.5 3.5 fusion.4
  588.0 2.7 fusion.9
  591.4 1.4 convolution_convert_fusion.2
  594.3 15.9 %pad_maximum_fusion = bf16[2048,2304]{0,1:T(8,128)(2,1)} fusion(bf16[2048,256]{0,1:T(8,128)(2,1)S(1)} %convolution_convert_fusion.3, bf16[2048,1024]{0,1:T(8,128)(2,1)S(1)} %convolution_convert_fusion.1, bf16[2048,1024]{0,1:T(8,128)(2,1)S(1)} %convolution_convert_fusion.2), kind=kLoop, calls=%fused_computation.1 | loop fusion | flops 28311552 | bytes 18874368 | tf_op jit(solution)/shard_map/concatenate | solution.py:297
  611.7 8.7 %fusion.108 = f32[384,2048]{1,0:T(8,128)} fusion(bf16[2048,384]{1,0:T(8,128)(2,1)S(1)} %copy-done.26, bf16[2048,2048]{1,0:T(8,128)(2,1)} %all-gather.16.cloned.1.call-done), kind=kOutput, calls=%fused_computation.208 | convolution fusion | flops 3221225472 | bytes 13107200 | tf_op jit(solution)/shard_map/dot_general | solution.py:87
  620.4 8.8 %fusion.106 = f32[384,2048]{1,0:T(8,128)} fusion(bf16[2048,384]{1,0:T(8,128)(2,1)S(1)} %copy-done.15, bf16[2048,2048]{1,0:T(8,128)(2,1)} %all-gather.12.cloned.1.call-done), kind=kOutput, calls=%fused_computation.206 | convolution fusion | flops 3221225472 | bytes 13107200 | tf_op jit(solution)/shard_map/dot_general | solution.py:87
  629.2 5.3 fusion.107
  634.5 1.4 add_convert_fusion.2
  635.9 1.5 fusion.47
  637.4 10.4 %psum.22 = f32[256]{0:T(256)S(1)} all-reduce(f32[256]{0:T(256)S(1)} %get-tuple-element.55), channel_id=1, replica_groups=mesh['ep'=8,'tp'=4] {'tp'}, use_global_device_ids=true, to_apply=%region_24.25 | all-reduce | flops 256 | bytes 2048 | tf_op jit(solution)/shard_map/psum | solution.py:312
  647.8 1.4 fusion.46
  650.5 3.6 all-to-all-start.1
  654.4 47.9 %psum.23 = f32[4352]{0:T(1024)S(1)} all-reduce(f32[4352]{0:T(1024)S(1)} %pad_maximum_fusion.10), channel_id=1, replica_groups=mesh['ep'=8,'tp'=4] {'ep','tp'}, use_global_device_ids=true, to_apply=%region_31.32 | all-reduce | flops 4352 | bytes 34816 | tf_op jit(solution)/shard_map/psum | solution.py:320
  705.5 4.1 reduce-scatter.17.cloned.1.call-done
  712.0 2.3 fusion.96
  714.3 2.6 copy.93
  (287 shorter events, 47.6 us)
Async XLA Ops:
  7.2 314.5 %copy-start = (bf16[2,192,2048]{2,1,0:T(8,128)(2,1)S(1)}, bf16[2,192,2048]{2,1,0:T(8,128)(2,1)}, u32[]{:S(2)}) copy-start(bf16[2,192,2048]{2,1,0:T(8,128)(2,1)} %param.31) | copy-start | bytes 4718596
  9.2 18.4 %copy-start.38 = (bf16[256,1024]{1,0:T(8,128)(2,1)S(1)}, bf16[256,1024]{1,0:T(8,128)(2,1)}, u32[]{:S(2)}) copy-start(bf16[256,1024]{1,0:T(8,128)(2,1)} %param.25) | copy-start | bytes 1572868
  9.2 18.4 %copy-start.39 = (bf16[256,1024]{1,0:T(8,128)(2,1)S(1)}, bf16[256,1024]{1,0:T(8,128)(2,1)}, u32[]{:S(2)}) copy-start(bf16[256,1024]{1,0:T(8,128)(2,1)} %param.22) | copy-start | bytes 1572868
  9.2 18.5 %copy-start.47 = (bf16[256,128]{1,0:T(8,128)(2,1)S(1)}, bf16[256,128]{1,0:T(8,128)(2,1)}, u32[]{:S(2)}) copy-start(bf16[256,128]{1,0:T(8,128)(2,1)} %param.24) | copy-start | bytes 196612
  9.2 18.5 %copy-start.48 = (bf16[256,128]{1,0:T(8,128)(2,1)S(1)}, bf16[256,128]{1,0:T(8,128)(2,1)}, u32[]{:S(2)}) copy-start(bf16[256,128]{1,0:T(8,128)(2,1)} %param.23) | copy-start | bytes 196612
  11.5 14.9 %all-to-all-start = ((bf16[8,32,1024]{2,1,0:T(8,128)(2,1)}), bf16[8,32,1024]{2,1,0:T(8,128)(2,1)S(1)}, u32[]{:S(2)}, u32[]{:S(2)}) async-start(bf16[8,32,1024]{2,1,0:T(8,128)(2,1)} %bitcast), calls=%async_computation | async-start | bytes 1048576 | tf_op jit(solution)/shard_map/all_to_all | solution.py:104
  16.7 40.8 %all-gather.8.cloned.1.call-start = ((), (), s32[]{:S(2)}) async-start(), calls=%async_computation.8 | async-start | bytes 1310720 | tf_op jit(solution)/shard_map/all_gather | solution.py:141
  18.4 10.4 %copy-start.65 = (s32[256]{0:T(256)}, s32[256]{0:T(256)S(1)}, u32[]{:S(2)}) copy-start(s32[256]{0:T(256)S(1)} %multiply_add_fusion.1) | copy-start | bytes 3076
  27.6 88.1 %all-gather.10.cloned.1.call-start = ((), (), s32[]{:S(2)}) async-start(), calls=%async_computation.9 | async-start | bytes 10616832 | tf_op jit(solution)/shard_map/all_gather | solution.py:146
  28.8 117.0 %all-gather.14.cloned.1.call-start = ((), (), s32[]{:S(2)}) async-start(), calls=%async_computation.14 | async-start | bytes 1310720 | tf_op jit(solution)/shard_map/all_gather | solution.py:142
  54.6 67.5 %copy-start.59 = (f32[128]{0:T(128)}, f32[128]{0:T(128)S(1)}, u32[]{:S(2)}) copy-start(f32[128]{0:T(128)S(1)} %mul.459) | copy-start | bytes 1540
  54.6 67.6 %copy-start.61 = (f32[128]{0:T(128)}, f32[128]{0:T(128)S(1)}, u32[]{:S(2)}) copy-start(f32[128]{0:T(128)S(1)} %mul.473) | copy-start | bytes 1540
  55.3 68.8 %copy-start.63 = (f32[64]{0:T(128)}, f32[64]{0:T(128)S(1)}, u32[]{:S(2)}) copy-start(f32[64]{0:T(128)S(1)} %multiply_power_fusion) | copy-start | bytes 772
  55.5 68.6 %copy-start.52 = (f32[256]{0:T(256)}, f32[256]{0:T(256)S(1)}, u32[]{:S(2)}) copy-start(f32[256]{0:T(256)S(1)} %convert_bitcast_fusion.1) | copy-start | bytes 3076
  57.4 69.3 %copy-start.31 = (f32[256,64]{1,0:T(8,128)}, f32[256,64]{1,0:T(8,128)S(1)}, u32[]{:S(2)}) copy-start(f32[256,64]{1,0:T(8,128)S(1)} %get-tuple-element.94) | copy-start | bytes 196612
  57.4 142.5 %all-reduce.3.cloned.1.call-start = ((), (), s32[]{:S(2)}) async-start(), calls=%async_computation.10 | async-start | bytes 2097152 | tf_op jit(solution)/shard_map/psum | solution.py:212
  57.5 60.5 %copy-start.3 = (bf16[256,2048]{1,0:T(8,128)(2,1)S(1)}, bf16[256,2048]{1,0:T(8,128)(2,1)}, u32[]{:S(2)}) copy-start(bf16[256,2048]{1,0:T(8,128)(2,1)} %all-gather.8.cloned.1.call-done) | copy-start | bytes 3145732
  59.1 62.4 %copy-start.50 = (f32[256]{0:T(256)}, f32[256]{0:T(256)S(1)}, u32[]{:S(2)}) copy-start(f32[256]{0:T(256)S(1)} %add_rsqrt_fusion.3) | copy-start | bytes 3076
  139.8 115.7 %all-gather.16.cloned.1.call-start = ((), (), s32[]{:S(2)}) async-start(), calls=%async_computation.15 | async-start | bytes 9437184 | tf_op jit(solution)/shard_map/all_gather | solution.py:166
  145.9 165.6 %all-gather.12.cloned.1.call-start = ((), (), s32[]{:S(2)}) async-start(), calls=%async_computation.11 | async-start | bytes 9437184 | tf_op jit(solution)/shard_map/all_gather | solution.py:218
  205.9 228.3 %reduce-scatter.11.cloned.1.call-start = ((), (), s32[]{:S(2)}) async-start(), calls=%async_computation.16 | async-start | bytes 9437184 | tf_op jit(solution)/shard_map/reduce_scatter | solution.py:235
  311.5 10.2 %copy-start.2 = (bf16[2048,2048]{1,0:T(8,128)(2,1)S(1)}, bf16[2048,2048]{1,0:T(8,128)(2,1)}, u32[]{:S(2)}) copy-start(bf16[2048,2048]{1,0:T(8,128)(2,1)} %all-gather.12.cloned.1.call-done) | copy-start | bytes 25165828
  311.5 10.2 %copy-start.24 = (f32[2048,384]{1,0:T(8,128)S(1)}, f32[2048,384]{1,0:T(8,128)}, u32[]{:S(2)}) copy-start(f32[2048,384]{1,0:T(8,128)} %copy.81) | copy-start | bytes 9437188
  311.5 10.2 %copy-start.75 = (f32[2048,384]{1,0:T(8,128)S(1)}, f32[2048,384]{1,0:T(8,128)}, u32[]{:S(2)}) copy-start(f32[2048,384]{1,0:T(8,128)} %convolution_multiply_fusion) | copy-start | bytes 9437188
  321.7 8.6 %copy-start.29 = (bf16[2,192,2048]{2,1,0:T(8,128)(2,1)S(1)}, bf16[2,192,2048]{2,1,0:T(8,128)(2,1)}, u32[]{:S(2)}) copy-start(bf16[2,192,2048]{2,1,0:T(8,128)(2,1)} %param.30) | copy-start | bytes 4718596
  330.2 22.1 %copy-start.14 = (bf16[2048,384]{1,0:T(8,128)(2,1)}, bf16[2048,384]{1,0:T(8,128)(2,1)S(1)}, u32[]{:S(2)}) copy-start(bf16[2048,384]{1,0:T(8,128)(2,1)S(1)} %get-tuple-element.61) | copy-start | bytes 4718596
  330.2 22.1 %copy-start.12 = (bf16[2048,384]{1,0:T(8,128)(2,1)}, bf16[2048,384]{1,0:T(8,128)(2,1)S(1)}, u32[]{:S(2)}) copy-start(bf16[2048,384]{1,0:T(8,128)(2,1)S(1)} %get-tuple-element.62) | copy-start | bytes 4718596
  362.5 71.7 %copy-start.25 = (bf16[2048,384]{1,0:T(8,128)(2,1)S(1)}, bf16[2048,384]{1,0:T(8,128)(2,1)}, u32[]{:S(2)}) copy-start(bf16[2048,384]{1,0:T(8,128)(2,1)} %get-tuple-element.60) | copy-start | bytes 4718596
  362.5 101.3 %reduce-scatter.13.cloned.1.call-start = ((), (), s32[]{:S(2)}) async-start(), calls=%async_computation.17 | async-start | bytes 1310720 | tf_op jit(solution)/shard_map/reduce_scatter | solution.py:238
  434.2 103.1 %reduce-scatter.7.cloned.1.call-start = ((), (), s32[]{:S(2)}) async-start(), calls=%async_computation.12 | async-start | bytes 9437184 | tf_op jit(solution)/shard_map/reduce_scatter | solution.py:240
  442.4 22.7 %copy-start.19 = (bf16[2,8,128,128]{2,3,1,0:T(8,128)(2,1)S(1)}, bf16[2,8,128,128]{2,3,1,0:T(8,128)(2,1)}, u32[]{:S(2)}) copy-start(bf16[2,8,128,128]{2,3,1,0:T(8,128)(2,1)} %copy-done.18) | copy-start | bytes 1572868
  442.4 124.3 %copy-start.11 = (bf16[256,2048]{1,0:T(8,128)(2,1)S(1)}, bf16[256,2048]{1,0:T(8,128)(2,1)}, u32[]{:S(2)}) copy-start(bf16[256,2048]{1,0:T(8,128)(2,1)} %all-reduce.3.cloned.1.call-done) | copy-start | bytes 3145732
  442.4 124.3 %all-gather.18.cloned.1.call-start = ((), (), s32[]{:S(2)}) async-start(), calls=%async_computation.18 | async-start | bytes 1310720 | tf_op jit(solution)/shard_map/all_gather | solution.py:249
  463.8 170.6 %reduce-scatter.9.cloned.1.call-start = ((), (), s32[]{:S(2)}) async-start(), calls=%async_computation.13 | async-start | bytes 1310720 | tf_op jit(solution)/shard_map/reduce_scatter | solution.py:241
  537.3 32.4 %copy-start.43 = (f32[1,2,8,128]{3,1,2,0:T(2,128)S(1)}, f32[1,2,8,128]{3,1,2,0:T(2,128)}, u32[]{:S(2)}) copy-start(f32[1,2,8,128]{3,1,2,0:T(2,128)} %copy.118) | copy-start | bytes 24580
  537.3 32.4 %copy-start.57 = (f32[256]{0:T(256)S(1)}, f32[256]{0:T(256)}, u32[]{:S(2)}) copy-start(f32[256]{0:T(256)} %copy-done.56) | copy-start | bytes 3076
  537.3 98.5 %reduce-scatter.15.cloned.1.call-start = ((), (), s32[]{:S(2)}) async-start(), calls=%async_computation.19 | async-start | bytes 1310720 | tf_op jit(solution)/shard_map/reduce_scatter | solution.py:294
  570.7 4.4 copy-start.9
  570.7 4.4 copy-start.41
  590.7 118.8 %reduce-scatter.17.cloned.1.call-start = ((), (), s32[]{:S(2)}) async-start(), calls=%async_computation.20 | async-start | bytes 10616832 | tf_op jit(solution)/shard_map/reduce_scatter | solution.py:305
  611.7 8.7 %copy-start.15 = (bf16[2048,384]{1,0:T(8,128)(2,1)S(1)}, bf16[2048,384]{1,0:T(8,128)(2,1)}, u32[]{:S(2)}) copy-start(bf16[2048,384]{1,0:T(8,128)(2,1)} %copy-done.14) | copy-start | bytes 4718596
  611.7 17.5 %slice-start = ((s8[8388608]{0:T(1024)(128)(4,1)}), s8[4194304]{0:T(1024)(128)(4,1)S(1)}, s32[]{:S(2)}) async-start(s8[8388608]{0:T(1024)(128)(4,1)} %bitcast.163), calls=%async_computation.21 | async-start | bytes 8388608
  620.4 8.8 %slice-start.1 = ((s8[8388608]{0:T(1024)(128)(4,1)}), s8[4194304]{0:T(1024)(128)(4,1)S(1)}, s32[]{:S(2)}) async-start(s8[8388608]{0:T(1024)(128)(4,1)} %bitcast.163), calls=%async_computation.22 | async-start | bytes 8388608
  620.4 8.8 %copy-start.13 = (bf16[2048,384]{1,0:T(8,128)(2,1)S(1)}, bf16[2048,384]{1,0:T(8,128)(2,1)}, u32[]{:S(2)}) copy-start(bf16[2048,384]{1,0:T(8,128)(2,1)} %copy-done.12) | copy-start | bytes 4718596
  634.5 14.8 %copy-start.66 = (s32[256]{0:T(256)S(1)}, s32[256]{0:T(256)}, u32[]{:S(2)}) copy-start(s32[256]{0:T(256)} %copy-done.65) | copy-start | bytes 3076
  637.4 16.7 %copy-start.49 = (f32[2048]{0:T(1024)S(1)}, f32[2048]{0:T(1024)}, u32[]{:S(2)}) copy-start(f32[2048]{0:T(1024)} %get-tuple-element.52) | copy-start | bytes 24580
  637.4 66.1 %copy-start.69 = (s32[256]{0:T(256)S(1)}, s32[256]{0:T(256)}, u32[]{:S(2)}) copy-start(s32[256]{0:T(256)} %copy-done.68) | copy-start | bytes 3076
  650.5 53.1 %all-to-all-start.1 = ((bf16[8,32,1024]{2,1,0:T(8,128)(2,1)}), bf16[8,32,1024]{2,1,0:T(8,128)(2,1)S(1)}, u32[]{:S(2)}, u32[]{:S(2)}) async-start(bf16[8,32,1024]{2,1,0:T(8,128)(2,1)} %bitcast.45), calls=%async_computation.6 | async-start | bytes 1048576 | tf_op jit(solution)/shard_map/all_to_all | solution.py:104
  (45 other events, 94.3 us)
Sparse Core Ops, SparseCore 0:
  27.7 27.3 all-gather.7
  57.6 58.0 all-gather.9
  117.9 27.9 all-gather.13
  148.7 51.2 all-reduce.2
  201.7 53.7 all-gather.15
  257.2 54.2 all-gather.11
  362.7 71.4 reduce-scatter.10
  436.5 27.2 reduce-scatter.12
  467.3 69.9 reduce-scatter.6
  538.7 27.9 all-gather.17
  569.0 26.6 reduce-scatter.8
  598.5 25.7 reduce-scatter.14
  627.8 81.7 reduce-scatter.16

commit v2 on v1

--- a/solution.py
+++ b/solution.py
@@ -1,12 +1,18 @@
+import functools
+
 import jax
 import jax.numpy as jnp
 from jax import lax
+from jax.experimental import pallas as pl
+from jax.experimental.pallas import tpu as pltpu
 from jax.sharding import PartitionSpec as P
 
 HEAD_DIM = 128
 MICRO = 2
 F32 = jnp.float32
 BF16 = jnp.bfloat16
+SCALE_TERMS = 3
+VMEM_LIMIT = 66 * 1000 * 1000
 
 epsilon = 1e-06
 rope_base = 1000000.0
@@ -103,6 +109,612 @@
     split = rows.reshape(ep_count, rows.shape[0] // ep_count, rows.shape[1])
     moved = lax.all_to_all(split, "ep", split_axis=0, concat_axis=0, tiled=True)
     return moved.reshape(rows.shape)
+
+
+MESH_ID = pl.DeviceIdType.MESH
+HALF = 2
+E0, E1, P0, P1, A0, B0, PA0, PB0, A1, B1, PA1, PB1, D0, PD0, D1, PD1 = range(16)
+SLOT_E, SLOT_P, SLOT_A, SLOT_B = (E0, E1), (P0, P1), (A0, A1), (B0, B1)
+SLOT_D, SLOT_PA, SLOT_PB, SLOT_PD = (D0, D1), (PA0, PA1), (PB0, PB1), (PD0, PD1)
+FOR_PARTNER = (P0, P1, PB0, PB1, PA0, PA1, PD0, PD1)
+
+
+def roles():
+    e = lax.axis_index("ep")
+    core, x, y = e % 2, (e // 2) % 2, e // 4
+    other = 1 - 2 * core
+    over_x, over_y = e + 2 - 4 * x, e + 4 - 8 * y
+    a = over_x * (1 - core) + over_y * core
+    b = over_y * (1 - core) + over_x * core
+    d = over_x + over_y - e
+    return dict(e=e, p=e + other, a=a, b=b, d=d, pa=a + other, pb=b + other, pd=d + other)
+
+
+def slot_owner(r):
+    names = ("e", "e", "p", "p", "a", "b", "pa", "pb", "a", "b", "pa", "pb", "d", "pd", "d", "pd")
+    halves = (0, 1, 0, 1, 0, 0, 0, 0, 1, 1, 1, 1, 0, 0, 1, 1)
+    return [(r[name], half) for name, half in zip(names, halves)]
+
+
+def greet(plane, line):
+    barrier = pltpu.get_barrier_semaphore()
+    for device in plane:
+        pl.semaphore_signal(barrier, inc=1, device_id={"ep": device}, device_id_type=MESH_ID)
+    for device in line:
+        pl.semaphore_signal(barrier, inc=1, device_id={"tp": device}, device_id_type=MESH_ID)
+    pl.semaphore_wait(barrier, len(plane) + len(line))
+
+
+def send_to(src, dst, send_sem, recv_sem, **device):
+    return pltpu.make_async_remote_copy(
+        src_ref=src,
+        dst_ref=dst,
+        send_sem=send_sem,
+        recv_sem=recv_sem,
+        device_id=device,
+        device_id_type=MESH_ID,
+    )
+
+
+class PlaneGather:
+    kinds = 7
+
+    def __init__(self, r, held, half, send, recv):
+        self.r, self.held, self.half, self.send, self.recv = r, held, half, send, recv
+
+    def slot(self, index):
+        return self.held.at[pl.ds(index * self.half, self.half)]
+
+    def copy(self, kind, k):
+        source, target, device = (
+            (SLOT_E, SLOT_A, "a"),
+            (SLOT_E, SLOT_B, "b"),
+            (SLOT_E, SLOT_P, "p"),
+            (SLOT_A, SLOT_D, "b"),
+            (SLOT_A, SLOT_PB, "p"),
+            (SLOT_B, SLOT_PA, "p"),
+            (SLOT_D, SLOT_PD, "p"),
+        )[kind]
+        return send_to(
+            self.slot(source[k]),
+            self.slot(target[k]),
+            self.send.at[kind, k],
+            self.recv.at[kind, k],
+            ep=self.r[device],
+        )
+
+    def begin(self):
+        for k in range(HALF):
+            for kind in range(3):
+                self.copy(kind, k).start()
+
+    def arrived(self, kind, k):
+        self.copy(kind, k).wait_recv()
+
+    def pass_near(self, k):
+        self.arrived(0, k)
+        self.copy(3, k).start()
+        self.copy(4, k).start()
+        self.arrived(1, k)
+        self.copy(5, k).start()
+
+    def pass_far(self, k):
+        self.arrived(3, k)
+        self.copy(6, k).start()
+
+    def sent(self):
+        for k in range(HALF):
+            for kind in range(self.kinds):
+                self.copy(kind, k).wait_send()
+
+
+class PlaneSum:
+    def __init__(self, r, part, near, far, first, second, half, sems):
+        self.r, self.part, self.half = r, part, half
+        self.near, self.far, self.first, self.second = near, far, first, second
+        self.near_send, self.near_recv, self.send, self.recv = sems
+
+    def slot(self, index):
+        return self.part.at[pl.ds(index * self.half, self.half)]
+
+    def rows(self, buffer, index):
+        return buffer.at[pl.ds(index * self.half, self.half)]
+
+    def near_copy(self, index):
+        return send_to(
+            self.slot(FOR_PARTNER[index]),
+            self.rows(self.near, index),
+            self.near_send.at[index],
+            self.near_recv.at[index],
+            ep=self.r["p"],
+        )
+
+    def far_copy(self, kind, k):
+        source, target, device = (
+            (SLOT_D, self.far, "b"),
+            (SLOT_A, self.first, "a"),
+            (SLOT_B, self.second, "b"),
+        )[kind]
+        return send_to(
+            self.slot(source[k]),
+            self.rows(target, k),
+            self.send.at[kind, k],
+            self.recv.at[kind, k],
+            ep=self.r[device],
+        )
+
+    def add_up(self, slot, others):
+        total = self.slot(slot)[...].astype(F32)
+        for other in others:
+            total = total + other[...].astype(F32)
+        return total
+
+    def near_sum(self, name, k):
+        index = 2 * name + k
+        slot = (SLOT_E, SLOT_A, SLOT_B, SLOT_D)[name][k]
+        self.near_copy(index).wait_recv()
+        return slot, [self.rows(self.near, index)]
+
+    def pass_far(self, k):
+        slot, others = self.near_sum(3, k)
+        self.slot(slot)[...] = self.add_up(slot, others).astype(BF16)
+        self.far_copy(0, k).start()
+
+    def pass_second(self, k):
+        slot, others = self.near_sum(2, k)
+        self.slot(slot)[...] = self.add_up(slot, others).astype(BF16)
+        self.far_copy(2, k).start()
+
+    def pass_first(self, k):
+        slot, others = self.near_sum(1, k)
+        self.far_copy(0, k).wait_recv()
+        self.slot(slot)[...] = self.add_up(slot, others + [self.rows(self.far, k)]).astype(BF16)
+        self.far_copy(1, k).start()
+
+    def total(self, k):
+        slot, others = self.near_sum(0, k)
+        self.far_copy(1, k).wait_recv()
+        self.far_copy(2, k).wait_recv()
+        return self.add_up(slot, others + [self.rows(self.first, k), self.rows(self.second, k)])
+
+    def sent(self):
+        for index in range(4 * HALF):
+            self.near_copy(index).wait_send()
+        for kind in range(3):
+            for k in range(HALF):
+                self.far_copy(kind, k).wait_send()
+
+
+def plane_sum_scratch(half, width, kinds=3):
+    return [
+        pltpu.VMEM((8 * half, width), BF16),
+        pltpu.VMEM((2 * half, width), BF16),
+        pltpu.VMEM((2 * half, width), BF16),
+        pltpu.VMEM((2 * half, width), BF16),
+        pltpu.SemaphoreType.DMA((4 * HALF,)),
+        pltpu.SemaphoreType.DMA((4 * HALF,)),
+        pltpu.SemaphoreType.DMA((kinds, HALF)),
+        pltpu.SemaphoreType.DMA((kinds, HALF)),
+    ]
+
+
+def any_spec():
+    return pl.BlockSpec(memory_space=pl.ANY)
+
+
+def vmem_spec():
+    return pl.BlockSpec(memory_space=pltpu.VMEM)
+
+
+def comm_params(collective_id):
+    return pltpu.CompilerParams(
+        collective_id=collective_id, has_side_effects=True, vmem_limit_bytes=VMEM_LIMIT
+    )
+
+
+def expert_body(
+    flat,
+    rows,
+    parts,
+    own_hbm,
+    grad_hbm,
+    scale_hbm,
+    pick_ref,
+    gate_hbm,
+    up_hbm,
+    down_hbm,
+    total_ref,
+    active_hbm,
+    d_gate_hbm,
+    d_up_hbm,
+    d_down_hbm,
+    held,
+    grads,
+    scales,
+    both,
+    down,
+    grad_act,
+    grad_both,
+    active,
+    d_weights,
+    part,
+    near,
+    far,
+    first,
+    second,
+    near_send,
+    near_recv,
+    sum_send,
+    sum_recv,
+    gather_send,
+    gather_recv,
+    local_sem,
+    grad_sem,
+    out_sem,
+):
+    r = roles()
+    half = rows // HALF
+    unit = 2 * half
+    owners = slot_owner(r)
+    loads = [
+        pltpu.make_async_copy(own_hbm, held.at[pl.ds(0, rows)], local_sem.at[0]),
+        pltpu.make_async_copy(gate_hbm, both.at[pl.ds(0, flat)], local_sem.at[1]),
+        pltpu.make_async_copy(up_hbm, both.at[pl.ds(flat, flat)], local_sem.at[2]),
+        pltpu.make_async_copy(down_hbm, down, local_sem.at[3]),
+    ]
+    for load in loads:
+        load.start()
+    slots = []
+    for index, (owner, k) in enumerate(owners):
+        slots.append(
+            (
+                pltpu.make_async_copy(
+                    scale_hbm.at[pl.ds(owner * parts, parts), pl.ds(k * half, half)],
+                    scales.at[index],
+                    grad_sem.at[0, index],
+                ),
+                pltpu.make_async_copy(
+                    grad_hbm.at[pl.ds(owner * rows + k * half, half)],
+                    grads.at[pl.ds(index * half, half)],
+                    grad_sem.at[1, index],
+                ),
+            )
+        )
+        for load in slots[-1]:
+            load.start()
+    greet([r["p"], r["a"], r["b"]], [])
+    gather = PlaneGather(r, held, half, gather_send, gather_recv)
+    loads[0].wait()
+    gather.begin()
+    for load in loads[1:]:
+        load.wait()
+    for pair in slots:
+        for load in pair:
+            load.wait()
+    psum = PlaneSum(
+        r, part, near, far, first, second, half, (near_send, near_recv, sum_send, sum_recv)
+    )
+
+    def expand(index):
+        return jnp.concatenate(
+            [dot_tn(scales[2 * index], pick_ref[...]), dot_tn(scales[2 * index + 1], pick_ref[...])],
+            axis=0,
+        )
+
+    @pl.loop(0, 8)
+    def _(index):
+        at = pl.ds(pl.multiple_of(index * unit, unit), unit)
+        grad_act[at, :] = dot_nt(grads[at, :], down[...]) * expand(index)
+
+    @pl.loop(0, 8)
+    def _(index):
+        @pl.when(index == 1)
+        def _():
+            gather.arrived(2, 0)
+            gather.arrived(2, 1)
+
+        for k, first_unit in ((0, 2), (1, 4)):
+
+            @pl.when(index == first_unit)
+            def _():
+                gather.pass_near(k)
+
+            @pl.when(index == first_unit + 1)
+            def _():
+                gather.arrived(4, k)
+                gather.arrived(5, k)
+
+            @pl.when(index == 6 + k)
+            def _():
+                gather.pass_far(k)
+                gather.arrived(6, k)
+
+        at = pl.ds(pl.multiple_of(index * unit, unit), unit)
+        pre = dot_nt(held[at, :], both[...])
+        gate_pre, up_pre = pre[:, :flat], pre[:, flat:]
+        grad_active = grad_act[at, :]
+        sigmoid_gate = jax.nn.sigmoid(gate_pre)
+        silu_gate = gate_pre * sigmoid_gate
+        active[at, :] = (silu_gate * up_pre * expand(index)).astype(BF16)
+        grad_both[at, flat:] = (grad_active * silu_gate).astype(BF16)
+        grad_both[at, :flat] = (
+            grad_active * up_pre * sigmoid_gate * (1.0 + gate_pre * (1.0 - sigmoid_gate))
+        ).astype(BF16)
+        part[at, :] = dot_nn(grad_both[at, :], both[...]).astype(BF16)
+
+        @pl.when(index == 1)
+        def _():
+            psum.near_copy(0).start()
+            psum.near_copy(1).start()
+
+        for k, last_unit in ((0, 3), (1, 5)):
+
+            @pl.when(index == last_unit)
+            def _():
+                psum.near_copy(2 + k).start()
+                psum.near_copy(4 + k).start()
+
+            @pl.when(index == last_unit + 1)
+            def _():
+                psum.pass_second(k)
+
+            @pl.when(index == 6 + k)
+            def _():
+                psum.near_copy(6 + k).start()
+
+    active_out = pltpu.make_async_copy(active, active_hbm, local_sem.at[0])
+    active_out.start()
+    psum.pass_far(0)
+    psum.pass_far(1)
+    group = 128
+    pieces = flat // group
+
+    def weight_piece(which, index):
+        source, other, column = (
+            (active, grads, 0),
+            (grad_both, held, 0),
+            (grad_both, held, flat),
+        )[which]
+        lanes = pl.ds(pl.multiple_of(column + index * group, group), group)
+        place = pl.ds(pl.multiple_of(which * flat + index * group, group), group)
+        d_weights[place, :] = dot_tn(source[:, lanes], other[...])
+
+    def weight_out(which):
+        target = (d_down_hbm, d_gate_hbm, d_up_hbm)[which]
+        return pltpu.make_async_copy(
+            d_weights.at[pl.ds(which * flat, flat)], target, out_sem.at[which]
+        )
+
+    @pl.loop(0, pieces)
+    def _(index):
+        weight_piece(0, index)
+
+    weight_out(0).start()
+    psum.pass_first(0)
+    psum.pass_first(1)
+
+    @pl.loop(0, 2 * pieces)
+    def _(index):
+        lanes = pl.ds(pl.multiple_of(index * group, group), group)
+        place = pl.ds(pl.multiple_of(flat + index * group, group), group)
+        d_weights[place, :] = dot_tn(grad_both[:, lanes], held[...])
+
+    weight_out(1).start()
+    weight_out(2).start()
+    for k in range(HALF):
+        total_ref[pl.ds(k * half, half), :] = psum.total(k).astype(BF16)
+    active_out.wait()
+    for which in range(3):
+        weight_out(which).wait()
+    gather.sent()
+    psum.sent()
+
+
+def expert_call(own, all_grad, scale_parts, pick, gate_matrix, up_matrix, down_matrix):
+    rows, width = own.shape
+    flat = gate_matrix.shape[0]
+    everything = all_grad.shape[0]
+    parts = pick.shape[0]
+    half = rows // HALF
+    f32_weight = jax.ShapeDtypeStruct((flat, width), F32)
+    return pl.pallas_call(
+        functools.partial(expert_body, flat, rows, parts),
+        out_shape=(
+            jax.ShapeDtypeStruct((rows, width), BF16),
+            jax.ShapeDtypeStruct((everything, flat), BF16),
+            f32_weight,
+            f32_weight,
+            f32_weight,
+        ),
+        in_specs=[any_spec(), any_spec(), any_spec(), vmem_spec()] + [any_spec()] * 3,
+        out_specs=(vmem_spec(), any_spec(), any_spec(), any_spec(), any_spec()),
+        scratch_shapes=[
+            pltpu.VMEM((everything, width), BF16),
+            pltpu.VMEM((everything, width), BF16),
+            pltpu.VMEM((16, parts, half), BF16),
+            pltpu.VMEM((2 * flat, width), BF16),
+            pltpu.VMEM((flat, width), BF16),
+            pltpu.VMEM((everything, flat), F32),
+            pltpu.VMEM((everything, 2 * flat), BF16),
+            pltpu.VMEM((everything, flat), BF16),
+            pltpu.VMEM((3 * flat, width), F32),
+            pltpu.VMEM((everything, width), BF16),
+        ]
+        + plane_sum_scratch(half, width)
+        + [
+            pltpu.SemaphoreType.DMA((PlaneGather.kinds, HALF)),
+            pltpu.SemaphoreType.DMA((PlaneGather.kinds, HALF)),
+            pltpu.SemaphoreType.DMA((4,)),
+            pltpu.SemaphoreType.DMA((2, 16)),
+            pltpu.SemaphoreType.DMA((3,)),
+        ],
+        compiler_params=comm_params(1),
+        name="experts",
+    )(own, all_grad, scale_parts, pick, gate_matrix, up_matrix, down_matrix)
+
+
+class LineSum:
+    def __init__(self, count, source, arrived, send, recv):
+        self.count, self.source, self.arrived, self.send, self.recv = (
+            count,
+            source,
+            arrived,
+            send,
+            recv,
+        )
+        self.z = lax.axis_index("tp")
+        self.share = source.shape[1] // count
+
+    def columns(self, z):
+        return pl.ds(pl.multiple_of(z * self.share, self.share), self.share)
+
+    def copy(self, j):
+        target = (self.z + j) % self.count
+        return send_to(
+            self.source.at[:, self.columns(target)],
+            self.arrived.at[j - 1],
+            self.send.at[j - 1],
+            self.recv.at[j - 1],
+            tp=target,
+        )
+
+    def begin(self):
+        for j in range(1, self.count):
+            self.copy(j).start()
+
+    def total(self):
+        total = self.source[:, self.columns(self.z)].astype(F32)
+        for j in range(1, self.count):
+            self.copy(j).wait_recv()
+            total = total + self.arrived[j - 1].astype(F32)
+        return total
+
+    def sent(self):
+        for j in range(1, self.count):
+            self.copy(j).wait_send()
+
+
+class LineGather:
+    def __init__(self, count, whole, send, recv):
+        self.count, self.whole, self.send, self.recv = count, whole, send, recv
+        self.z = lax.axis_index("tp")
+        self.share = whole.shape[1] // count
+
+    def columns(self, z):
+        return pl.ds(pl.multiple_of(z * self.share, self.share), self.share)
+
+    def copy(self, j):
+        mine = self.whole.at[:, self.columns(self.z)]
+        return send_to(
+            mine, mine, self.send.at[j - 1], self.recv.at[j - 1], tp=(self.z + j) % self.count
+        )
+
+    def arrival(self, j):
+        theirs = self.whole.at[:, self.columns((self.z + self.count - j) % self.count)]
+        return send_to(
+            theirs, theirs, self.send.at[j - 1], self.recv.at[j - 1], tp=(self.z + j) % self.count
+        )
+
+    def begin(self):
+        for j in range(1, self.count):
+            self.copy(j).start()
+
+    def wait(self):
+        for j in range(1, self.count):
+            self.arrival(j).wait_recv()
+
+    def sent(self):
+        for j in range(1, self.count):
+            self.copy(j).wait_send()
+
+
+def line_peers(count):
+    z = lax.axis_index("tp")
+    return [(z + j) % count for j in range(1, count)]
+
+
+def mix_body(
+    tp_count,
+    rows,
+    partial_ref,
+    active_ref,
+    down_ref,
+    grad_ref,
+    mixed_ref,
+    part,
+    line,
+    near,
+    far,
+    first,
+    second,
+    near_send,
+    near_recv,
+    sum_send,
+    sum_recv,
+    line_send,
+    line_recv,
+    back_send,
+    back_recv,
+):
+    r = roles()
+    half = rows // HALF
+    unit = 2 * half
+    greet([r["p"], r["a"], r["b"]], line_peers(tp_count))
+    over_line = LineSum(tp_count, partial_ref, line, line_send, line_recv)
+    over_line.begin()
+    psum = PlaneSum(
+        r, part, near, far, first, second, half, (near_send, near_recv, sum_send, sum_recv)
+    )
+
+    @pl.loop(0, 8)
+    def _(step):
+        index = (step + 6) % 8
+        at = pl.ds(pl.multiple_of(index * unit, unit), unit)
+        part[at, :] = dot_nn(active_ref[at, :], down_ref[...]).astype(BF16)
+        for unit_done, copies in ((6, (6,)), (7, (7,)), (1, (0, 1)), (3, (2, 4)), (5, (3, 5))):
+
+            @pl.when(index == unit_done)
+            def _():
+                for copy in copies:
+                    psum.near_copy(copy).start()
+
+    for k in range(HALF):
+        psum.pass_far(k)
+    for k in range(HALF):
+        psum.pass_second(k)
+    for k in range(HALF):
+        psum.pass_first(k)
+    back = LineGather(tp_count, grad_ref, back_send, back_recv)
+    grad_ref[:, back.columns(back.z)] = over_line.total().astype(BF16)
+    back.begin()
+    for k in range(HALF):
+        mixed_ref[pl.ds(k * half, half), :] = psum.total(k).astype(BF16)
+    back.wait()
+    over_line.sent()
+    back.sent()
+    psum.sent()
+
+
+def mix_call(partial, active, down_matrix, tp_count):
+    rows, width = partial.shape
+    everything = active.shape[0]
+    half = rows // HALF
+    whole = jax.ShapeDtypeStruct((rows, width), BF16)
+    line_sems = pltpu.SemaphoreType.DMA((tp_count - 1,))
+    return pl.pallas_call(
+        functools.partial(mix_body, tp_count, rows),
+        out_shape=(whole, whole),
+        in_specs=[vmem_spec()] * 3,
+        out_specs=(vmem_spec(), vmem_spec()),
+        scratch_shapes=[
+            pltpu.VMEM((everything, width), BF16),
+            pltpu.VMEM((tp_count - 1, rows, width // tp_count), BF16),
+        ]
+        + plane_sum_scratch(half, width)
+        + [line_sems] * 4,
+        compiler_params=comm_params(2),
+        name="mix",
+    )(partial, active, down_matrix)
 
 
 def on_device(
@@ -134,6 +746,7 @@
     micro_rows = rows_dev // MICRO
     share_width = layer_in.shape[1]
     score_scale = HEAD_DIM ** (-0.5)
+    planes = ep_count == 8 and tp_count == 4
 
     send, recv = deal_matrices(token_order, ep_index, rows_dev, ep_count)
     both = jnp.concatenate([layer_in, grad_out], axis=1)
@@ -158,11 +771,22 @@
 
     expert_ids = jnp.arange(experts, dtype=jnp.int32)
     dense = jnp.sum(
-        jnp.where(routes[:, :, None] == expert_ids[None, None, :], route_weights[:, :, None], 0.0),
+        jnp.where(
+            routes.T[None, :, :] == expert_ids[:, None, None], route_weights.T[None, :, :], 0.0
+        ),
         axis=1,
     )
-    scale_all = lax.all_gather(dense, "ep", axis=0, tiled=True)
-    scale = lax.dynamic_slice_in_dim(scale_all, ep_index * local_experts, local_experts, 1)
+    terms = []
+    for _ in range(SCALE_TERMS):
+        terms.append(lax.reduce_precision(dense, 8, 7))
+        dense = dense - terms[-1]
+    scale_parts = jnp.concatenate(terms, axis=0).astype(BF16)
+    scale_all = lax.all_gather(scale_parts, "ep", axis=0, tiled=True)
+    flat_expert = ep_index * local_experts + jnp.repeat(
+        jnp.arange(local_experts, dtype=jnp.int32), hidden_here
+    )
+    part_expert = jnp.arange(scale_parts.shape[0], dtype=jnp.int32) % experts
+    pick = (part_expert[:, None] == flat_expert[None, :]).astype(BF16)
     all_grad = lax.all_gather(grad_full, "ep", axis=0, tiled=True)
 
     heads_here = q_width // HEAD_DIM
@@ -215,38 +839,51 @@
     unit_two = hidden * inverse_two
     moe_in = (unit_two * gain_moe).astype(BF16)
 
-    all_in = lax.all_gather(moe_in, "ep", axis=0, tiled=True)
     flat = local_experts * hidden_here
     gate_matrix = w_gate.reshape(flat, model_width)
     up_matrix = w_up.reshape(flat, model_width)
     down_matrix = w_down.reshape(flat, model_width)
-    row_scale = jnp.repeat(scale, hidden_here, axis=1)
-    gate_pre = dot_nt(all_in, gate_matrix)
-    up_pre = dot_nt(all_in, up_matrix)
-    grad_active = dot_nt(all_grad, down_matrix) * row_scale
-    sigmoid_gate = jax.nn.sigmoid(gate_pre)
-    silu_gate = gate_pre * sigmoid_gate
-    active = (silu_gate * up_pre * row_scale).astype(BF16)
-    grad_up_pre = (grad_active * silu_gate).astype(BF16)
-    grad_gate_pre = (
-        grad_active * up_pre * sigmoid_gate * (1.0 + gate_pre * (1.0 - sigmoid_gate))
-    ).astype(BF16)
-    grad_partial = dot_nn(grad_gate_pre, gate_matrix) + dot_nn(grad_up_pre, up_matrix)
-    grad_partial = lax.psum_scatter(
-        grad_partial.astype(BF16), "ep", scatter_dimension=0, tiled=True
-    )
-    grad_share = lax.psum_scatter(grad_partial, "tp", scatter_dimension=1, tiled=True)
-    out_partial = dot_nn(active, down_matrix)
-    out_partial = lax.psum_scatter(out_partial.astype(BF16), "ep", scatter_dimension=0, tiled=True)
-    mixed = lax.psum_scatter(out_partial, "tp", scatter_dimension=1, tiled=True)
+    if planes:
+        grad_partial, active, grad_w_gate, grad_w_up, grad_w_down = expert_call(
+            moe_in, all_grad, scale_all, pick, gate_matrix, up_matrix, down_matrix
+        )
+        grad_moe_in, mixed_plane = mix_call(grad_partial, active, down_matrix, tp_count)
+        mixed = lax.psum_scatter(mixed_plane, "tp", scatter_dimension=1, tiled=True)
+    else:
+        all_in = lax.all_gather(moe_in, "ep", axis=0, tiled=True)
+        parts_all = scale_all.reshape(ep_count, pick.shape[0], rows_dev)
+        row_scale = lax.dot_general(
+            parts_all, pick, (((1,), (0,)), ((), ())), preferred_element_type=F32
+        ).reshape(ep_count * rows_dev, flat)
+        gate_pre = dot_nt(all_in, gate_matrix)
+        up_pre = dot_nt(all_in, up_matrix)
+        grad_active = dot_nt(all_grad, down_matrix) * row_scale
+        sigmoid_gate = jax.nn.sigmoid(gate_pre)
+        silu_gate = gate_pre * sigmoid_gate
+        active = (silu_gate * up_pre * row_scale).astype(BF16)
+        grad_up_pre = (grad_active * silu_gate).astype(BF16)
+        grad_gate_pre = (
+            grad_active * up_pre * sigmoid_gate * (1.0 + gate_pre * (1.0 - sigmoid_gate))
+        ).astype(BF16)
+        grad_partial = dot_nn(grad_gate_pre, gate_matrix) + dot_nn(grad_up_pre, up_matrix)
+        grad_partial = lax.psum_scatter(
+            grad_partial.astype(BF16), "ep", scatter_dimension=0, tiled=True
+        )
+        grad_share = lax.psum_scatter(grad_partial, "tp", scatter_dimension=1, tiled=True)
+        grad_moe_in = lax.all_gather(grad_share, "tp", axis=1, tiled=True)
+        out_partial = dot_nn(active, down_matrix)
+        out_partial = lax.psum_scatter(
+            out_partial.astype(BF16), "ep", scatter_dimension=0, tiled=True
+        )
+        mixed = lax.psum_scatter(out_partial, "tp", scatter_dimension=1, tiled=True)
+        grad_w_down = dot_tn(active, all_grad)
+        grad_w_gate = dot_tn(grad_gate_pre, all_in)
+        grad_w_up = dot_tn(grad_up_pre, all_in)
     hidden_share = lax.dynamic_slice_in_dim(hidden, tp_index * share_width, share_width, 1)
     layer_dealt = (hidden_share + mixed.astype(F32)).astype(BF16)
-    grad_w_down = dot_tn(active, all_grad).reshape(w_down.shape)
-    grad_w_gate = dot_tn(grad_gate_pre, all_in).reshape(w_gate.shape)
-    grad_w_up = dot_tn(grad_up_pre, all_in).reshape(w_up.shape)
 
     grad_float = grad_full.astype(F32)
-    grad_moe_in = lax.all_gather(grad_share, "tp", axis=1, tiled=True).astype(F32)
+    grad_moe_in = grad_moe_in.astype(F32)
     norm_moe_part = jnp.sum(grad_moe_in * unit_two, axis=0)
     grad_hidden = grad_float + norm_back(grad_moe_in * gain_moe, unit_two, inverse_two)
     grad_attn = grad_hidden.astype(BF16)
@@ -341,9 +978,9 @@
         grad_norm_moe,
         grad_query_gain,
         grad_key_gain,
-        grad_w_gate,
-        grad_w_up,
-        grad_w_down,
+        grad_w_gate.reshape(w_gate.shape),
+        grad_w_up.reshape(w_up.shape),
+        grad_w_down.reshape(w_down.shape),
     )
 
 

time: 734 us -> 591 us (0.81)
  waiting for transfers between devices: 399 us -> 221 us
  Pallas kernels: 0 us -> 130 us
  matrix products: 125 us -> 33.2 us
    reduce_scatter x4 -> x1, waiting for transfers between devices: 164 us -> 17.4 us  [on_device(): mixed = lax.psum_scatter(mixed_plane, 'tp', scatter_dimension=1, tiled=True)]
    pallas_call x0 -> x2, Pallas kernels: none -> 130 us  [the longest x1 78.7 us: expert_call(): pl.pallas_call(functools.partial(expert_body, flat, rows, parts), out_sha...]
    all_gather x2 -> x0, waiting for transfers between devices: 74.4 us -> none  [the longest x1 45.1 us: on_device(): all_in = lax.all_gather(moe_in, 'ep', axis=0, tiled=True)]
    dot_general x8 -> x5, matrix products: 52.9 us -> 11.9 us  [dot_nn(): return jnp.dot(left, right, preferred_element_type=F32)]
    dot_general x6 -> x3, matrix products: 40.5 us -> 11.3 us  [dot_nt(): lax.dot_general(left_rows, right_matrix, (((1,), (1,)), ((), ())), prefer...]
    reduce_scatter x1, waiting for transfers between devices: 4.07 us -> 27.1 us  [on_device(): lax.psum_scatter(grad_packed, 'ep', scatter_dimension=0, tiled=True)]
    dot_general x8 -> x5, matrix products: 27.6 us -> 4.79 us  [dot_tn(): lax.dot_general(left_rows, right_rows, (((0,), (0,)), ((), ())), preferre...]
    all_gather x1, waiting for transfers between devices: 33.1 us -> 49.9 us  [on_device(): all_grad = lax.all_gather(grad_full, 'ep', axis=0, tiled=True)]
  transfers between devices with their start and end apart: 15 -> 10, of which waited for: 11 -> 8; matrix products, arithmetic and copies ran while one was open for 19% -> 11% of each run, Pallas kernels for 0% -> 0%
where the time goes in v2:
time: 591 us; the launch traced here: 582 us
  waiting for transfers between devices  221 us (37%)
  Pallas kernels  130 us (22%)
  blocking collectives  84.6 us (14%)
  other arithmetic  49.3 us (8%)
  local copies, waits for them, and re-layouts  39 us (7%)
  matrix products  33.2 us (6%)
  between operations  16.3 us (3%)
  starting transfers between devices  9.17 us (2%)
    pallas_call x1, Pallas kernels, expert_call(): pl.pallas_call(functools.partial(expert_body, flat, rows, parts), out_sha...  78.7 us
    all_gather x1, waiting for transfers between devices, on_device(): packed = lax.all_gather(packed, 'ep', axis=0, tiled=True)  56.5 us
    pallas_call x1, Pallas kernels, mix_call(): pl.pallas_call(functools.partial(mix_body, tp_count, rows), out_shape=(wh...  50.8 us
    all_gather x1, waiting for transfers between devices, on_device(): all_grad = lax.all_gather(grad_full, 'ep', axis=0, tiled=True)  49.9 us
    psum x1, blocking collectives, on_device(): small = lax.psum(small, ('ep', 'tp'))  41.3 us
    psum x1, waiting for transfers between devices, on_device(): attn_out = lax.psum(attn_part.astype(BF16), 'tp').astype(F32)  41.1 us
    reduce_scatter x1, waiting for transfers between devices, on_device(): lax.psum_scatter(grad_packed, 'ep', scatter_dimension=0, tiled=True)  27.1 us
    unnamed x1, blocking collectives  23.5 us
  transfers between devices with their start and end apart: 10, of which 8 were waited for; matrix products, arithmetic and copies ran while one was open for 11% of the time, Pallas kernels for 0%

profile of v2, /device:TPU:0, one launch (start us, length us, event | category | flops | bytes accessed | tf_op | source)
XLA Modules:
  0.0 582.1 jit_solution(13245355889574829418)
XLA Ops:
  9.1 2.2 convolution_convert_fusion.6
  11.3 5.2 all-to-all-start
  18.3 7.9 %all-to-all-done = bf16[8,32,1024]{2,1,0:T(8,128)(2,1)S(1)} async-done(((bf16[8,32,1024]{2,1,0:T(8,128)(2,1)}), bf16[8,32,1024]{2,1,0:T(8,128)(2,1)S(1)}, u32[]{:S(2)}, u32[]{:S(2)}) %all-to-all-start) | async-done | bytes 524320 | tf_op jit(solution)/shard_map/all_to_all | solution.py:110
  30.6 23.5 %all-reduce = bf16[4352]{0:T(1024)(128)(2,1)S(1)} all-reduce(bf16[4352]{0:T(1024)(128)(2,1)S(1)} %dynamic-update-slice), channel_id=2, replica_groups=mesh['ep'=8,'tp'=4] {'ep'}, use_global_device_ids=true, to_apply=%add | all-reduce | flops 4352 | bytes 17408
  57.5 1.6 fusion.18
  59.1 56.5 %all-gather.8.cloned.1.call-done = bf16[2048,2304]{1,0:T(8,128)(2,1)} async-done(((bf16[256,2304]{1,0:T(8,128)(2,1)}), bf16[2048,2304]{1,0:T(8,128)(2,1)}) %all-gather.8.cloned.1.call-update) | async-done | bytes 9437200 | tf_op jit(solution)/shard_map/all_gather | solution.py:759
  115.6 2.2 fusion.38
  117.8 3.6 fusion.6
  125.0 1.4 subtract_convert_fusion
  129.8 4.6 fusion.9
  134.6 11.2 %all-gather.10.cloned.1.call-done = bf16[256,2048]{1,0:T(8,128)(2,1)} async-done(((bf16[256,512]{1,0:T(8,128)(2,1)}), bf16[256,2048]{1,0:T(8,128)(2,1)}) %all-gather.10.cloned.1.call-update) | async-done | bytes 1048592 | tf_op jit(solution)/shard_map/all_gather | solution.py:755
  146.0 10.4 %all_gather.23.scale_hbm = bf16[384,256]{1,0:T(8,128)(2,1)} all-gather(bf16[48,256]{1,0:T(8,128)(2,1)S(1)} %pad_maximum_fusion.10), channel_id=1, replica_groups=mesh['ep'=8,'tp'=4] {'ep'}, dimensions={0}, use_global_device_ids=true | all-gather | bytes 221184 | tf_op jit(solution)/shard_map/all_gather | solution.py:784
  158.8 41.1 %all-reduce.3.cloned.1.call-done = bf16[256,2048]{1,0:T(8,128)(2,1)} async-done(((bf16[256,2048]{1,0:T(8,128)(2,1)}), bf16[256,2048]{1,0:T(8,128)(2,1)}) %all-reduce.3.cloned.1.call-update) | async-done | bytes 1048592 | tf_op jit(solution)/shard_map/psum | solution.py:836
  199.8 3.9 convert_add_fusion
  203.7 1.5 multiply_convert_fusion.own_hbm
  205.2 49.9 %all-gather.12.cloned.1.call-done.grad_hbm = bf16[2048,2048]{1,0:T(8,128)(2,1)} async-done(((bf16[256,2048]{1,0:T(8,128)(2,1)}), bf16[2048,2048]{1,0:T(8,128)(2,1)}) %all-gather.12.cloned.1.call-update) | async-done | bytes 8388624 | tf_op jit(solution)/shard_map/all_gather | solution.py:790
  255.1 78.7 %experts.1 = (bf16[256,2048]{1,0:T(8,128)(2,1)}, bf16[2048,384]{1,0:T(8,128)(2,1)}, f32[384,2048]{1,0:T(8,128)}, f32[384,2048]{1,0:T(8,128)}, f32[384,2048]{1,0:T(8,128)}) custom-call(bf16[256,2048]{1,0:T(8,128)(2,1)} %multiply_convert_fusion.own_hbm, bf16[2048,2048]{1,0:T(8,128)(2,1)} %all-gather.12.cloned.1.call-done.grad_hbm, ...), custom_call_target="tpu_custom_call" | custom-call | tf_op jit(solution)/shard_map/experts/pallas_call | solution.py:520
  333.8 50.8 %mix.1 = (bf16[256,2048]{1,0:T(8,128)(2,1)}, bf16[256,2048]{1,0:T(8,128)(2,1)}) custom-call(bf16[256,2048]{1,0:T(8,128)(2,1)} %get-tuple-element.20.partial_ref, bf16[2048,384]{1,0:T(8,128)(2,1)} %get-tuple-element.21.active_ref, bf16[384,2048]{1,0:T(8,128)(2,1)} %bitcast.148), custom_call_target="tpu_custom_call" | custom-call | tf_op jit(solution)/shard_map/mix/pallas_call | solution.py:704
  384.7 3.6 fusion.17
  388.3 2.2 fusion.16
  390.6 3.5 fusion.25
  396.6 1.4 fusion.19
  398.8 1.6 copy.105
  400.4 1.6 copy.106
  403.2 1.3 multiply_reduce_fusion.4
  404.6 1.4 multiply_convert_fusion.3
  406.0 2.2 fusion.30
  408.2 1.6 copy.104
  409.8 1.8 copy.78
  415.9 3.7 fusion.4
  419.7 2.9 fusion.8
  424.5 1.4 convolution_convert_fusion.1
  425.9 1.3 convolution_convert_fusion
  427.2 15.7 %pad_maximum_fusion = bf16[2048,2304]{0,1:T(8,128)(2,1)} fusion(bf16[2048,256]{0,1:T(8,128)(2,1)S(1)} %convolution_convert_fusion.2, bf16[2048,1024]{0,1:T(8,128)(2,1)S(1)} %convolution_convert_fusion, bf16[2048,1024]{0,1:T(8,128)(2,1)S(1)} %convolution_convert_fusion.1), kind=kLoop, calls=%fused_computation | loop fusion | flops 28311552 | bytes 18874368 | tf_op jit(solution)/shard_map/concatenate | solution.py:934
  443.1 9.2 %reduce-scatter.6.cloned.1.call-done = bf16[256,512]{1,0:T(8,128)(2,1)} async-done(((bf16[256,2048]{1,0:T(8,128)(2,1)}), bf16[256,512]{1,0:T(8,128)(2,1)}) %reduce-scatter.6.cloned.1.call-update) | async-done | bytes 262160 | tf_op jit(solution)/shard_map/reduce_scatter | solution.py:931
  452.2 1.3 fusion.46
  453.6 9.4 %psum.22 = f32[256]{0:T(256)S(1)} all-reduce(f32[256]{0:T(256)S(1)} %get-tuple-element.69), channel_id=1, replica_groups=mesh['ep'=8,'tp'=4] {'tp'}, use_global_device_ids=true, to_apply=%region_21.22 | all-reduce | flops 256 | bytes 2048 | tf_op jit(solution)/shard_map/psum | solution.py:949
  462.9 17.4 %reduce-scatter.4.cloned.1.call-done = bf16[256,512]{1,0:T(8,128)(2,1)} async-done(((bf16[256,2048]{1,0:T(8,128)(2,1)}), bf16[256,512]{1,0:T(8,128)(2,1)}) %reduce-scatter.4.cloned.1.call-update) | async-done | bytes 262160 | tf_op jit(solution)/shard_map/reduce_scatter | solution.py:851
  484.1 3.6 all-to-all-start.1
  488.1 41.3 %psum.23 = f32[4352]{0:T(1024)S(1)} all-reduce(f32[4352]{0:T(1024)S(1)} %pad_maximum_fusion.11), channel_id=1, replica_groups=mesh['ep'=8,'tp'=4] {'ep','tp'}, use_global_device_ids=true, to_apply=%region_28.29 | all-reduce | flops 4352 | bytes 34816 | tf_op jit(solution)/shard_map/psum | solution.py:957
  532.6 27.1 %reduce-scatter.8.cloned.1.call-done = bf16[256,2304]{0,1:T(8,128)(2,1)} async-done(((bf16[2048,2304]{0,1:T(8,128)(2,1)}), bf16[256,2304]{0,1:T(8,128)(2,1)}) %reduce-scatter.8.cloned.1.call-update) | async-done | bytes 1179664 | tf_op jit(solution)/shard_map/reduce_scatter | solution.py:942
  559.7 1.4 fusion.97
  561.0 1.3 copy.82
  562.4 1.3 copy.85
  566.1 4.1 copy.138
  570.1 1.7 copy.139
  571.8 1.4 copy-done.15
  573.2 1.7 copy.140
  (258 shorter events, 40.1 us)
Async XLA Ops:
  9.1 18.4 %copy-start.28 = (bf16[256,1024]{1,0:T(8,128)(2,1)S(1)}, bf16[256,1024]{1,0:T(8,128)(2,1)}, u32[]{:S(2)}) copy-start(bf16[256,1024]{1,0:T(8,128)(2,1)} %param.25) | copy-start | bytes 1572868
  9.1 18.4 %copy-start.29 = (bf16[256,1024]{1,0:T(8,128)(2,1)S(1)}, bf16[256,1024]{1,0:T(8,128)(2,1)}, u32[]{:S(2)}) copy-start(bf16[256,1024]{1,0:T(8,128)(2,1)} %param.22) | copy-start | bytes 1572868
  9.1 18.5 %copy-start.40 = (bf16[256,128]{1,0:T(8,128)(2,1)S(1)}, bf16[256,128]{1,0:T(8,128)(2,1)}, u32[]{:S(2)}) copy-start(bf16[256,128]{1,0:T(8,128)(2,1)} %param.24) | copy-start | bytes 196612
  9.1 18.5 %copy-start.41 = (bf16[256,128]{1,0:T(8,128)(2,1)S(1)}, bf16[256,128]{1,0:T(8,128)(2,1)}, u32[]{:S(2)}) copy-start(bf16[256,128]{1,0:T(8,128)(2,1)} %param.23) | copy-start | bytes 196612
  11.3 14.9 %all-to-all-start = ((bf16[8,32,1024]{2,1,0:T(8,128)(2,1)}), bf16[8,32,1024]{2,1,0:T(8,128)(2,1)S(1)}, u32[]{:S(2)}, u32[]{:S(2)}) async-start(bf16[8,32,1024]{2,1,0:T(8,128)(2,1)} %bitcast), calls=%async_computation | async-start | bytes 1048576 | tf_op jit(solution)/shard_map/all_to_all | solution.py:110
  16.5 40.9 %all-gather.6.cloned.1.call-start = ((), (), s32[]{:S(2)}) async-start(), calls=%async_computation.5 | async-start | bytes 1310720 | tf_op jit(solution)/shard_map/all_gather | solution.py:754
  18.3 10.4 %copy-start.61 = (s32[256]{0:T(256)}, s32[256]{0:T(256)S(1)}, u32[]{:S(2)}) copy-start(s32[256]{0:T(256)S(1)} %multiply_add_fusion.1) | copy-start | bytes 3076
  27.5 88.1 %all-gather.8.cloned.1.call-start = ((), (), s32[]{:S(2)}) async-start(), calls=%async_computation.6 | async-start | bytes 10616832 | tf_op jit(solution)/shard_map/all_gather | solution.py:759
  28.7 117.0 %all-gather.10.cloned.1.call-start = ((), (), s32[]{:S(2)}) async-start(), calls=%async_computation.8 | async-start | bytes 1310720 | tf_op jit(solution)/shard_map/all_gather | solution.py:755
  54.9 67.1 %copy-start.54 = (f32[128]{0:T(128)}, f32[128]{0:T(128)S(1)}, u32[]{:S(2)}) copy-start(f32[128]{0:T(128)S(1)} %mul.432) | copy-start | bytes 1540
  55.1 67.1 %copy-start.55 = (f32[128]{0:T(128)}, f32[128]{0:T(128)S(1)}, u32[]{:S(2)}) copy-start(f32[128]{0:T(128)S(1)} %mul.446) | copy-start | bytes 1540
  55.1 67.4 %copy-start.60 = (f32[64]{0:T(128)}, f32[64]{0:T(128)S(1)}, u32[]{:S(2)}) copy-start(f32[64]{0:T(128)S(1)} %multiply_power_fusion) | copy-start | bytes 772
  55.3 67.2 %copy-start.47 = (f32[256]{0:T(256)}, f32[256]{0:T(256)S(1)}, u32[]{:S(2)}) copy-start(f32[256]{0:T(256)S(1)} %convert_bitcast_fusion.1) | copy-start | bytes 3076
  57.4 142.5 %all-reduce.3.cloned.1.call-start = ((), (), s32[]{:S(2)}) async-start(), calls=%async_computation.7 | async-start | bytes 2097152 | tf_op jit(solution)/shard_map/psum | solution.py:836
  57.4 60.4 %copy-start = (bf16[256,2048]{1,0:T(8,128)(2,1)S(1)}, bf16[256,2048]{1,0:T(8,128)(2,1)}, u32[]{:S(2)}) copy-start(bf16[256,2048]{1,0:T(8,128)(2,1)} %all-gather.6.cloned.1.call-done) | copy-start | bytes 3145732
  59.1 62.4 %copy-start.44 = (f32[256]{0:T(256)}, f32[256]{0:T(256)S(1)}, u32[]{:S(2)}) copy-start(f32[256]{0:T(256)S(1)} %add_rsqrt_fusion.3) | copy-start | bytes 3076
  117.8 4.2 copy-start.49
  128.9 5.5 copy-start.38
  129.8 4.7 copy-start.20
  134.5 11.4 %copy-start.43 = (f32[1,2,8,128]{3,2,1,0:T(8,128)S(1)}, f32[1,2,8,128]{3,2,1,0:T(8,128)}, u32[]{:S(2)}) copy-start(f32[1,2,8,128]{3,2,1,0:T(8,128)} %get-tuple-element.101) | copy-start | bytes 24580
  134.5 11.5 %copy-start.58 = (f32[256,8]{0,1:T(8,128)S(1)}, f32[256,8]{0,1:T(8,128)}, u32[]{:S(2)}) copy-start(f32[256,8]{0,1:T(8,128)} %param.21) | copy-start | bytes 24580
  134.5 11.5 %copy-start.59 = (s32[256,8]{0,1:T(8,128)S(1)}, s32[256,8]{0,1:T(8,128)}, u32[]{:S(2)}) copy-start(s32[256,8]{0,1:T(8,128)} %param.20) | copy-start | bytes 24580
  134.5 21.9 %copy-start.56 = (f32[128]{0:T(128)S(1)}, f32[128]{0:T(128)}, u32[]{:S(2)}) copy-start(f32[128]{0:T(128)} %copy-done.55) | copy-start | bytes 1540
  134.5 65.3 %copy-start.45 = (f32[256]{0:T(256)S(1)}, f32[256]{0:T(256)}, u32[]{:S(2)}) copy-start(f32[256]{0:T(256)} %copy-done.44) | copy-start | bytes 3076
  134.5 120.6 %all-gather.12.cloned.1.call-start = ((), (), s32[]{:S(2)}) async-start(), calls=%async_computation.9 | async-start | bytes 9437184 | tf_op jit(solution)/shard_map/all_gather | solution.py:790
  145.8 306.5 %reduce-scatter.6.cloned.1.call-start = ((), (), s32[]{:S(2)}) async-start(), calls=%async_computation.11 | async-start | bytes 1310720 | tf_op jit(solution)/shard_map/reduce_scatter | solution.py:931
  145.8 57.9 %copy-start.35 = (f32[1,2,8,128]{3,1,2,0:T(2,128)}, f32[1,2,8,128]{3,1,2,0:T(2,128)S(1)}, u32[]{:S(2)}) copy-start(f32[1,2,8,128]{3,1,2,0:T(2,128)S(1)} %copy.110) | copy-start | bytes 24580
  199.8 3.9 copy-start.6
  384.7 3.6 copy-start.1
  384.7 3.6 copy-start.7
  390.5 3.7 copy-start.5
  390.5 3.7 copy-start.33
  390.6 3.7 copy-start.39
  396.2 5.8 %copy-start.48 = (f32[256]{0:T(256)S(1)}, f32[256]{0:T(256)}, u32[]{:S(2)}) copy-start(f32[256]{0:T(256)} %copy-done.47) | copy-start | bytes 3076
  396.2 7.0 %copy-start.50 = (f32[256]{0:T(256)S(1)}, f32[256]{0:T(256)}, u32[]{:S(2)}) copy-start(f32[256]{0:T(256)} %copy-done.49) | copy-start | bytes 3076
  406.0 5.6 copy-start.22
  406.0 5.6 copy-start.27
  415.9 3.8 copy-start.17
  415.9 3.8 copy-start.30
  415.9 3.8 copy-start.31
  422.7 57.7 %reduce-scatter.4.cloned.1.call-start = ((), (), s32[]{:S(2)}) async-start(), calls=%async_computation.10 | async-start | bytes 1310720 | tf_op jit(solution)/shard_map/reduce_scatter | solution.py:851
  423.4 136.3 %reduce-scatter.8.cloned.1.call-start = ((), (), s32[]{:S(2)}) async-start(), calls=%async_computation.12 | async-start | bytes 10616832 | tf_op jit(solution)/shard_map/reduce_scatter | solution.py:942
  443.0 39.9 %copy-start.62 = (s32[256]{0:T(256)S(1)}, s32[256]{0:T(256)}, u32[]{:S(2)}) copy-start(s32[256]{0:T(256)} %copy-done.61) | copy-start | bytes 3076
  481.5 6.2 %copy-start.42 = (f32[2048]{0:T(1024)S(1)}, f32[2048]{0:T(1024)}, u32[]{:S(2)}) copy-start(f32[2048]{0:T(1024)} %get-tuple-element.66) | copy-start | bytes 24580
  481.6 6.5 %copy-start.66 = (f32[128]{0:T(128)S(1)}, f32[128]{0:T(128)}, u32[]{:S(2)}) copy-start(f32[128]{0:T(128)} %get-tuple-element.70) | copy-start | bytes 1540
  481.6 49.1 %copy-start.65 = (s32[256]{0:T(256)S(1)}, s32[256]{0:T(256)}, u32[]{:S(2)}) copy-start(s32[256]{0:T(256)} %copy-done.64) | copy-start | bytes 3076
  484.1 46.5 %all-to-all-start.1 = ((bf16[8,32,1024]{2,1,0:T(8,128)(2,1)}), bf16[8,32,1024]{2,1,0:T(8,128)(2,1)S(1)}, u32[]{:S(2)}, u32[]{:S(2)}) async-start(bf16[8,32,1024]{2,1,0:T(8,128)(2,1)} %bitcast.46), calls=%async_computation.3 | async-start | bytes 1048576 | tf_op jit(solution)/shard_map/all_to_all | solution.py:110
  566.1 4.1 copy-start.16
  (34 other events, 57.6 us)
Sparse Core Ops, SparseCore 0:
  27.6 27.3 all-gather.5
  57.5 58.0 all-gather.7
  117.7 27.9 all-gather.9
  148.5 51.2 all-reduce.2
  201.6 53.5 all-gather.11
  422.8 29.4 reduce-scatter.5
  454.5 25.7 reduce-scatter.3
  483.8 75.7 reduce-scatter.7

commit v3 on v2

--- a/solution.py
+++ b/solution.py
@@ -364,12 +364,13 @@
     ]
     for load in loads:
         load.start()
+    stride = scale_hbm.shape[0] // 8
     slots = []
     for index, (owner, k) in enumerate(owners):
         slots.append(
             (
                 pltpu.make_async_copy(
-                    scale_hbm.at[pl.ds(owner * parts, parts), pl.ds(k * half, half)],
+                    scale_hbm.at[pl.ds(owner * stride, parts), pl.ds(k * half, half)],
                     scales.at[index],
                     grad_sem.at[0, index],
                 ),
@@ -594,38 +595,97 @@
             self.copy(j).wait_send()
 
 
+class OrderedGather(PlaneGather):
+    def place(self, name, k):
+        return self.held.at[pl.ds((self.r[name] * HALF + k) * self.half, self.half)]
+
+    def copy(self, kind, k):
+        source, device = (
+            ("e", "a"),
+            ("e", "b"),
+            ("e", "p"),
+            ("a", "b"),
+            ("a", "p"),
+            ("b", "p"),
+            ("d", "p"),
+        )[kind]
+        block = self.place(source, k)
+        return send_to(
+            block, block, self.send.at[kind, k], self.recv.at[kind, k], ep=self.r[device]
+        )
+
+    def arrived(self, kind, k):
+        source, device = (
+            ("a", "a"),
+            ("b", "b"),
+            ("p", "p"),
+            ("d", "b"),
+            ("pb", "p"),
+            ("pa", "p"),
+            ("pd", "p"),
+        )[kind]
+        block = self.place(source, k)
+        send_to(
+            block, block, self.send.at[kind, k], self.recv.at[kind, k], ep=self.r[device]
+        ).wait_recv()
+
+    def finish(self):
+        for k in range(HALF):
+            for kind in (2, 4, 5, 6):
+                self.arrived(kind, k)
+
+
 class LineGather:
-    def __init__(self, count, whole, send, recv):
-        self.count, self.whole, self.send, self.recv = count, whole, send, recv
+    def __init__(self, count, whole, up_send, up_recv, down_send, down_recv):
+        self.count, self.whole = count, whole
+        self.up_sems, self.down_sems = (up_send, up_recv), (down_send, down_recv)
         self.z = lax.axis_index("tp")
         self.share = whole.shape[1] // count
 
     def columns(self, z):
         return pl.ds(pl.multiple_of(z * self.share, self.share), self.share)
 
-    def copy(self, j):
-        mine = self.whole.at[:, self.columns(self.z)]
-        return send_to(
-            mine, mine, self.send.at[j - 1], self.recv.at[j - 1], tp=(self.z + j) % self.count
-        )
-
-    def arrival(self, j):
-        theirs = self.whole.at[:, self.columns((self.z + self.count - j) % self.count)]
-        return send_to(
-            theirs, theirs, self.send.at[j - 1], self.recv.at[j - 1], tp=(self.z + j) % self.count
-        )
+    def move(self, share, j, sems, target):
+        block = self.whole.at[:, self.columns(share)]
+        return send_to(block, block, sems[0].at[j - 1], sems[1].at[j - 1], tp=target)
+
+    def up(self, j):
+        return self.move(self.z - j + 1, j, self.up_sems, self.z + 1)
+
+    def down(self, j):
+        return self.move(self.z + j - 1, j, self.down_sems, self.z - 1)
+
+    def sends(self, j, act):
+        @pl.when((self.z < self.count - 1) & (self.z >= j - 1))
+        def _():
+            act(self.up(j))
+
+        @pl.when((self.z > 0) & (self.z + j <= self.count))
+        def _():
+            act(self.down(j))
 
     def begin(self):
-        for j in range(1, self.count):
-            self.copy(j).start()
+        self.sends(1, lambda copy: copy.start())
+
+    def step(self, j):
+        @pl.when(self.z >= j)
+        def _():
+            self.move(self.z - j, j, self.up_sems, self.z - 1).wait_recv()
+
+        @pl.when(self.z + j < self.count)
+        def _():
+            self.move(self.z + j, j, self.down_sems, self.z + 1).wait_recv()
+
+        if j + 1 < self.count:
+            self.sends(j + 1, lambda copy: copy.start())
 
     def wait(self):
         for j in range(1, self.count):
-            self.arrival(j).wait_recv()
+            self.step(j)
 
     def sent(self):
         for j in range(1, self.count):
-            self.copy(j).wait_send()
+            self.sends(j, lambda copy: copy.wait_send())
 
 
 def line_peers(count):
@@ -653,8 +713,7 @@
     sum_recv,
     line_send,
     line_recv,
-    back_send,
-    back_recv,
+    back_line,
 ):
     r = roles()
     half = rows // HALF
@@ -684,12 +743,14 @@
         psum.pass_second(k)
     for k in range(HALF):
         psum.pass_first(k)
-    back = LineGather(tp_count, grad_ref, back_send, back_recv)
+    back = LineGather(tp_count, grad_ref, *[back_line.at[i] for i in range(4)])
     grad_ref[:, back.columns(back.z)] = over_line.total().astype(BF16)
     back.begin()
+    back.step(1)
+    back.step(2)
     for k in range(HALF):
         mixed_ref[pl.ds(k * half, half), :] = psum.total(k).astype(BF16)
-    back.wait()
+    back.step(3)
     over_line.sent()
     back.sent()
     psum.sent()
@@ -711,13 +772,301 @@
             pltpu.VMEM((tp_count - 1, rows, width // tp_count), BF16),
         ]
         + plane_sum_scratch(half, width)
-        + [line_sems] * 4,
+        + [line_sems] * 2
+        + [pltpu.SemaphoreType.DMA((4, tp_count - 1))],
         compiler_params=comm_params(2),
         name="mix",
     )(partial, active, down_matrix)
 
 
-def on_device(
+def turn(values, cosine, sine_table):
+    return values * cosine + pltpu.roll(values, HEAD_DIM // 2, 1) * sine_table
+
+
+def unit_of(values):
+    return values * lax.rsqrt(jnp.mean(values * values, axis=-1, keepdims=True) + epsilon)
+
+
+def front_body(
+    gain_at,
+    ep_count,
+    tp_count,
+    rows,
+    heads,
+    send_ref,
+    recv_ref,
+    small_ref,
+    cosine_ref,
+    sine_ref,
+    mask_ref,
+    query_hbm,
+    key_hbm,
+    value_hbm,
+    out_hbm,
+    x_ref,
+    grad_ref,
+    hidden_ref,
+    moe_ref,
+    proj_ref,
+    turned_ref,
+    keys_ref,
+    values_ref,
+    probs_ref,
+    context_ref,
+    small_all,
+    normed,
+    all_grad,
+    w_in_hbm,
+    w_out_hbm,
+    w_in,
+    w_out,
+    dealt,
+    x_wire,
+    grad_wire,
+    back_wire,
+    attn,
+    line,
+    deal_send,
+    deal_recv,
+    small_send,
+    small_recv,
+    in_send,
+    in_recv,
+    out_send,
+    out_recv,
+    grad_send,
+    grad_recv,
+    x_line,
+    grad_line,
+    back_line,
+    line_send,
+    line_recv,
+    local_sem,
+):
+    r = roles()
+    e = r["e"]
+    z = lax.axis_index("tp")
+    half = rows // HALF
+    q_width = heads * HEAD_DIM
+    share = x_wire.shape[1] // tp_count
+    per_pair = rows // ep_count
+    micro_rows = rows // MICRO
+    own = pl.ds(e * rows, rows)
+    loads = [
+        pltpu.make_async_copy(query_hbm, w_in.at[own, pl.ds(0, q_width)], local_sem.at[0]),
+        pltpu.make_async_copy(key_hbm, w_in.at[own, pl.ds(q_width, HEAD_DIM)], local_sem.at[1]),
+        pltpu.make_async_copy(
+            value_hbm, w_in.at[own, pl.ds(q_width + HEAD_DIM, HEAD_DIM)], local_sem.at[2]
+        ),
+        pltpu.make_async_copy(out_hbm, w_out.at[own], local_sem.at[3]),
+    ]
+    for load in loads:
+        load.start()
+    small_rows = small_ref.shape[0]
+    small_all[pl.ds(e * small_rows, small_rows), :] = small_ref[...]
+    others = [(e + j) % ep_count for j in range(1, ep_count)]
+    greet(others, line_peers(tp_count))
+
+    def deal(j, source, target):
+        return send_to(
+            send_ref.at[pl.ds(target * per_pair, per_pair)],
+            dealt.at[pl.ds(source * per_pair, per_pair)],
+            deal_send.at[j - 1],
+            deal_recv.at[j - 1],
+            ep=target,
+        )
+
+    for j in range(1, ep_count):
+        deal(j, e, (e + j) % ep_count).start()
+    mine = pl.ds(pl.multiple_of(e * per_pair, per_pair), per_pair)
+    dealt[mine, :] = send_ref[mine, :]
+    gather_small = OrderedGather(r, small_all, small_rows // HALF, small_send, small_recv)
+    gather_in = OrderedGather(r, w_in, half, in_send, in_recv)
+    gather_out = OrderedGather(r, w_out, half, out_send, out_recv)
+    gather_grad = OrderedGather(r, all_grad, half, grad_send, grad_recv)
+    gather_small.begin()
+    for load in loads:
+        load.wait()
+    gather_in.begin()
+    for j in range(1, ep_count):
+        deal(j, (e + ep_count - j) % ep_count, (e + j) % ep_count).wait_recv()
+    x_gather = LineGather(tp_count, x_wire, *[x_line.at[i] for i in range(4)])
+    grad_gather = LineGather(tp_count, grad_wire, *[grad_line.at[i] for i in range(4)])
+    x_wire[:, x_gather.columns(z)] = dealt[:, :share]
+    grad_wire[:, x_gather.columns(z)] = dealt[:, share:]
+    x_gather.begin()
+    for k in range(HALF):
+        gather_small.pass_near(k)
+    x_gather.step(1)
+    gather_in.pass_near(0)
+    x_gather.step(2)
+    grad_gather.begin()
+    gather_in.pass_near(1)
+    gather_out.begin()
+    x_gather.step(3)
+    for k in range(HALF):
+        gather_small.pass_far(k)
+    gather_small.finish()
+
+    def gain_row(place, column, width):
+        at = place * small_rows + gain_at
+        return small_all[at : at + 1, column : column + width].astype(F32)
+
+    x_rows = dot_nn(recv_ref[...], x_wire[...])
+    x_ref[...] = x_rows.astype(BF16)
+    unit_one = unit_of(x_rows)
+    for place in range(ep_count):
+        at = slice(place * rows, (place + 1) * rows)
+        normed[:, at] = (unit_one[:, at] * gain_row(place, 0, rows)).astype(BF16)
+    for k in range(HALF):
+        gather_in.pass_far(k)
+    grad_gather.step(1)
+    gather_in.finish()
+    gather_out.pass_near(0)
+
+    proj_ref[...] = dot_nn(normed[...], w_in[...])
+    grad_gather.step(2)
+    gather_out.pass_near(1)
+    column = 2 * rows
+    gain_query = sum(gain_row(place, column, HEAD_DIM) for place in range(ep_count))
+    gain_key = sum(gain_row(place, column + HEAD_DIM, HEAD_DIM) for place in range(ep_count))
+    cosine, sine_table = cosine_ref[...], sine_ref[...]
+    keys_ref[...] = turn(
+        unit_of(proj_ref[:, q_width : q_width + HEAD_DIM]) * gain_key, cosine, sine_table
+    ).astype(BF16)
+    values_ref[...] = proj_ref[:, q_width + HEAD_DIM :].astype(BF16)
+
+    @pl.loop(0, heads)
+    def _(head):
+        lanes = pl.ds(pl.multiple_of(head * HEAD_DIM, HEAD_DIM), HEAD_DIM)
+        queries = turn(unit_of(proj_ref[:, lanes]) * gain_query, cosine, sine_table).astype(BF16)
+        for micro in range(MICRO):
+            at = pl.ds(
+                pl.multiple_of((micro * heads + head) * micro_rows, micro_rows), micro_rows
+            )
+            turned_ref[at, :] = queries[micro * micro_rows : (micro + 1) * micro_rows]
+
+    grad_gather.step(3)
+    for micro in range(MICRO):
+        within = slice(micro * micro_rows, (micro + 1) * micro_rows)
+        stacked = slice(micro * heads * micro_rows, (micro + 1) * heads * micro_rows)
+        scores = dot_nt(turned_ref[stacked, :], keys_ref[within, :]) * HEAD_DIM ** (-0.5)
+        mask = mask_ref[within, :]
+        scores = scores.reshape(heads, micro_rows, micro_rows)
+        scores = jnp.where(mask[None] > 0.0, scores, -1e30)
+        exponent = jnp.exp(scores - jnp.max(scores, axis=-1, keepdims=True))
+        probs = exponent / jnp.sum(exponent, axis=-1, keepdims=True)
+        probs = probs.reshape(heads * micro_rows, micro_rows)
+        probs_ref[stacked, :] = probs
+        context = dot_nn(probs.astype(BF16), values_ref[within, :]).astype(BF16)
+        for head in range(heads):
+            context_ref[within, head * HEAD_DIM : (head + 1) * HEAD_DIM] = context[
+                head * micro_rows : (head + 1) * micro_rows
+            ]
+
+    grad_ref[...] = dot_nn(recv_ref[...], grad_wire[...]).astype(BF16)
+    grad_here = pltpu.make_async_copy(grad_ref, all_grad.at[own], local_sem.at[4])
+    grad_here.start()
+    for k in range(HALF):
+        gather_out.pass_far(k)
+    grad_here.wait()
+    gather_grad.begin()
+    gather_out.finish()
+
+    attn[...] = dot_nt(context_ref[...], w_out[...]).astype(BF16)
+    over_line = LineSum(tp_count, attn, line, line_send, line_recv)
+    over_line.begin()
+    w_in_out = pltpu.make_async_copy(w_in, w_in_hbm, local_sem.at[0])
+    w_out_out = pltpu.make_async_copy(w_out, w_out_hbm, local_sem.at[1])
+    w_in_out.start()
+    w_out_out.start()
+    gather_grad.pass_near(0)
+    total = over_line.total()
+    back = LineGather(tp_count, back_wire, *[back_line.at[i] for i in range(4)])
+    back_wire[:, back.columns(z)] = total.astype(BF16)
+    back.begin()
+    back.step(1)
+    gather_grad.pass_near(1)
+    back.step(2)
+    gather_grad.pass_far(0)
+    back.step(3)
+    hidden = x_ref[...].astype(F32) + back_wire[...].astype(F32)
+    hidden_ref[...] = hidden
+    unit_two = unit_of(hidden)
+    for place in range(ep_count):
+        at = slice(place * rows, (place + 1) * rows)
+        moe_ref[:, at] = (unit_two[:, at] * gain_row(place, rows, rows)).astype(BF16)
+    gather_grad.pass_far(1)
+    gather_grad.finish()
+    for j in range(1, ep_count):
+        deal(j, e, (e + j) % ep_count).wait_send()
+    x_gather.sent()
+    grad_gather.sent()
+    back.sent()
+    over_line.sent()
+    for gather in (gather_small, gather_in, gather_out, gather_grad):
+        gather.sent()
+    w_in_out.wait()
+    w_out_out.wait()
+
+
+def front_call(
+    gain_at, ep_count, tp_count, send_rows, recv, small, cosine, sine_table, mask, query, key, value, out
+):
+    rows = send_rows.shape[0]
+    share = send_rows.shape[1] // 2
+    width = share * tp_count
+    q_width = query.shape[1]
+    heads = q_width // HEAD_DIM
+    everything = rows * ep_count
+    in_width = q_width + 2 * HEAD_DIM
+    micro_rows = rows // MICRO
+    shape = jax.ShapeDtypeStruct
+    gather_sems = pltpu.SemaphoreType.DMA((PlaneGather.kinds, HALF))
+    line_sems = pltpu.SemaphoreType.DMA((4, tp_count - 1))
+    return pl.pallas_call(
+        functools.partial(front_body, gain_at, ep_count, tp_count, rows, heads),
+        out_shape=(
+            shape((rows, width), BF16),
+            shape((rows, width), BF16),
+            shape((rows, width), F32),
+            shape((rows, width), BF16),
+            shape((rows, in_width), F32),
+            shape((heads * rows, HEAD_DIM), BF16),
+            shape((rows, HEAD_DIM), BF16),
+            shape((rows, HEAD_DIM), BF16),
+            shape((heads * rows, micro_rows), F32),
+            shape((rows, q_width), BF16),
+            shape((ep_count * small.shape[0], small.shape[1]), BF16),
+            shape((rows, width), BF16),
+            shape((everything, width), BF16),
+            shape((everything, in_width), BF16),
+            shape((everything, q_width), BF16),
+        ),
+        in_specs=[vmem_spec()] * 6 + [any_spec()] * 4,
+        out_specs=tuple([vmem_spec()] * 12 + [any_spec()] * 3),
+        scratch_shapes=[
+            pltpu.VMEM((everything, in_width), BF16),
+            pltpu.VMEM((everything, q_width), BF16),
+            pltpu.VMEM(send_rows.shape, BF16),
+            pltpu.VMEM((rows, width), BF16),
+            pltpu.VMEM((rows, width), BF16),
+            pltpu.VMEM((rows, width), BF16),
+            pltpu.VMEM((rows, width), BF16),
+            pltpu.VMEM((tp_count - 1, rows, share), BF16),
+            pltpu.SemaphoreType.DMA((ep_count - 1,)),
+            pltpu.SemaphoreType.DMA((ep_count - 1,)),
+        ]
+        + [gather_sems] * 8
+        + [line_sems] * 3
+        + [pltpu.SemaphoreType.DMA((tp_count - 1,))] * 2
+        + [pltpu.SemaphoreType.DMA((5,))],
+        compiler_params=comm_params(3),
+        name="front",
+    )(send_rows, recv, small, cosine, sine_table, mask, query, key, value, out)
+
+
+def plain_layer(
     layer_in,
     token_order,
     seq_lengths,
@@ -746,7 +1095,6 @@
     micro_rows = rows_dev // MICRO
     share_width = layer_in.shape[1]
     score_scale = HEAD_DIM ** (-0.5)
-    planes = ep_count == 8 and tp_count == 4
 
     send, recv = deal_matrices(token_order, ep_index, rows_dev, ep_count)
     both = jnp.concatenate([layer_in, grad_out], axis=1)
@@ -771,22 +1119,11 @@
 
     expert_ids = jnp.arange(experts, dtype=jnp.int32)
     dense = jnp.sum(
-        jnp.where(
-            routes.T[None, :, :] == expert_ids[:, None, None], route_weights.T[None, :, :], 0.0
-        ),
+        jnp.where(routes[:, :, None] == expert_ids[None, None, :], route_weights[:, :, None], 0.0),
         axis=1,
     )
-    terms = []
-    for _ in range(SCALE_TERMS):
-        terms.append(lax.reduce_precision(dense, 8, 7))
-        dense = dense - terms[-1]
-    scale_parts = jnp.concatenate(terms, axis=0).astype(BF16)
-    scale_all = lax.all_gather(scale_parts, "ep", axis=0, tiled=True)
-    flat_expert = ep_index * local_experts + jnp.repeat(
-        jnp.arange(local_experts, dtype=jnp.int32), hidden_here
-    )
-    part_expert = jnp.arange(scale_parts.shape[0], dtype=jnp.int32) % experts
-    pick = (part_expert[:, None] == flat_expert[None, :]).astype(BF16)
+    scale_all = lax.all_gather(dense, "ep", axis=0, tiled=True)
+    scale = lax.dynamic_slice_in_dim(scale_all, ep_index * local_experts, local_experts, 1)
     all_grad = lax.all_gather(grad_full, "ep", axis=0, tiled=True)
 
     heads_here = q_width // HEAD_DIM
@@ -839,48 +1176,290 @@
     unit_two = hidden * inverse_two
     moe_in = (unit_two * gain_moe).astype(BF16)
 
+    all_in = lax.all_gather(moe_in, "ep", axis=0, tiled=True)
     flat = local_experts * hidden_here
     gate_matrix = w_gate.reshape(flat, model_width)
     up_matrix = w_up.reshape(flat, model_width)
     down_matrix = w_down.reshape(flat, model_width)
-    if planes:
-        grad_partial, active, grad_w_gate, grad_w_up, grad_w_down = expert_call(
-            moe_in, all_grad, scale_all, pick, gate_matrix, up_matrix, down_matrix
-        )
-        grad_moe_in, mixed_plane = mix_call(grad_partial, active, down_matrix, tp_count)
-        mixed = lax.psum_scatter(mixed_plane, "tp", scatter_dimension=1, tiled=True)
-    else:
-        all_in = lax.all_gather(moe_in, "ep", axis=0, tiled=True)
-        parts_all = scale_all.reshape(ep_count, pick.shape[0], rows_dev)
-        row_scale = lax.dot_general(
-            parts_all, pick, (((1,), (0,)), ((), ())), preferred_element_type=F32
-        ).reshape(ep_count * rows_dev, flat)
-        gate_pre = dot_nt(all_in, gate_matrix)
-        up_pre = dot_nt(all_in, up_matrix)
-        grad_active = dot_nt(all_grad, down_matrix) * row_scale
-        sigmoid_gate = jax.nn.sigmoid(gate_pre)
-        silu_gate = gate_pre * sigmoid_gate
-        active = (silu_gate * up_pre * row_scale).astype(BF16)
-        grad_up_pre = (grad_active * silu_gate).astype(BF16)
-        grad_gate_pre = (
-            grad_active * up_pre * sigmoid_gate * (1.0 + gate_pre * (1.0 - sigmoid_gate))
-        ).astype(BF16)
-        grad_partial = dot_nn(grad_gate_pre, gate_matrix) + dot_nn(grad_up_pre, up_matrix)
-        grad_partial = lax.psum_scatter(
-            grad_partial.astype(BF16), "ep", scatter_dimension=0, tiled=True
-        )
-        grad_share = lax.psum_scatter(grad_partial, "tp", scatter_dimension=1, tiled=True)
-        grad_moe_in = lax.all_gather(grad_share, "tp", axis=1, tiled=True)
-        out_partial = dot_nn(active, down_matrix)
-        out_partial = lax.psum_scatter(
-            out_partial.astype(BF16), "ep", scatter_dimension=0, tiled=True
-        )
-        mixed = lax.psum_scatter(out_partial, "tp", scatter_dimension=1, tiled=True)
-        grad_w_down = dot_tn(active, all_grad)
-        grad_w_gate = dot_tn(grad_gate_pre, all_in)
-        grad_w_up = dot_tn(grad_up_pre, all_in)
+    row_scale = jnp.repeat(scale, hidden_here, axis=1)
+    gate_pre = dot_nt(all_in, gate_matrix)
+    up_pre = dot_nt(all_in, up_matrix)
+    grad_active = dot_nt(all_grad, down_matrix) * row_scale
+    sigmoid_gate = jax.nn.sigmoid(gate_pre)
+    silu_gate = gate_pre * sigmoid_gate
+    active = (silu_gate * up_pre * row_scale).astype(BF16)
+    grad_up_pre = (grad_active * silu_gate).astype(BF16)
+    grad_gate_pre = (
+        grad_active * up_pre * sigmoid_gate * (1.0 + gate_pre * (1.0 - sigmoid_gate))
+    ).astype(BF16)
+    grad_partial = dot_nn(grad_gate_pre, gate_matrix) + dot_nn(grad_up_pre, up_matrix)
+    grad_partial = lax.psum_scatter(
+        grad_partial.astype(BF16), "ep", scatter_dimension=0, tiled=True
+    )
+    grad_share = lax.psum_scatter(grad_partial, "tp", scatter_dimension=1, tiled=True)
+    out_partial = dot_nn(active, down_matrix)
+    out_partial = lax.psum_scatter(out_partial.astype(BF16), "ep", scatter_dimension=0, tiled=True)
+    mixed = lax.psum_scatter(out_partial, "tp", scatter_dimension=1, tiled=True)
     hidden_share = lax.dynamic_slice_in_dim(hidden, tp_index * share_width, share_width, 1)
     layer_dealt = (hidden_share + mixed.astype(F32)).astype(BF16)
+    grad_w_down = dot_tn(active, all_grad).reshape(w_down.shape)
+    grad_w_gate = dot_tn(grad_gate_pre, all_in).reshape(w_gate.shape)
+    grad_w_up = dot_tn(grad_up_pre, all_in).reshape(w_up.shape)
+
+    grad_float = grad_full.astype(F32)
+    grad_moe_in = lax.all_gather(grad_share, "tp", axis=1, tiled=True).astype(F32)
+    norm_moe_part = jnp.sum(grad_moe_in * unit_two, axis=0)
+    grad_hidden = grad_float + norm_back(grad_moe_in * gain_moe, unit_two, inverse_two)
+    grad_attn = grad_hidden.astype(BF16)
+    grad_w_out = dot_tn(grad_attn, context_low)
+    grad_context = (
+        dot_nn(grad_attn, full_out)
+        .astype(BF16)
+        .reshape(MICRO, micro_rows, kv_here, group_size, HEAD_DIM)
+    )
+    grad_probs = jnp.einsum("mqkgd,mtkd->mkgqt", grad_context, values, preferred_element_type=F32)
+    prob_delta = jnp.sum(attn_probs * grad_probs, axis=-1, keepdims=True)
+    grad_scores = (attn_probs * (grad_probs - prob_delta)).astype(BF16)
+    grad_queries = (
+        jnp.einsum("mkgqt,mtkd->mqkgd", grad_scores, key_rows, preferred_element_type=F32).reshape(
+            rows_dev, heads_here, HEAD_DIM
+        )
+        * score_scale
+    )
+    grad_keys = (
+        jnp.einsum("mkgqt,mqkgd->mtkd", grad_scores, queries, preferred_element_type=F32).reshape(
+            rows_dev, kv_here, HEAD_DIM
+        )
+        * score_scale
+    )
+    grad_values = jnp.einsum(
+        "mkgqt,mqkgd->mtkd", probs_low, grad_context, preferred_element_type=F32
+    )
+    grad_unit_query = rotate_back(grad_queries, cosine, sine_table)
+    grad_unit_key = rotate_back(grad_keys, cosine, sine_table)
+    query_gain_part = jnp.sum(grad_unit_query * unit_query, axis=(0, 1))
+    key_gain_part = jnp.sum(grad_unit_key * unit_key, axis=(0, 1))
+    grad_query_proj = (
+        norm_back(grad_unit_query * gain_query, unit_query, inverse_query)
+        .reshape(rows_dev, heads_here * HEAD_DIM)
+        .astype(BF16)
+    )
+    grad_key_proj = (
+        norm_back(grad_unit_key * gain_key, unit_key, inverse_key)
+        .reshape(rows_dev, kv_width)
+        .astype(BF16)
+    )
+    grad_value_proj = grad_values.reshape(rows_dev, kv_width).astype(BF16)
+    grad_kv_proj = jnp.concatenate([grad_key_proj, grad_value_proj], axis=1)
+    normed_part = dot_nt(grad_query_proj, full_query) + dot_nt(grad_kv_proj, full_kv)
+    grad_normed = lax.psum_scatter(
+        normed_part.astype(BF16), "tp", scatter_dimension=1, tiled=True
+    ).astype(F32)
+    grad_packed = jnp.concatenate(
+        [
+            dot_tn(normed, grad_query_proj).astype(BF16),
+            grad_w_out.astype(BF16),
+            dot_tn(normed, grad_kv_proj).astype(BF16),
+        ],
+        axis=1,
+    )
+    grad_packed = lax.psum_scatter(grad_packed, "ep", scatter_dimension=0, tiled=True).astype(F32)
+
+    start = tp_index * share_width
+    gain_share = lax.dynamic_slice_in_dim(gain_attn, start, share_width, 0)
+    unit_share = lax.dynamic_slice_in_dim(unit_one, start, share_width, 1)
+    hidden_grad_share = lax.dynamic_slice_in_dim(grad_hidden, start, share_width, 1)
+    scaled = grad_normed * gain_share
+    row_mean = lax.psum(jnp.sum(scaled * unit_share, axis=1), "tp") / model_width
+    grad_layer = hidden_grad_share + inverse_one * (scaled - unit_share * row_mean[:, None])
+    norm_attn_part = lax.dynamic_update_slice_in_dim(
+        jnp.zeros((model_width,), F32), jnp.sum(grad_normed * unit_share, axis=0), start, 0
+    )
+    small = jnp.concatenate(
+        [norm_attn_part, norm_moe_part / tp_count, query_gain_part, key_gain_part]
+    )
+    small = lax.psum(small, ("ep", "tp"))
+    grad_norm_attn = lax.dynamic_slice_in_dim(small, ep_index * part, part, 0)
+    grad_norm_moe = lax.dynamic_slice_in_dim(small, model_width + ep_index * part, part, 0)
+    grad_query_gain = lax.dynamic_slice_in_dim(
+        small, 2 * model_width + ep_index * head_part, head_part, 0
+    )
+    grad_key_gain = lax.dynamic_slice_in_dim(
+        small, 2 * model_width + HEAD_DIM + ep_index * head_part, head_part, 0
+    )
+
+    back = jnp.concatenate([layer_dealt, grad_layer.astype(BF16)], axis=1)
+    home = exchange(dot_tn(recv, back).astype(BF16), ep_count)
+    home = dot_tn(send, home)
+    return (
+        home[:, :share_width].astype(BF16),
+        home[:, share_width:],
+        grad_packed[:, :q_width],
+        grad_packed[:, 2 * q_width : 2 * q_width + kv_width],
+        grad_packed[:, 2 * q_width + kv_width :],
+        grad_packed[:, q_width : 2 * q_width],
+        grad_norm_attn,
+        grad_norm_moe,
+        grad_query_gain,
+        grad_key_gain,
+        grad_w_gate,
+        grad_w_up,
+        grad_w_down,
+    )
+
+
+def route_scales(routes, route_weights, experts, local_experts, hidden_here, ep_index):
+    expert_ids = jnp.arange(experts, dtype=jnp.int32)
+    dense = jnp.sum(
+        jnp.where(
+            routes.T[None, :, :] == expert_ids[:, None, None], route_weights.T[None, :, :], 0.0
+        ),
+        axis=1,
+    )
+    terms = []
+    for _ in range(SCALE_TERMS):
+        terms.append(lax.reduce_precision(dense, 8, 7))
+        dense = dense - terms[-1]
+    parts = jnp.concatenate(terms, axis=0).astype(BF16)
+    flat_expert = ep_index * local_experts + jnp.repeat(
+        jnp.arange(local_experts, dtype=jnp.int32), hidden_here
+    )
+    part_expert = jnp.arange(parts.shape[0], dtype=jnp.int32) % experts
+    return (parts, (part_expert[:, None] == flat_expert[None, :]).astype(BF16))
+
+
+def plane_layer(
+    layer_in,
+    token_order,
+    seq_lengths,
+    routes,
+    route_weights,
+    w_query,
+    w_key,
+    w_value,
+    w_out,
+    norm_attn,
+    norm_moe,
+    query_gain,
+    key_gain,
+    w_gate,
+    w_up,
+    w_down,
+    grad_out,
+):
+    ep_count = lax.axis_size("ep")
+    tp_count = lax.axis_size("tp")
+    tp_index = lax.axis_index("tp")
+    ep_index = lax.axis_index("ep")
+    local_experts, hidden_here, model_width = w_gate.shape
+    experts = local_experts * ep_count
+    rows_dev = layer_in.shape[0]
+    micro_rows = rows_dev // MICRO
+    share_width = layer_in.shape[1]
+    score_scale = HEAD_DIM ** (-0.5)
+
+    q_width, kv_width = w_query.shape[1], w_key.shape[1]
+    heads_here = q_width // HEAD_DIM
+    kv_here = kv_width // HEAD_DIM
+    group_size = heads_here // kv_here
+    send, recv = deal_matrices(token_order, ep_index, rows_dev, ep_count)
+    send_rows = permute_rows(send, jnp.concatenate([layer_in, grad_out], axis=1))
+    part = norm_attn.shape[0]
+    head_part = query_gain.shape[0]
+    scale_parts, pick = route_scales(
+        routes, route_weights, experts, local_experts, hidden_here, ep_index
+    )
+    gain_at = scale_parts.shape[0]
+    gains = jnp.zeros((1, 2 * part + 2 * HEAD_DIM), BF16)
+    for vector, at in (
+        (norm_attn, 0),
+        (norm_moe, part),
+        (query_gain, 2 * part + ep_index * head_part),
+        (key_gain, 2 * part + HEAD_DIM + ep_index * head_part),
+    ):
+        gains = lax.dynamic_update_slice(gains, vector[None], (0, at))
+    small_rows = -(-(gain_at + 1) // 32) * 32
+    small = jnp.pad(scale_parts, ((0, 0), (0, gains.shape[1] - scale_parts.shape[1])))
+    small = jnp.pad(
+        jnp.concatenate([small, gains], axis=0), ((0, small_rows - gain_at - 1), (0, 0))
+    )
+    segment, position = jax.vmap(positions_of, in_axes=(0, None))(seq_lengths, micro_rows)
+    cosine, sine_table = rope_tables(position.reshape(-1), HEAD_DIM // 2)
+    cosine_wide = jnp.concatenate([cosine[:, 0], cosine[:, 0]], axis=1)
+    sine_wide = jnp.concatenate([-sine_table[:, 0], sine_table[:, 0]], axis=1)
+    offsets = jnp.arange(micro_rows, dtype=jnp.int32)
+    allowed = (segment[:, :, None] == segment[:, None, :]) & (
+        offsets[None, None, :] <= offsets[None, :, None]
+    )
+    mask = allowed.astype(F32).reshape(rows_dev, micro_rows)
+    (
+        layer_full,
+        grad_full,
+        hidden,
+        moe_in,
+        proj,
+        turned,
+        key_flat,
+        value_flat,
+        probs,
+        context_low,
+        small_all,
+        normed,
+        all_grad,
+        w_in_all,
+        full_out,
+    ) = front_call(
+        gain_at,
+        ep_count,
+        tp_count,
+        send_rows,
+        recv,
+        small,
+        cosine_wide,
+        sine_wide,
+        mask,
+        w_query,
+        w_key,
+        w_value,
+        w_out,
+    )
+
+    flat = local_experts * hidden_here
+    gate_matrix = w_gate.reshape(flat, model_width)
+    up_matrix = w_up.reshape(flat, model_width)
+    down_matrix = w_down.reshape(flat, model_width)
+    grad_partial, active, grad_w_gate, grad_w_up, grad_w_down = expert_call(
+        moe_in, all_grad, small_all, pick, gate_matrix, up_matrix, down_matrix
+    )
+    grad_moe_in, mixed_plane = mix_call(grad_partial, active, down_matrix, tp_count)
+    mixed = lax.psum_scatter(mixed_plane, "tp", scatter_dimension=1, tiled=True)
+    hidden_share = lax.dynamic_slice_in_dim(hidden, tp_index * share_width, share_width, 1)
+    layer_dealt = (hidden_share + mixed.astype(F32)).astype(BF16)
+
+    gain_rows = small_all.reshape(ep_count, small_rows, -1)[:, gain_at].astype(F32)
+    gain_attn = gain_rows[:, :part].reshape(-1)
+    gain_moe = gain_rows[:, part : 2 * part].reshape(-1)
+    gain_query = jnp.sum(gain_rows[:, 2 * part : 2 * part + HEAD_DIM], axis=0)
+    gain_key = jnp.sum(gain_rows[:, 2 * part + HEAD_DIM :], axis=0)
+    full_query, full_kv = w_in_all[:, :q_width], w_in_all[:, q_width:]
+    layer_float = layer_full.astype(F32)
+    inverse_one = inverse_rms(layer_float)
+    unit_one = layer_float * inverse_one
+    inverse_two = inverse_rms(hidden)
+    unit_two = hidden * inverse_two
+    query_proj = proj[:, :q_width].reshape(rows_dev, heads_here, HEAD_DIM)
+    key_proj = proj[:, q_width : q_width + kv_width].reshape(rows_dev, kv_here, HEAD_DIM)
+    inverse_query = inverse_rms(query_proj)
+    unit_query = query_proj * inverse_query
+    inverse_key = inverse_rms(key_proj)
+    unit_key = key_proj * inverse_key
+    attn_probs = probs.reshape(MICRO, kv_here, group_size, micro_rows, micro_rows)
+    probs_low = attn_probs.astype(BF16)
+    queries = jnp.transpose(
+        turned.reshape(MICRO, kv_here, group_size, micro_rows, HEAD_DIM), (0, 3, 1, 2, 4)
+    )
+    key_rows = key_flat.reshape(MICRO, micro_rows, kv_here, HEAD_DIM)
+    values = value_flat.reshape(MICRO, micro_rows, kv_here, HEAD_DIM)
 
     grad_float = grad_full.astype(F32)
     grad_moe_in = grad_moe_in.astype(F32)
@@ -1024,3 +1603,47 @@
         ),
         check_vma=False,
     )
+
+
+def solution(mesh):
+    shape = dict(mesh.shape)
+    planes = shape["ep"] == 8 and shape["tp"] == 4
+    return jax.shard_map(
+        plane_layer if planes else plain_layer,
+        mesh=mesh,
+        in_specs=(
+            P("ep", "tp"),
+            P(),
+            P("ep", None),
+            P("ep", None),
+            P("ep", None),
+            P("ep", "tp"),
+            P("ep", "tp"),
+            P("ep", "tp"),
+            P("ep", "tp"),
+            P("ep"),
+            P("ep"),
+            P("ep"),
+            P("ep"),
+            P("ep", "tp", None),
+            P("ep", "tp", None),
+            P("ep", "tp", None),
+            P("ep", "tp"),
+        ),
+        out_specs=(
+            P("ep", "tp"),
+            P("ep", "tp"),
+            P("ep", "tp"),
+            P("ep", "tp"),
+            P("ep", "tp"),
+            P("ep", "tp"),
+            P("ep"),
+            P("ep"),
+            P("ep"),
+            P("ep"),
+            P("ep", "tp", None),
+            P("ep", "tp", None),
+            P("ep", "tp", None),
+        ),
+        check_vma=False,
+    )

time: 591 us -> 457 us (0.77)
  waiting for transfers between devices: 221 us -> 51 us
  Pallas kernels: 130 us -> 242 us
  blocking collectives: 84.6 us -> 50.8 us
  matrix products: 33.2 us -> 13.6 us
  local copies, waits for them, and re-layouts: 39 us -> 31.5 us
  other arithmetic: 49.3 us -> 42.4 us
    all_gather x4 -> x0, waiting for transfers between devices: 118 us -> none  [the longest x1 56.5 us: on_device(): packed = lax.all_gather(packed, 'ep', axis=0, tiled=True)]
    pallas_call x0 -> x1, Pallas kernels: none -> 113 us  [front_call(): pl.pallas_call(functools.partial(front_body, gain_at, ep_count, tp_count,...]
    psum x1 -> x0, waiting for transfers between devices: 41.1 us -> none  [on_device(): attn_out = lax.psum(attn_part.astype(BF16), 'tp').astype(F32)]
    unnamed x1 -> x0, blocking collectives: 23.5 us -> none
    all_gather x1 -> x0, blocking collectives: 10.4 us -> none  [on_device(): scale_all = lax.all_gather(scale_parts, 'ep', axis=0, tiled=True)]
    dot_general x5 -> x2, matrix products: 11.9 us -> 3.4 us  [dot_nn(): return jnp.dot(left, right, preferred_element_type=F32)]
    dot_general x3 -> x2, matrix products: 11.3 us -> 2.91 us  [dot_nt(): lax.dot_general(left_rows, right_matrix, (((1,), (1,)), ((), ())), prefer...]
    all_to_all x2 -> x1, waiting for transfers between devices: 7.94 us -> 0.01 us  [exchange(): moved = lax.all_to_all(split, 'ep', split_axis=0, concat_axis=0, tiled=True)]
  transfers between devices with their start and end apart: 10 -> 4, of which waited for: 8 -> 3; matrix products, arithmetic and copies ran while one was open for 11% -> 7% of each run, Pallas kernels for 0% -> 0%
where the time goes in v3:
time: 457 us; the launch traced here: 449 us
  Pallas kernels  242 us (53%)
  waiting for transfers between devices  51 us (11%)
  blocking collectives  50.8 us (11%)
  other arithmetic  42.4 us (9%)
  local copies, waits for them, and re-layouts  31.5 us (7%)
  between operations  14.5 us (3%)
  matrix products  13.6 us (3%)
    pallas_call x1, Pallas kernels, front_call(): pl.pallas_call(functools.partial(front_body, gain_at, ep_count, tp_count,...  113 us
    pallas_call x1, Pallas kernels, expert_call(): pl.pallas_call(functools.partial(expert_body, flat, rows, parts), out_sha...  79.4 us
    pallas_call x1, Pallas kernels, mix_call(): pl.pallas_call(functools.partial(mix_body, tp_count, rows), out_shape=(wh...  49.9 us
    psum x1, blocking collectives, plane_layer(): small = lax.psum(small, ('ep', 'tp'))  41.4 us
    reduce_scatter x1, waiting for transfers between devices, plane_layer(): lax.psum_scatter(grad_packed, 'ep', scatter_dimension=0, tiled=True)  27.1 us
    unnamed x60, local copies, waits for them, and re-layouts  20.1 us
    reduce_scatter x1, waiting for transfers between devices, plane_layer(): mixed = lax.psum_scatter(mixed_plane, 'tp', scatter_dimension=1, tiled=True)  17.3 us
    concatenate x1, other arithmetic, plane_layer(): jnp.concatenate([dot_tn(normed, grad_query_proj).astype(BF16), grad_w_out...  15.7 us
  transfers between devices with their start and end apart: 4, of which 3 were waited for; matrix products, arithmetic and copies ran while one was open for 7% of the time, Pallas kernels for 0%

profile of v3, /device:TPU:0, one launch (start us, length us, event | category | flops | bytes accessed | tf_op | source)
XLA Modules:
  0.0 449.3 jit_solution(17121357256867427667)
XLA Ops:
  7.2 0.9 reduce_window_sum.11
  8.9 1.1 select_reduce_fusion
  10.0 0.8 and_select_fusion.1
  11.2 0.8 fusion.36.recv_ref
  15.1 0.8 dynamic_update_slice.18
  17.9 2.1 convolution_convert_fusion.4.send_ref
  20.0 0.8 pad_maximum_fusion.2
  20.8 112.5 %front.1 = (bf16[256,2048]{1,0:T(8,128)(2,1)}, bf16[256,2048]{1,0:T(8,128)(2,1)}, f32[256,2048]{1,0:T(8,128)}, bf16[256,2048]{1,0:T(8,128)(2,1)}, f32[256,1280]{...) custom-call(bf16[256,1024]{1,0:T(8,128)(2,1)} %convolution_convert_f, ...), custom_call_target="tpu_custom_call" | custom-call | tf_op jit(solution)/shard_map/front/pallas_call | solution.py:1027
  133.4 1.1 slice_convert_fusion.1
  134.5 1.0 multiply_reduce_fusion.7
  135.5 2.3 slice_bitcast_fusion
  138.8 79.4 %experts.1 = (bf16[256,2048]{1,0:T(8,128)(2,1)}, bf16[2048,384]{1,0:T(8,128)(2,1)}, f32[384,2048]{1,0:T(8,128)}, f32[384,2048]{1,0:T(8,128)}, f32[384,2048]{1,0:T(8,128)}) custom-call(bf16[256,2048]{1,0:T(8,128)(2,1)} %get-tuple-element.36.own_hbm, bf16[2048,2048]{1,0:T(8,128)(2,1)} %get-tuple-element.37.grad_hbm, ...), custom_call_target="tpu_custom_call" | custom-call | tf_op jit(solution)/shard_map/experts/pallas_call | solution.py:521
  218.2 49.9 %mix.1 = (bf16[256,2048]{1,0:T(8,128)(2,1)}, bf16[256,2048]{1,0:T(8,128)(2,1)}) custom-call(bf16[256,2048]{1,0:T(8,128)(2,1)} %get-tuple-element.39.partial_ref, bf16[2048,384]{1,0:T(8,128)(2,1)} %get-tuple-element.40.active_ref, bf16[384,2048]{1,0:T(8,128)(2,1)} %bitcast.141), custom_call_target="tpu_custom_call" | custom-call | tf_op jit(solution)/shard_map/mix/pallas_call | solution.py:765
  268.2 2.8 fusion.8
  271.1 2.0 fusion.7
  273.6 1.3 fusion.10
  274.8 0.9 copy.72
  275.7 0.8 convert_element_type.141
  276.6 1.6 copy.55
  278.2 1.4 multiply_reduce_fusion.3
  284.2 0.9 multiply_reduce_fusion.2
  286.6 0.9 fusion.16
  287.5 1.3 fusion
  288.8 1.6 fusion.2
  292.4 1.3 convolution_convert_fusion.1
  294.1 1.3 convolution_convert_fusion
  295.4 15.7 %pad_maximum_fusion = bf16[2048,2304]{0,1:T(8,128)(2,1)} fusion(bf16[2048,256]{0,1:T(8,128)(2,1)S(1)} %convolution_convert_fusion.2, bf16[2048,1024]{0,1:T(8,128)(2,1)S(1)} %convolution_convert_fusion, bf16[2048,1024]{0,1:T(8,128)(2,1)S(1)} %convolution_convert_fusion.1), kind=kLoop, calls=%fused_computation | loop fusion | flops 28311552 | bytes 18874368 | tf_op jit(solution)/shard_map/concatenate | solution.py:1513
  311.1 1.2 copy-done.7
  312.3 1.6 convert_element_type.135
  314.2 5.8 %reduce-scatter.6.cloned.1.call-done = bf16[256,512]{1,0:T(8,128)(2,1)} async-done(((bf16[256,2048]{1,0:T(8,128)(2,1)}), bf16[256,512]{1,0:T(8,128)(2,1)}) %reduce-scatter.6.cloned.1.call-update) | async-done | bytes 262160 | tf_op jit(solution)/shard_map/reduce_scatter | solution.py:1510
  320.0 1.4 fusion.24
  321.4 9.4 %psum.14 = f32[256]{0:T(256)S(1)} all-reduce(f32[256]{0:T(256)S(1)} %get-tuple-element.99), channel_id=1, replica_groups=mesh['ep'=8,'tp'=4] {'tp'}, use_global_device_ids=true, to_apply=%region_20.21 | all-reduce | flops 256 | bytes 2048 | tf_op jit(solution)/shard_map/psum | solution.py:1528
  330.8 17.3 %reduce-scatter.4.cloned.1.call-done = bf16[256,512]{1,0:T(8,128)(2,1)} async-done(((bf16[256,2048]{1,0:T(8,128)(2,1)}), bf16[256,512]{1,0:T(8,128)(2,1)}) %reduce-scatter.4.cloned.1.call-update) | async-done | bytes 262160 | tf_op jit(solution)/shard_map/reduce_scatter | solution.py:1435
  348.1 1.0 add_convert_fusion
  349.2 1.5 fusion.23
  350.6 1.2 convolution_convert_fusion.3
  351.8 3.7 all-to-all-start
  355.8 41.4 %psum.15 = f32[4352]{0:T(1024)S(1)} all-reduce(f32[4352]{0:T(1024)S(1)} %pad_maximum_fusion.8), channel_id=1, replica_groups=mesh['ep'=8,'tp'=4] {'ep','tp'}, use_global_device_ids=true, to_apply=%region_27.28 | all-reduce | flops 4352 | bytes 34816 | tf_op jit(solution)/shard_map/psum | solution.py:1536
  398.8 0.8 slice.87
  400.4 27.1 %reduce-scatter.8.cloned.1.call-done = bf16[256,2304]{0,1:T(8,128)(2,1)} async-done(((bf16[2048,2304]{0,1:T(8,128)(2,1)}), bf16[256,2304]{0,1:T(8,128)(2,1)}) %reduce-scatter.8.cloned.1.call-update) | async-done | bytes 1179664 | tf_op jit(solution)/shard_map/reduce_scatter | solution.py:1521
  427.5 1.4 fusion.71
  428.8 1.3 copy.59
  430.2 1.3 copy.62
  431.5 0.9 fusion.72
  433.9 4.1 copy.96
  437.9 1.7 copy.97
  439.6 1.4 copy-done.11
  441.0 1.7 copy.98
  (121 shorter events, 20.6 us)
Async XLA Ops:
  7.2 312.9 %reduce-scatter.6.cloned.1.call-start = ((), (), s32[]{:S(2)}) async-start(), calls=%async_computation.5 | async-start | bytes 1310720 | tf_op jit(solution)/shard_map/reduce_scatter | solution.py:1510
  133.4 4.5 %copy-start = (f32[256,2048]{1,0:T(8,128)S(1)}, f32[256,2048]{1,0:T(8,128)}, u32[]{:S(2)}) copy-start(f32[256,2048]{1,0:T(8,128)} %get-tuple-element.35) | copy-start | bytes 6291460
  268.2 2.9 copy-start.1
  268.2 2.9 copy-start.10
  271.1 2.5 copy-start.20
  273.1 1.7 copy-start.2
  273.6 2.2 copy-start.9
  275.7 2.4 copy-start.19
  278.2 1.6 copy-start.16
  279.6 1.3 copy-start.5
  279.6 1.7 copy-start.18
  282.3 1.2 copy-start.8
  282.3 5.2 %slice-start = ((s8[5242880]{0:T(1024)(128)(4,1)}), s8[4194304]{0:T(1024)(128)(4,1)S(1)}, s32[]{:S(2)}) async-start(s8[5242880]{0:T(1024)(128)(4,1)} %bitcast.160), calls=%async_computation.7 | async-start | bytes 8388608
  284.1 1.0 copy-start.6
  284.1 1.2 copy-start.15
  284.2 3.3 slice-start.1
  287.5 1.3 copy-start.13
  290.4 1.2 copy-start.4
  290.5 57.7 %reduce-scatter.4.cloned.1.call-start = ((), (), s32[]{:S(2)}) async-start(), calls=%async_computation.4 | async-start | bytes 1310720 | tf_op jit(solution)/shard_map/reduce_scatter | solution.py:1435
  291.2 136.3 %reduce-scatter.8.cloned.1.call-start = ((), (), s32[]{:S(2)}) async-start(), calls=%async_computation.6 | async-start | bytes 10616832 | tf_op jit(solution)/shard_map/reduce_scatter | solution.py:1521
  291.3 1.1 copy-start.14
  292.4 1.6 copy-start.3
  292.4 1.7 copy-start.17
  311.1 1.2 copy-start.7
  351.8 46.6 %all-to-all-start = ((bf16[8,32,1024]{2,1,0:T(8,128)(2,1)}), bf16[8,32,1024]{2,1,0:T(8,128)(2,1)S(1)}, u32[]{:S(2)}, u32[]{:S(2)}) async-start(bf16[8,32,1024]{2,1,0:T(8,128)(2,1)} %bitcast.45), calls=%async_computation.2 | async-start | bytes 1048576 | tf_op jit(solution)/shard_map/all_to_all | solution.py:110
  433.9 4.1 copy-start.12
  437.9 3.0 copy-start.11
Sparse Core Ops, SparseCore 0:
  290.6 29.4 reduce-scatter.5
  322.3 25.7 reduce-scatter.3
  351.6 75.7 reduce-scatter.7

commit v4 on v3

--- a/solution.py
+++ b/solution.py
@@ -1066,6 +1066,401 @@
     )(send_rows, recv, small, cosine, sine_table, mask, query, key, value, out)
 
 
+def fold(values):
+    rows, width = values.shape
+    return jnp.sum(values.reshape(rows // 8, 8, width), axis=0)
+
+
+class Straight:
+    def __init__(self, axis, count, source, landed, send, recv):
+        self.axis, self.count, self.source, self.landed = axis, count, source, landed
+        self.send, self.recv = send, recv
+        self.me = lax.axis_index(axis)
+
+    def copy(self, j):
+        target = (self.me + j) % self.count
+        return send_to(
+            self.source(target),
+            self.landed(j),
+            self.send.at[j - 1],
+            self.recv.at[j - 1],
+            **{self.axis: target},
+        )
+
+    def begin(self):
+        for j in range(1, self.count):
+            self.copy(j).start()
+
+    def wait(self):
+        for j in range(1, self.count):
+            self.copy(j).wait_recv()
+
+    def sent(self):
+        for j in range(1, self.count):
+            self.copy(j).wait_send()
+
+
+def back_body(
+    gain_at,
+    ep_count,
+    tp_count,
+    rows,
+    heads,
+    grad_moe_ref,
+    mixed_ref,
+    x_ref,
+    hidden_ref,
+    grad_ref,
+    normed_ref,
+    proj_ref,
+    turned_ref,
+    keys_ref,
+    values_ref,
+    probs_ref,
+    context_ref,
+    small_all,
+    cosine_ref,
+    sine_ref,
+    send_ref,
+    recv_ref,
+    w_in_hbm,
+    w_out_hbm,
+    layer_out,
+    layer_grad,
+    d_query,
+    d_key,
+    d_value,
+    d_out,
+    sums_out,
+    w_in,
+    w_out,
+    grad_hidden,
+    grad_attn,
+    stacked_grad,
+    grad_turned,
+    grad_proj,
+    normed_part,
+    mixed_line,
+    normed_line,
+    row_sums,
+    row_line,
+    sums,
+    sums_near,
+    sums_line,
+    home_send,
+    home_recv,
+    out_part,
+    in_part,
+    *rest,
+):
+    out_bufs, out_sems = rest[0:4], rest[4:8]
+    in_bufs, in_sems = rest[8:12], rest[12:16]
+    mixed_sems, normed_sems, row_sems, sum_sems, sum_line_sems, home_sems = (
+        rest[16:18],
+        rest[18:20],
+        rest[20:22],
+        rest[22:24],
+        rest[24:26],
+        rest[26:28],
+    )
+    local_sem = rest[28]
+    r = roles()
+    e = r["e"]
+    z = lax.axis_index("tp")
+    half = rows // HALF
+    width = x_ref.shape[1]
+    share = width // tp_count
+    q_width = heads * HEAD_DIM
+    micro_rows = rows // MICRO
+    per_pair = rows // ep_count
+    small_rows = small_all.shape[0] // ep_count
+    loads = [
+        pltpu.make_async_copy(w_out_hbm, w_out, local_sem.at[0]),
+        pltpu.make_async_copy(w_in_hbm, w_in, local_sem.at[1]),
+    ]
+    for load in loads:
+        load.start()
+    greet([(e + j) % ep_count for j in range(1, ep_count)], line_peers(tp_count))
+    mixed_sum = LineSum(tp_count, mixed_ref, mixed_line, *mixed_sems)
+    mixed_sum.begin()
+    out_sum = PlaneSum(r, out_part, *out_bufs, half, out_sems)
+    in_sum = PlaneSum(r, in_part, *in_bufs, half, in_sems)
+
+    def gain_row(place, column, wide):
+        at = place * small_rows + gain_at
+        return small_all[at : at + 1, column : column + wide].astype(F32)
+
+    hidden = hidden_ref[...]
+    inverse_two = lax.rsqrt(jnp.mean(hidden * hidden, axis=-1, keepdims=True) + epsilon)
+    unit_two = hidden * inverse_two
+    grad_moe = grad_moe_ref[...].astype(F32)
+    moe_sums = fold(grad_moe * unit_two)
+    gain_moe = jnp.concatenate([gain_row(place, rows, rows) for place in range(ep_count)], axis=1)
+    scaled = grad_moe * gain_moe
+    grad_hidden[...] = grad_ref[...].astype(F32) + inverse_two * (
+        scaled - unit_two * jnp.mean(scaled * unit_two, axis=-1, keepdims=True)
+    )
+    grad_attn[...] = grad_hidden[...].astype(BF16)
+    sums[...] = jnp.zeros_like(sums)
+    for place in range(ep_count):
+        sums[place * 8 : place * 8 + 8, rows : 2 * rows] = moe_sums[
+            :, place * rows : (place + 1) * rows
+        ]
+
+    near_of = {"pd": (6, 7), "pb": (2, 3), "pa": (4, 5), "p": (0, 1)}
+    slots_of = {
+        "pd": SLOT_PD,
+        "d": SLOT_D,
+        "pb": SLOT_PB,
+        "b": SLOT_B,
+        "pa": SLOT_PA,
+        "a": SLOT_A,
+        "p": SLOT_P,
+        "e": SLOT_E,
+    }
+
+    def weight_blocks(plane, left, right):
+        for name, slots in slots_of.items():
+            lanes = pl.ds(pl.multiple_of(r[name] * rows, rows), rows)
+            block = dot_tn(left[:, lanes], right[...]).astype(BF16)
+            for k in range(HALF):
+                plane.slot(slots[k])[...] = block[k * half : (k + 1) * half]
+                if name in near_of:
+                    plane.near_copy(near_of[name][k]).start()
+
+    weight_blocks(out_sum, grad_attn, context_ref)
+    loads[0].wait()
+    grad_context = dot_nn(grad_attn[...], w_out[...]).astype(BF16)
+    for micro in range(MICRO):
+        for head in range(heads):
+            at = (micro * heads + head) * micro_rows
+            stacked_grad[at : at + micro_rows, :] = grad_context[
+                micro * micro_rows : (micro + 1) * micro_rows,
+                head * HEAD_DIM : (head + 1) * HEAD_DIM,
+            ]
+    for k in range(HALF):
+        out_sum.pass_far(k)
+    for k in range(HALF):
+        out_sum.pass_second(k)
+
+    cosine, sine_table = cosine_ref[...], -sine_ref[...]
+    column = 2 * rows
+    gain_query = sum(gain_row(place, column, HEAD_DIM) for place in range(ep_count))
+    gain_key = sum(gain_row(place, column + HEAD_DIM, HEAD_DIM) for place in range(ep_count))
+    scale = HEAD_DIM ** (-0.5)
+    grad_keys = []
+    for micro in range(MICRO):
+        within = slice(micro * micro_rows, (micro + 1) * micro_rows)
+        stacked = slice(micro * heads * micro_rows, (micro + 1) * heads * micro_rows)
+        probs = probs_ref[stacked, :]
+        grad_probs = dot_nt(stacked_grad[stacked, :], values_ref[within, :])
+        delta = jnp.sum(probs * grad_probs, axis=-1, keepdims=True)
+        grad_scores = (probs * (grad_probs - delta)).astype(BF16)
+        grad_turned[stacked, :] = dot_nn(grad_scores, keys_ref[within, :]) * scale
+        grad_keys.append(dot_tn(grad_scores, turned_ref[stacked, :]) * scale)
+        grad_proj[within, q_width + HEAD_DIM :] = dot_tn(
+            probs.astype(BF16), stacked_grad[stacked, :]
+        ).astype(BF16)
+
+    def unturn(grad, values, gain):
+        unturned = turn(grad, cosine, sine_table)
+        inverse = lax.rsqrt(jnp.mean(values * values, axis=-1, keepdims=True) + epsilon)
+        unit = values * inverse
+        scaled = unturned * gain
+        result = inverse * (scaled - unit * jnp.mean(scaled * unit, axis=-1, keepdims=True))
+        return fold(unturned * unit), result.astype(BF16)
+
+    key_sums, grad_key = unturn(
+        jnp.concatenate(grad_keys, axis=0), proj_ref[:, q_width : q_width + HEAD_DIM], gain_key
+    )
+    grad_proj[:, q_width : q_width + HEAD_DIM] = grad_key
+    for k in range(HALF):
+        out_sum.pass_first(k)
+
+    def one_head(head, total):
+        lanes = pl.ds(pl.multiple_of(head * HEAD_DIM, HEAD_DIM), HEAD_DIM)
+        grads = [
+            grad_turned[
+                pl.ds(pl.multiple_of((micro * heads + head) * micro_rows, micro_rows), micro_rows),
+                :,
+            ]
+            for micro in range(MICRO)
+        ]
+        part, grad = unturn(jnp.concatenate(grads, axis=0), proj_ref[:, lanes], gain_query)
+        grad_proj[:, lanes] = grad
+        return total + part
+
+    query_sums = lax.fori_loop(0, heads, one_head, jnp.zeros((8, HEAD_DIM), F32))
+    for place in range(ep_count):
+        at = slice(place * 8, place * 8 + 8)
+        sums[at, column : column + HEAD_DIM] = query_sums
+        sums[at, column + HEAD_DIM :] = key_sums
+
+    x_rows = x_ref[...].astype(F32)
+    inverse_one = lax.rsqrt(jnp.mean(x_rows * x_rows, axis=-1, keepdims=True) + epsilon)
+    gain_attn = jnp.concatenate([gain_row(place, 0, rows) for place in range(ep_count)], axis=1)
+    loads[1].wait()
+    partial = dot_nt(grad_proj[...], w_in[...])
+    normed_part[...] = partial.astype(BF16)
+    normed_sum = LineSum(tp_count, normed_part, normed_line, *normed_sems)
+    normed_sum.begin()
+    weight_blocks(in_sum, normed_ref, grad_proj)
+    along = jnp.sum(partial * gain_attn * (x_rows * inverse_one), axis=-1, keepdims=True)
+    row_sums[...] = jnp.transpose(jnp.broadcast_to(along, (rows, HEAD_DIM)))[:8]
+    over_rows = Straight("tp", tp_count, lambda _: row_sums, lambda j: row_line.at[j - 1], *row_sems)
+    over_rows.begin()
+    for k in range(HALF):
+        in_sum.pass_far(k)
+    for k in range(HALF):
+        in_sum.pass_second(k)
+    for k in range(HALF):
+        d_out[pl.ds(k * half, half), :] = out_sum.total(k)
+    for k in range(HALF):
+        in_sum.pass_first(k)
+
+    lanes = pl.ds(pl.multiple_of(z * share, share), share)
+    layer_rows = (hidden_ref[:, lanes] + mixed_sum.total()).astype(BF16)
+    over_rows.wait()
+    all_rows = row_sums[...]
+    for j in range(1, tp_count):
+        all_rows = all_rows + row_line[j - 1]
+    mean = jnp.transpose(jnp.broadcast_to(all_rows[:1], (HEAD_DIM, rows)))[:, :1] / width
+    grad_normed = normed_sum.total()
+    unit_share = x_ref[:, lanes].astype(F32) * inverse_one
+    places = share // rows
+    gain_share = []
+    for place in range(places):
+        at = pl.multiple_of((z * places + place) * small_rows + gain_at, 16)
+        gain_share.append(small_all[pl.ds(at, 16), :rows][:1].astype(F32))
+    scaled = grad_normed * jnp.concatenate(gain_share, axis=1)
+    grad_rows = grad_hidden[:, lanes] + inverse_one * (scaled - unit_share * mean)
+    both = jnp.concatenate([layer_rows, grad_rows.astype(BF16)], axis=1)
+    home_send[...] = dot_tn(recv_ref[...], both).astype(BF16)
+    home = Straight(
+        "ep",
+        ep_count,
+        lambda target: home_send.at[pl.ds(pl.multiple_of(target * per_pair, per_pair), per_pair)],
+        lambda j: home_recv.at[pl.ds(pl.multiple_of(e * per_pair, per_pair), per_pair)],
+        *home_sems,
+    )
+    home.begin()
+    norm_sums = fold(grad_normed * unit_share)
+    for place in range(places):
+        at = pl.multiple_of((z * places + place) * 8, 8)
+        sums[pl.ds(at, 8), :rows] = norm_sums[:, place * rows : (place + 1) * rows]
+    over_plane = Straight(
+        "ep",
+        ep_count,
+        lambda target: sums.at[pl.ds(pl.multiple_of(target * 8, 8), 8)],
+        lambda j: sums_near.at[j - 1],
+        *sum_sems,
+    )
+    over_plane.begin()
+    mine = pl.ds(pl.multiple_of(e * per_pair, per_pair), per_pair)
+    home_recv[mine, :] = home_send[mine, :]
+    over_plane.wait()
+    plane_sums = sums[pl.ds(pl.multiple_of(e * 8, 8), 8), :]
+    for j in range(1, ep_count):
+        plane_sums = plane_sums + sums_near[j - 1]
+    sums_line[0] = plane_sums
+    over_line = Straight(
+        "tp", tp_count, lambda _: sums_line.at[0], lambda j: sums_line.at[j], *sum_line_sems
+    )
+    over_line.begin()
+    for j in range(1, ep_count):
+        source = (e + ep_count - j) % ep_count
+        block = home_recv.at[pl.ds(pl.multiple_of(source * per_pair, per_pair), per_pair)]
+        send_to(block, block, home_sems[0].at[j - 1], home_sems[1].at[j - 1], ep=source).wait_recv()
+    arrived = dot_tn(send_ref[...], home_recv[...])
+    layer_out[...] = arrived[:, :share].astype(BF16)
+    layer_grad[...] = arrived[:, share:]
+    over_line.wait()
+    line_sums = plane_sums
+    for j in range(1, tp_count):
+        line_sums = line_sums + sums_line[j]
+    sums_out[:, :rows] = line_sums[:, :rows]
+    sums_out[:, rows : 2 * rows] = plane_sums[:, rows : 2 * rows]
+    sums_out[:, 2 * rows :] = line_sums[:, 2 * rows :]
+    for k in range(HALF):
+        total = in_sum.total(k)
+        at = pl.ds(k * half, half)
+        d_query[at, :] = total[:, :q_width]
+        d_key[at, :] = total[:, q_width : q_width + HEAD_DIM]
+        d_value[at, :] = total[:, q_width + HEAD_DIM :]
+    for op in (
+        mixed_sum,
+        normed_sum,
+        over_rows,
+        home,
+        over_plane,
+        over_line,
+        out_sum,
+        in_sum,
+    ):
+        op.sent()
+
+
+def back_call(gain_at, ep_count, tp_count, operands, w_in_all, w_out_all):
+    grad_moe, x = operands[0], operands[2]
+    rows, width = x.shape
+    share = width // tp_count
+    in_width = w_in_all.shape[1]
+    q_width = w_out_all.shape[1]
+    heads = q_width // HEAD_DIM
+    half = rows // HALF
+    everything = rows * ep_count
+    sums_width = 2 * rows + 2 * HEAD_DIM
+    shape = jax.ShapeDtypeStruct
+
+    def pair(count):
+        return [pltpu.SemaphoreType.DMA((count,))] * 2
+
+    return pl.pallas_call(
+        functools.partial(back_body, gain_at, ep_count, tp_count, rows, heads),
+        out_shape=(
+            shape((rows, share), BF16),
+            shape((rows, share), F32),
+            shape((rows, q_width), F32),
+            shape((rows, HEAD_DIM), F32),
+            shape((rows, HEAD_DIM), F32),
+            shape((rows, q_width), F32),
+            shape((8, sums_width), F32),
+        ),
+        in_specs=[vmem_spec()] * len(operands) + [any_spec()] * 2,
+        out_specs=tuple([vmem_spec()] * 7),
+        scratch_shapes=[
+            pltpu.VMEM((everything, in_width), BF16),
+            pltpu.VMEM((everything, q_width), BF16),
+            pltpu.VMEM((rows, width), F32),
+            pltpu.VMEM((rows, width), BF16),
+            pltpu.VMEM((heads * rows, HEAD_DIM), BF16),
+            pltpu.VMEM((heads * rows, HEAD_DIM), F32),
+            pltpu.VMEM((rows, in_width), BF16),
+            pltpu.VMEM((rows, width), BF16),
+            pltpu.VMEM((tp_count - 1, rows, share), BF16),
+            pltpu.VMEM((tp_count - 1, rows, share), BF16),
+            pltpu.VMEM((8, rows), F32),
+            pltpu.VMEM((tp_count - 1, 8, rows), F32),
+            pltpu.VMEM((8 * ep_count, sums_width), F32),
+            pltpu.VMEM((ep_count - 1, 8, sums_width), F32),
+            pltpu.VMEM((tp_count, 8, sums_width), F32),
+            pltpu.VMEM((rows, 2 * share), BF16),
+            pltpu.VMEM((rows, 2 * share), BF16),
+            pltpu.VMEM((everything, q_width), BF16),
+            pltpu.VMEM((everything, in_width), BF16),
+        ]
+        + plane_sum_scratch(half, q_width)
+        + plane_sum_scratch(half, in_width)
+        + pair(tp_count - 1) * 3
+        + pair(ep_count - 1)
+        + pair(tp_count - 1)
+        + pair(ep_count - 1)
+        + [pltpu.SemaphoreType.DMA((2,))],
+        compiler_params=comm_params(4),
+        name="back",
+    )(*operands, w_in_all, w_out_all)
+
+
 def plain_layer(
     layer_in,
     token_order,
@@ -1432,131 +1827,45 @@
         moe_in, all_grad, small_all, pick, gate_matrix, up_matrix, down_matrix
     )
     grad_moe_in, mixed_plane = mix_call(grad_partial, active, down_matrix, tp_count)
-    mixed = lax.psum_scatter(mixed_plane, "tp", scatter_dimension=1, tiled=True)
-    hidden_share = lax.dynamic_slice_in_dim(hidden, tp_index * share_width, share_width, 1)
-    layer_dealt = (hidden_share + mixed.astype(F32)).astype(BF16)
-
-    gain_rows = small_all.reshape(ep_count, small_rows, -1)[:, gain_at].astype(F32)
-    gain_attn = gain_rows[:, :part].reshape(-1)
-    gain_moe = gain_rows[:, part : 2 * part].reshape(-1)
-    gain_query = jnp.sum(gain_rows[:, 2 * part : 2 * part + HEAD_DIM], axis=0)
-    gain_key = jnp.sum(gain_rows[:, 2 * part + HEAD_DIM :], axis=0)
-    full_query, full_kv = w_in_all[:, :q_width], w_in_all[:, q_width:]
-    layer_float = layer_full.astype(F32)
-    inverse_one = inverse_rms(layer_float)
-    unit_one = layer_float * inverse_one
-    inverse_two = inverse_rms(hidden)
-    unit_two = hidden * inverse_two
-    query_proj = proj[:, :q_width].reshape(rows_dev, heads_here, HEAD_DIM)
-    key_proj = proj[:, q_width : q_width + kv_width].reshape(rows_dev, kv_here, HEAD_DIM)
-    inverse_query = inverse_rms(query_proj)
-    unit_query = query_proj * inverse_query
-    inverse_key = inverse_rms(key_proj)
-    unit_key = key_proj * inverse_key
-    attn_probs = probs.reshape(MICRO, kv_here, group_size, micro_rows, micro_rows)
-    probs_low = attn_probs.astype(BF16)
-    queries = jnp.transpose(
-        turned.reshape(MICRO, kv_here, group_size, micro_rows, HEAD_DIM), (0, 3, 1, 2, 4)
-    )
-    key_rows = key_flat.reshape(MICRO, micro_rows, kv_here, HEAD_DIM)
-    values = value_flat.reshape(MICRO, micro_rows, kv_here, HEAD_DIM)
-
-    grad_float = grad_full.astype(F32)
-    grad_moe_in = grad_moe_in.astype(F32)
-    norm_moe_part = jnp.sum(grad_moe_in * unit_two, axis=0)
-    grad_hidden = grad_float + norm_back(grad_moe_in * gain_moe, unit_two, inverse_two)
-    grad_attn = grad_hidden.astype(BF16)
-    grad_w_out = dot_tn(grad_attn, context_low)
-    grad_context = (
-        dot_nn(grad_attn, full_out)
-        .astype(BF16)
-        .reshape(MICRO, micro_rows, kv_here, group_size, HEAD_DIM)
-    )
-    grad_probs = jnp.einsum("mqkgd,mtkd->mkgqt", grad_context, values, preferred_element_type=F32)
-    prob_delta = jnp.sum(attn_probs * grad_probs, axis=-1, keepdims=True)
-    grad_scores = (attn_probs * (grad_probs - prob_delta)).astype(BF16)
-    grad_queries = (
-        jnp.einsum("mkgqt,mtkd->mqkgd", grad_scores, key_rows, preferred_element_type=F32).reshape(
-            rows_dev, heads_here, HEAD_DIM
-        )
-        * score_scale
-    )
-    grad_keys = (
-        jnp.einsum("mkgqt,mqkgd->mtkd", grad_scores, queries, preferred_element_type=F32).reshape(
-            rows_dev, kv_here, HEAD_DIM
-        )
-        * score_scale
-    )
-    grad_values = jnp.einsum(
-        "mkgqt,mqkgd->mtkd", probs_low, grad_context, preferred_element_type=F32
-    )
-    grad_unit_query = rotate_back(grad_queries, cosine, sine_table)
-    grad_unit_key = rotate_back(grad_keys, cosine, sine_table)
-    query_gain_part = jnp.sum(grad_unit_query * unit_query, axis=(0, 1))
-    key_gain_part = jnp.sum(grad_unit_key * unit_key, axis=(0, 1))
-    grad_query_proj = (
-        norm_back(grad_unit_query * gain_query, unit_query, inverse_query)
-        .reshape(rows_dev, heads_here * HEAD_DIM)
-        .astype(BF16)
-    )
-    grad_key_proj = (
-        norm_back(grad_unit_key * gain_key, unit_key, inverse_key)
-        .reshape(rows_dev, kv_width)
-        .astype(BF16)
-    )
-    grad_value_proj = grad_values.reshape(rows_dev, kv_width).astype(BF16)
-    grad_kv_proj = jnp.concatenate([grad_key_proj, grad_value_proj], axis=1)
-    normed_part = dot_nt(grad_query_proj, full_query) + dot_nt(grad_kv_proj, full_kv)
-    grad_normed = lax.psum_scatter(
-        normed_part.astype(BF16), "tp", scatter_dimension=1, tiled=True
-    ).astype(F32)
-    grad_packed = jnp.concatenate(
-        [
-            dot_tn(normed, grad_query_proj).astype(BF16),
-            grad_w_out.astype(BF16),
-            dot_tn(normed, grad_kv_proj).astype(BF16),
-        ],
-        axis=1,
-    )
-    grad_packed = lax.psum_scatter(grad_packed, "ep", scatter_dimension=0, tiled=True).astype(F32)
-
-    start = tp_index * share_width
-    gain_share = lax.dynamic_slice_in_dim(gain_attn, start, share_width, 0)
-    unit_share = lax.dynamic_slice_in_dim(unit_one, start, share_width, 1)
-    hidden_grad_share = lax.dynamic_slice_in_dim(grad_hidden, start, share_width, 1)
-    scaled = grad_normed * gain_share
-    row_mean = lax.psum(jnp.sum(scaled * unit_share, axis=1), "tp") / model_width
-    grad_layer = hidden_grad_share + inverse_one * (scaled - unit_share * row_mean[:, None])
-    norm_attn_part = lax.dynamic_update_slice_in_dim(
-        jnp.zeros((model_width,), F32), jnp.sum(grad_normed * unit_share, axis=0), start, 0
-    )
-    small = jnp.concatenate(
-        [norm_attn_part, norm_moe_part / tp_count, query_gain_part, key_gain_part]
-    )
-    small = lax.psum(small, ("ep", "tp"))
-    grad_norm_attn = lax.dynamic_slice_in_dim(small, ep_index * part, part, 0)
-    grad_norm_moe = lax.dynamic_slice_in_dim(small, model_width + ep_index * part, part, 0)
-    grad_query_gain = lax.dynamic_slice_in_dim(
-        small, 2 * model_width + ep_index * head_part, head_part, 0
-    )
-    grad_key_gain = lax.dynamic_slice_in_dim(
-        small, 2 * model_width + HEAD_DIM + ep_index * head_part, head_part, 0
-    )
-
-    back = jnp.concatenate([layer_dealt, grad_layer.astype(BF16)], axis=1)
-    home = exchange(dot_tn(recv, back).astype(BF16), ep_count)
-    home = dot_tn(send, home)
+    layer_out, layer_grad, d_query, d_key, d_value, d_out, sums = back_call(
+        gain_at,
+        ep_count,
+        tp_count,
+        (
+            grad_moe_in,
+            mixed_plane,
+            layer_full,
+            hidden,
+            grad_full,
+            normed,
+            proj,
+            turned,
+            key_flat,
+            value_flat,
+            probs,
+            context_low,
+            small_all,
+            cosine_wide,
+            sine_wide,
+            send,
+            recv,
+        ),
+        w_in_all,
+        full_out,
+    )
+    sums = jnp.sum(sums, axis=0)
+    head_at = 2 * part + ep_index * head_part
     return (
-        home[:, :share_width].astype(BF16),
-        home[:, share_width:],
-        grad_packed[:, :q_width],
-        grad_packed[:, 2 * q_width : 2 * q_width + kv_width],
-        grad_packed[:, 2 * q_width + kv_width :],
-        grad_packed[:, q_width : 2 * q_width],
-        grad_norm_attn,
-        grad_norm_moe,
-        grad_query_gain,
-        grad_key_gain,
+        layer_out,
+        layer_grad,
+        d_query,
+        d_key,
+        d_value,
+        d_out,
+        sums[:part],
+        sums[part : 2 * part],
+        lax.dynamic_slice_in_dim(sums, head_at, head_part, 0),
+        lax.dynamic_slice_in_dim(sums, head_at + HEAD_DIM, head_part, 0),
         grad_w_gate.reshape(w_gate.shape),
         grad_w_up.reshape(w_up.shape),
         grad_w_down.reshape(w_down.shape),

time: 457 us -> 347 us (0.76); the launches traced: 449 us -> 346 us
  Pallas kernels: 242 us -> 314 us
  waiting for transfers between devices: 51 us -> 0 us
  blocking collectives: 50.8 us -> 0 us
  other arithmetic: 42.4 us -> 10.7 us
  between operations: 14.5 us -> 0.8 us
  local copies, waits for them, and re-layouts: 31.5 us -> 18.9 us
  matrix products: 13.6 us -> 2.13 us
    pallas_call x0 -> x1, Pallas kernels: none -> 71.9 us  [back_call(): pl.pallas_call(functools.partial(back_body, gain_at, ep_count, tp_count,...]
    psum x2 -> x0, blocking collectives: 50.8 us -> none  [the longest x1 41.4 us: plane_layer(): small = lax.psum(small, ('ep', 'tp'))]
    reduce_scatter x3 -> x0, waiting for transfers between devices: 50.2 us -> none  [the longest x1 27.1 us: plane_layer(): lax.psum_scatter(grad_packed, 'ep', scatter_dimension=0, tiled=True)]
    concatenate x3 -> x0, other arithmetic: 16.3 us -> none  [the longest x1 15.7 us: plane_layer(): jnp.concatenate([dot_tn(normed, grad_query_proj).astype(BF16), grad_w_out...]
    dot_general x11 -> x0, matrix products: 10.2 us -> none  [the longest x5 4.64 us: dot_tn(): lax.dot_general(left_rows, right_rows, (((0,), (0,)), ((), ())), preferre...]
    reduce_sum x11 -> x1, other arithmetic: 8.07 us -> 0.85 us  [plane_layer(): sums = jnp.sum(sums, axis=0)]
    convert_element_type x7 -> x1, other arithmetic: 6.89 us -> 0.76 us  [deal_matrices(): send = (send_slot[None, :] == rows[:, None]).astype(BF16)]
    unnamed x60 -> x23, local copies, waits for them, and re-layouts: 20.1 us -> 14.6 us
  transfers between devices with their start and end apart: 4 -> 0, of which waited for: 3 -> 0; matrix products, arithmetic and copies ran while one was open for 7% -> 0% of each run, Pallas kernels for 0% -> 0%
where the time goes in v4:
time: 347 us; the launch traced here: 346 us
  Pallas kernels  314 us (90%)
  local copies, waits for them, and re-layouts  18.9 us (5%)
  other arithmetic  10.7 us (3%)
    pallas_call x1, Pallas kernels, front_call(): pl.pallas_call(functools.partial(front_body, gain_at, ep_count, tp_count,...  112 us
    pallas_call x1, Pallas kernels, expert_call(): pl.pallas_call(functools.partial(expert_body, flat, rows, parts), out_sha...  79.4 us
    pallas_call x1, Pallas kernels, back_call(): pl.pallas_call(functools.partial(back_body, gain_at, ep_count, tp_count,...  71.9 us
    pallas_call x1, Pallas kernels, mix_call(): pl.pallas_call(functools.partial(mix_body, tp_count, rows), out_shape=(wh...  50.1 us
    unnamed x23, local copies, waits for them, and re-layouts  14.6 us

profile of v4, /device:TPU:0, one launch (start us, length us, event | category | flops | bytes accessed | tf_op | source)
XLA Modules:
  0.0 346.2 jit_solution(4009394286082675711)
XLA Ops:
  0.7 1.1 select_reduce_fusion
  1.8 0.9 reduce_window_sum.11
  2.6 0.7 sub.38
  3.3 0.1 copy.30
  3.4 0.1 fusion.20
  3.5 0.1 copy.31
  3.6 0.1 fusion.21
  3.7 0.2 convert_reduce_fusion.1
  3.9 0.7 broadcast_in_dim.46
  4.6 0.8 and_select_fusion.1
  5.4 0.2 convert_reduce_fusion
  5.5 0.8 multiply_add_fusion
  6.3 0.1 add.97
  6.4 0.7 reshape_dynamic-update-slice_fusion
  7.1 0.8 dynamic_update_slice.14
  7.8 0.8 dynamic_update_slice.15
  8.6 0.8 select_reduce_fusion.1
  9.4 0.7 compare_convert_fusion.pick_ref
  10.1 0.7 fusion.14.small_ref
  10.8 0.8 fusion.13.mask_ref
  11.5 0.8 fusion.3
  12.3 0.5 fusion.17
  12.8 0.8 pad_maximum_fusion
  13.7 2.1 convolution_convert_fusion.send_ref
  15.8 112.4 %front.1 = (bf16[256,2048]{1,0:T(8,128)(2,1)}, bf16[256,2048]{1,0:T(8,128)(2,1)}, f32[256,2048]{1,0:T(8,128)}, bf16[256,2048]{1,0:T(8,128)(2,1)}, f32[256,1280]{...) custom-call(bf16[256,1024]{1,0:T(8,128)(2,1)} %convolution_convert_f, ...), custom_call_target="tpu_custom_call" | custom-call | tf_op jit(solution)/shard_map/front/pallas_call | solution.py:1027
  128.2 79.4 %experts.1 = (bf16[256,2048]{1,0:T(8,128)(2,1)}, bf16[2048,384]{1,0:T(8,128)(2,1)}, f32[384,2048]{1,0:T(8,128)}, f32[384,2048]{1,0:T(8,128)}, f32[384,2048]{1,0:T(8,128)}) custom-call(bf16[256,2048]{1,0:T(8,128)(2,1)} %get-tuple-element.42.own_hbm, bf16[2048,2048]{1,0:T(8,128)(2,1)} %get-tuple-element.43.grad_hbm, ...), custom_call_target="tpu_custom_call" | custom-call | tf_op jit(solution)/shard_map/experts/pallas_call | solution.py:521
  207.6 50.1 %mix.1 = (bf16[256,2048]{1,0:T(8,128)(2,1)}, bf16[256,2048]{1,0:T(8,128)(2,1)}) custom-call(bf16[256,2048]{1,0:T(8,128)(2,1)} %get-tuple-element.45.partial_ref, bf16[2048,384]{1,0:T(8,128)(2,1)} %get-tuple-element.46.active_ref, bf16[384,2048]{1,0:T(8,128)(2,1)} %bitcast.22), custom_call_target="tpu_custom_call" | custom-call | tf_op jit(solution)/shard_map/mix/pallas_call | solution.py:765
  257.7 71.9 %back.1 = (bf16[256,512]{1,0:T(8,128)(2,1)}, f32[256,512]{1,0:T(8,128)}, f32[256,1024]{1,0:T(8,128)}, f32[256,128]{1,0:T(8,128)}, f32[256,128]{1,0:T(8,128)}, /*index=5*/f32[256,1024]{1,0:T(8,128)}, f32[8,768]{1,0:T(8,128)}) custom-call(bf16[256,2048]{1,0:T(8,128)(2,1)} %get-tuple-element.47.grad_moe_ref, bf16[256,2048]{1,0:T(8,128)(2,1)} %get-tuple-element.48.mixed_ref, ...), custom_call_target="tpu_custom_call" | custom-call | tf_op jit(solution)/shard_map/back/pallas_call | solution.py:1418
  329.6 0.0 copy-start.4
  329.6 0.0 copy-start.6
  329.6 0.0 copy-start.5
  329.6 0.8 reduce_sum.69
  330.5 0.6 fusion.23
  331.1 0.6 fusion.24
  331.6 1.8 copy.44
  333.4 1.9 copy.45
  335.3 0.0 copy-done.4
  335.3 1.0 copy.46
  336.2 0.0 copy-done.6
  336.2 0.7 copy.47
  336.9 0.0 copy-done.5
  336.9 0.7 copy.48
  337.6 1.0 copy.49
  338.5 1.7 copy.50
  340.2 1.4 copy-done.1
  341.6 1.7 copy.51
  343.2 1.4 copy-done
  344.6 1.7 copy.52
  (17 shorter events, 0.1 us)
Async XLA Ops:
  329.6 5.7 %copy-start.4 = (f32[256,1024]{1,0:T(8,128)S(1)}, f32[256,1024]{1,0:T(8,128)}, u32[]{:S(2)}) copy-start(f32[256,1024]{1,0:T(8,128)} %get-tuple-element.100) | copy-start | bytes 3145732
  329.6 6.6 %copy-start.6 = (f32[256,128]{1,0:T(8,128)S(1)}, f32[256,128]{1,0:T(8,128)}, u32[]{:S(2)}) copy-start(f32[256,128]{1,0:T(8,128)} %get-tuple-element.101) | copy-start | bytes 393220
  329.6 7.3 %copy-start.5 = (f32[256,128]{1,0:T(8,128)S(1)}, f32[256,128]{1,0:T(8,128)}, u32[]{:S(2)}) copy-start(f32[256,128]{1,0:T(8,128)} %get-tuple-element.102) | copy-start | bytes 393220
  331.6 5.9 %copy-start.3 = (f32[256,1024]{1,0:T(8,128)S(1)}, f32[256,1024]{1,0:T(8,128)}, u32[]{:S(2)}) copy-start(f32[256,1024]{1,0:T(8,128)} %get-tuple-element.103) | copy-start | bytes 3145732
  335.3 3.3 copy-start.2
  338.5 3.0 copy-start.1
  341.6 3.0 copy-start

commit v5 on v4

--- a/solution.py
+++ b/solution.py
@@ -324,7 +324,7 @@
     up_hbm,
     down_hbm,
     total_ref,
-    active_hbm,
+    mixed_hbm,
     d_gate_hbm,
     d_up_hbm,
     d_down_hbm,
@@ -348,9 +348,13 @@
     sum_recv,
     gather_send,
     gather_recv,
+    mixed_near,
+    mixed_send,
+    mixed_recv,
     local_sem,
     grad_sem,
     out_sem,
+    mixed_sem,
 ):
     r = roles()
     half = rows // HALF
@@ -463,22 +467,10 @@
             def _():
                 psum.near_copy(6 + k).start()
 
-    active_out = pltpu.make_async_copy(active, active_hbm, local_sem.at[0])
-    active_out.start()
     psum.pass_far(0)
     psum.pass_far(1)
     group = 128
     pieces = flat // group
-
-    def weight_piece(which, index):
-        source, other, column = (
-            (active, grads, 0),
-            (grad_both, held, 0),
-            (grad_both, held, flat),
-        )[which]
-        lanes = pl.ds(pl.multiple_of(column + index * group, group), group)
-        place = pl.ds(pl.multiple_of(which * flat + index * group, group), group)
-        d_weights[place, :] = dot_tn(source[:, lanes], other[...])
 
     def weight_out(which):
         target = (d_down_hbm, d_gate_hbm, d_up_hbm)[which]
@@ -488,9 +480,27 @@
 
     @pl.loop(0, pieces)
     def _(index):
-        weight_piece(0, index)
+        place = pl.ds(pl.multiple_of(index * group, group), group)
+        d_weights[place, :] = dot_tn(active[:, place], grads[...]).astype(BF16)
 
     weight_out(0).start()
+
+    mixed = PlaneSum(
+        r, grads, mixed_near, None, None, None, half, (mixed_send, mixed_recv, None, None)
+    )
+
+    @pl.loop(0, 8)
+    def _(step):
+        index = (step + 6) % 8
+        at = pl.ds(pl.multiple_of(index * unit, unit), unit)
+        grads[at, :] = dot_nn(active[at, :], down[...]).astype(BF16)
+        for unit_done, copies in ((6, (6,)), (7, (7,)), (1, (0, 1)), (3, (2, 4)), (5, (3, 5))):
+
+            @pl.when(index == unit_done)
+            def _():
+                for copy in copies:
+                    mixed.near_copy(copy).start()
+
     psum.pass_first(0)
     psum.pass_first(1)
 
@@ -498,15 +508,32 @@
     def _(index):
         lanes = pl.ds(pl.multiple_of(index * group, group), group)
         place = pl.ds(pl.multiple_of(flat + index * group, group), group)
-        d_weights[place, :] = dot_tn(grad_both[:, lanes], held[...])
+        d_weights[place, :] = dot_tn(grad_both[:, lanes], held[...]).astype(BF16)
 
     weight_out(1).start()
     weight_out(2).start()
+    mixed_outs = []
+    for name in range(4):
+        for k in range(HALF):
+            slot, others = mixed.near_sum(name, k)
+            mixed.slot(slot)[...] = mixed.add_up(slot, others).astype(BF16)
+            index = HALF * name + k
+            mixed_outs.append(
+                pltpu.make_async_copy(
+                    mixed.slot(slot),
+                    mixed_hbm.at[pl.ds(index * half, half)],
+                    mixed_sem.at[index],
+                )
+            )
+            mixed_outs[-1].start()
     for k in range(HALF):
         total_ref[pl.ds(k * half, half), :] = psum.total(k).astype(BF16)
-    active_out.wait()
     for which in range(3):
         weight_out(which).wait()
+    for copy in mixed_outs:
+        copy.wait()
+    for index in range(4 * HALF):
+        mixed.near_copy(index).wait_send()
     gather.sent()
     psum.sent()
 
@@ -517,15 +544,15 @@
     everything = all_grad.shape[0]
     parts = pick.shape[0]
     half = rows // HALF
-    f32_weight = jax.ShapeDtypeStruct((flat, width), F32)
+    weight = jax.ShapeDtypeStruct((flat, width), BF16)
     return pl.pallas_call(
         functools.partial(expert_body, flat, rows, parts),
         out_shape=(
             jax.ShapeDtypeStruct((rows, width), BF16),
-            jax.ShapeDtypeStruct((everything, flat), BF16),
-            f32_weight,
-            f32_weight,
-            f32_weight,
+            jax.ShapeDtypeStruct((4 * rows, width), BF16),
+            weight,
+            weight,
+            weight,
         ),
         in_specs=[any_spec(), any_spec(), any_spec(), vmem_spec()] + [any_spec()] * 3,
         out_specs=(vmem_spec(), any_spec(), any_spec(), any_spec(), any_spec()),
@@ -538,16 +565,20 @@
             pltpu.VMEM((everything, flat), F32),
             pltpu.VMEM((everything, 2 * flat), BF16),
             pltpu.VMEM((everything, flat), BF16),
-            pltpu.VMEM((3 * flat, width), F32),
+            pltpu.VMEM((3 * flat, width), BF16),
             pltpu.VMEM((everything, width), BF16),
         ]
         + plane_sum_scratch(half, width)
         + [
             pltpu.SemaphoreType.DMA((PlaneGather.kinds, HALF)),
             pltpu.SemaphoreType.DMA((PlaneGather.kinds, HALF)),
+            pltpu.VMEM((4 * rows, width), BF16),
+            pltpu.SemaphoreType.DMA((4 * HALF,)),
+            pltpu.SemaphoreType.DMA((4 * HALF,)),
             pltpu.SemaphoreType.DMA((4,)),
             pltpu.SemaphoreType.DMA((2, 16)),
             pltpu.SemaphoreType.DMA((3,)),
+            pltpu.SemaphoreType.DMA((4 * HALF,)),
         ],
         compiler_params=comm_params(1),
         name="experts",
@@ -693,90 +724,45 @@
     return [(z + j) % count for j in range(1, count)]
 
 
-def mix_body(
-    tp_count,
-    rows,
-    partial_ref,
-    active_ref,
-    down_ref,
-    grad_ref,
-    mixed_ref,
-    part,
-    line,
-    near,
-    far,
-    first,
-    second,
-    near_send,
-    near_recv,
-    sum_send,
-    sum_recv,
-    line_send,
-    line_recv,
-    back_line,
-):
-    r = roles()
-    half = rows // HALF
-    unit = 2 * half
-    greet([r["p"], r["a"], r["b"]], line_peers(tp_count))
-    over_line = LineSum(tp_count, partial_ref, line, line_send, line_recv)
-    over_line.begin()
-    psum = PlaneSum(
-        r, part, near, far, first, second, half, (near_send, near_recv, sum_send, sum_recv)
-    )
-
-    @pl.loop(0, 8)
-    def _(step):
-        index = (step + 6) % 8
-        at = pl.ds(pl.multiple_of(index * unit, unit), unit)
-        part[at, :] = dot_nn(active_ref[at, :], down_ref[...]).astype(BF16)
-        for unit_done, copies in ((6, (6,)), (7, (7,)), (1, (0, 1)), (3, (2, 4)), (5, (3, 5))):
-
-            @pl.when(index == unit_done)
-            def _():
-                for copy in copies:
-                    psum.near_copy(copy).start()
-
-    for k in range(HALF):
-        psum.pass_far(k)
-    for k in range(HALF):
-        psum.pass_second(k)
-    for k in range(HALF):
-        psum.pass_first(k)
-    back = LineGather(tp_count, grad_ref, *[back_line.at[i] for i in range(4)])
-    grad_ref[:, back.columns(back.z)] = over_line.total().astype(BF16)
-    back.begin()
-    back.step(1)
-    back.step(2)
-    for k in range(HALF):
-        mixed_ref[pl.ds(k * half, half), :] = psum.total(k).astype(BF16)
-    back.step(3)
-    over_line.sent()
-    back.sent()
-    psum.sent()
-
-
-def mix_call(partial, active, down_matrix, tp_count):
-    rows, width = partial.shape
-    everything = active.shape[0]
-    half = rows // HALF
-    whole = jax.ShapeDtypeStruct((rows, width), BF16)
-    line_sems = pltpu.SemaphoreType.DMA((tp_count - 1,))
-    return pl.pallas_call(
-        functools.partial(mix_body, tp_count, rows),
-        out_shape=(whole, whole),
-        in_specs=[vmem_spec()] * 3,
-        out_specs=(vmem_spec(), vmem_spec()),
-        scratch_shapes=[
-            pltpu.VMEM((everything, width), BF16),
-            pltpu.VMEM((tp_count - 1, rows, width // tp_count), BF16),
-        ]
-        + plane_sum_scratch(half, width)
-        + [line_sems] * 2
-        + [pltpu.SemaphoreType.DMA((4, tp_count - 1))],
-        compiler_params=comm_params(2),
-        name="mix",
-    )(partial, active, down_matrix)
+class FarSum:
+    def __init__(self, r, part, far, first, second, half, send, recv):
+        self.r, self.part, self.half = r, part, half
+        self.far, self.first, self.second = far, first, second
+        self.send, self.recv = send, recv
+
+    def rows(self, buffer, index):
+        return buffer.at[pl.ds(index * self.half, self.half)]
+
+    def copy(self, kind, k):
+        block, target, device = (
+            (3, self.far, "b"),
+            (1, self.first, "a"),
+            (2, self.second, "b"),
+        )[kind]
+        return send_to(
+            self.rows(self.part, HALF * block + k),
+            self.rows(target, k),
+            self.send.at[kind, k],
+            self.recv.at[kind, k],
+            ep=self.r[device],
+        )
+
+    def pass_first(self, k):
+        self.copy(0, k).wait_recv()
+        block = self.rows(self.part, HALF + k)
+        block[...] = (block[...].astype(F32) + self.rows(self.far, k)[...].astype(F32)).astype(BF16)
+        self.copy(1, k).start()
+
+    def total(self, k):
+        self.copy(1, k).wait_recv()
+        self.copy(2, k).wait_recv()
+        total = self.rows(self.part, k)[...].astype(F32)
+        return total + self.rows(self.first, k)[...].astype(F32) + self.rows(self.second, k)[...].astype(F32)
+
+    def sent(self):
+        for kind in range(3):
+            for k in range(HALF):
+                self.copy(kind, k).wait_send()
 
 
 def turn(values, cosine, sine_table):
@@ -936,6 +922,13 @@
     ).astype(BF16)
     values_ref[...] = proj_ref[:, q_width + HEAD_DIM :].astype(BF16)
 
+    grad_gather.step(3)
+    grad_ref[...] = dot_nn(recv_ref[...], grad_wire[...]).astype(BF16)
+    grad_here = pltpu.make_async_copy(grad_ref, all_grad.at[own], local_sem.at[4])
+    grad_here.start()
+    grad_here.wait()
+    gather_grad.begin()
+
     @pl.loop(0, heads)
     def _(head):
         lanes = pl.ds(pl.multiple_of(head * HEAD_DIM, HEAD_DIM), HEAD_DIM)
@@ -946,7 +939,8 @@
             )
             turned_ref[at, :] = queries[micro * micro_rows : (micro + 1) * micro_rows]
 
-    grad_gather.step(3)
+    for k in range(HALF):
+        gather_out.pass_far(k)
     for micro in range(MICRO):
         within = slice(micro * micro_rows, (micro + 1) * micro_rows)
         stacked = slice(micro * heads * micro_rows, (micro + 1) * heads * micro_rows)
@@ -964,13 +958,6 @@
                 head * micro_rows : (head + 1) * micro_rows
             ]
 
-    grad_ref[...] = dot_nn(recv_ref[...], grad_wire[...]).astype(BF16)
-    grad_here = pltpu.make_async_copy(grad_ref, all_grad.at[own], local_sem.at[4])
-    grad_here.start()
-    for k in range(HALF):
-        gather_out.pass_far(k)
-    grad_here.wait()
-    gather_grad.begin()
     gather_out.finish()
 
     attn[...] = dot_nt(context_ref[...], w_out[...]).astype(BF16)
@@ -1106,35 +1093,59 @@
     tp_count,
     rows,
     heads,
-    grad_moe_ref,
-    mixed_ref,
-    x_ref,
-    hidden_ref,
-    grad_ref,
-    normed_ref,
-    proj_ref,
-    turned_ref,
-    keys_ref,
-    values_ref,
-    probs_ref,
-    context_ref,
-    small_all,
-    cosine_ref,
-    sine_ref,
-    send_ref,
-    recv_ref,
+    operand_count,
+    partial_ref,
+    mixed_hbm,
+    w_in_hbm,
+    w_out_hbm,
+    *rest,
+):
+    operand_hbm, rest = rest[:operand_count], rest[operand_count:]
+    outs, rest = rest[:5], rest[5:]
+    operand_refs, rest = rest[:operand_count], rest[operand_count:]
+    back_steps(
+        gain_at,
+        ep_count,
+        tp_count,
+        rows,
+        heads,
+        operand_hbm,
+        operand_refs,
+        partial_ref,
+        mixed_hbm,
+        w_in_hbm,
+        w_out_hbm,
+        *outs,
+        *rest,
+    )
+
+
+def back_steps(
+    gain_at,
+    ep_count,
+    tp_count,
+    rows,
+    heads,
+    operand_hbm,
+    operand_refs,
+    partial_ref,
+    mixed_hbm,
     w_in_hbm,
     w_out_hbm,
     layer_out,
     layer_grad,
-    d_query,
-    d_key,
-    d_value,
+    d_in,
     d_out,
     sums_out,
     w_in,
     w_out,
-    grad_hidden,
+    mixed_part,
+    mixed_far,
+    mixed_first,
+    mixed_second,
+    mixed_ref,
+    grad_moe_ref,
+    grad_line,
     grad_attn,
     stacked_grad,
     grad_turned,
@@ -1153,6 +1164,23 @@
     in_part,
     *rest,
 ):
+    (
+        x_ref,
+        hidden_ref,
+        grad_ref,
+        normed_ref,
+        proj_ref,
+        turned_ref,
+        keys_ref,
+        values_ref,
+        probs_ref,
+        context_ref,
+        small_all,
+        cosine_ref,
+        sine_ref,
+        send_ref,
+        recv_ref,
+    ) = operand_refs
     out_bufs, out_sems = rest[0:4], rest[4:8]
     in_bufs, in_sems = rest[8:12], rest[12:16]
     mixed_sems, normed_sems, row_sems, sum_sems, sum_line_sems, home_sems = (
@@ -1163,7 +1191,11 @@
         rest[24:26],
         rest[26:28],
     )
-    local_sem = rest[28]
+    far_sems, grad_sems, gather_sem, operand_sem, mixed_sem, local_sem = (
+        rest[28:30],
+        rest[30:32],
+        *rest[32:36],
+    )
     r = roles()
     e = r["e"]
     z = lax.axis_index("tp")
@@ -1178,11 +1210,44 @@
         pltpu.make_async_copy(w_out_hbm, w_out, local_sem.at[0]),
         pltpu.make_async_copy(w_in_hbm, w_in, local_sem.at[1]),
     ]
-    for load in loads:
+    blocks = [
+        pltpu.make_async_copy(
+            mixed_hbm.at[pl.ds(index * half, half)],
+            mixed_part.at[pl.ds(index * half, half)],
+            mixed_sem.at[index],
+        )
+        for index in range(4 * HALF)
+    ]
+    for index in (6, 7, 4, 5, 2, 3, 0, 1):
+        blocks[index].start()
+    operand_loads = [
+        pltpu.make_async_copy(source, target, operand_sem.at[index])
+        for index, (source, target) in enumerate(zip(operand_hbm, operand_refs))
+    ]
+    for load in operand_loads + loads:
         load.start()
     greet([(e + j) % ep_count for j in range(1, ep_count)], line_peers(tp_count))
+
+    grad_sum = LineSum(tp_count, partial_ref, grad_line, *grad_sems)
+    grad_sum.begin()
+    over_chips = FarSum(r, mixed_part, mixed_far, mixed_first, mixed_second, half, *far_sems)
+    for kind, block in ((0, 6), (2, 4)):
+        for k in range(HALF):
+            blocks[block + k].wait()
+            over_chips.copy(kind, k).start()
+    for index in range(4):
+        blocks[index].wait()
+    for load in operand_loads:
+        load.wait()
+    spread = LineGather(tp_count, grad_moe_ref, *[gather_sem.at[i] for i in range(4)])
+    grad_moe_ref[:, spread.columns(z)] = grad_sum.total().astype(BF16)
+    spread.begin()
+    spread.step(1)
+    over_chips.pass_first(0)
+    spread.step(2)
+    over_chips.pass_first(1)
+    spread.step(3)
     mixed_sum = LineSum(tp_count, mixed_ref, mixed_line, *mixed_sems)
-    mixed_sum.begin()
     out_sum = PlaneSum(r, out_part, *out_bufs, half, out_sems)
     in_sum = PlaneSum(r, in_part, *in_bufs, half, in_sems)
 
@@ -1197,10 +1262,10 @@
     moe_sums = fold(grad_moe * unit_two)
     gain_moe = jnp.concatenate([gain_row(place, rows, rows) for place in range(ep_count)], axis=1)
     scaled = grad_moe * gain_moe
-    grad_hidden[...] = grad_ref[...].astype(F32) + inverse_two * (
+    grad_hidden = grad_ref[...].astype(F32) + inverse_two * (
         scaled - unit_two * jnp.mean(scaled * unit_two, axis=-1, keepdims=True)
     )
-    grad_attn[...] = grad_hidden[...].astype(BF16)
+    grad_attn[...] = grad_hidden.astype(BF16)
     sums[...] = jnp.zeros_like(sums)
     for place in range(ep_count):
         sums[place * 8 : place * 8 + 8, rows : 2 * rows] = moe_sums[
@@ -1276,6 +1341,9 @@
     grad_proj[:, q_width : q_width + HEAD_DIM] = grad_key
     for k in range(HALF):
         out_sum.pass_first(k)
+    for k in range(HALF):
+        mixed_ref[pl.ds(k * half, half), :] = over_chips.total(k).astype(BF16)
+    mixed_sum.begin()
 
     def one_head(head, total):
         lanes = pl.ds(pl.multiple_of(head * HEAD_DIM, HEAD_DIM), HEAD_DIM)
@@ -1314,7 +1382,7 @@
     for k in range(HALF):
         in_sum.pass_second(k)
     for k in range(HALF):
-        d_out[pl.ds(k * half, half), :] = out_sum.total(k)
+        d_out[pl.ds(k * half, half), :] = out_sum.total(k).astype(BF16)
     for k in range(HALF):
         in_sum.pass_first(k)
 
@@ -1333,7 +1401,7 @@
         at = pl.multiple_of((z * places + place) * small_rows + gain_at, 16)
         gain_share.append(small_all[pl.ds(at, 16), :rows][:1].astype(F32))
     scaled = grad_normed * jnp.concatenate(gain_share, axis=1)
-    grad_rows = grad_hidden[:, lanes] + inverse_one * (scaled - unit_share * mean)
+    grad_rows = grad_attn[:, lanes].astype(F32) + inverse_one * (scaled - unit_share * mean)
     both = jnp.concatenate([layer_rows, grad_rows.astype(BF16)], axis=1)
     home_send[...] = dot_tn(recv_ref[...], both).astype(BF16)
     home = Straight(
@@ -1373,7 +1441,7 @@
         send_to(block, block, home_sems[0].at[j - 1], home_sems[1].at[j - 1], ep=source).wait_recv()
     arrived = dot_tn(send_ref[...], home_recv[...])
     layer_out[...] = arrived[:, :share].astype(BF16)
-    layer_grad[...] = arrived[:, share:]
+    layer_grad[...] = arrived[:, share:].astype(BF16)
     over_line.wait()
     line_sums = plane_sums
     for j in range(1, tp_count):
@@ -1382,12 +1450,11 @@
     sums_out[:, rows : 2 * rows] = plane_sums[:, rows : 2 * rows]
     sums_out[:, 2 * rows :] = line_sums[:, 2 * rows :]
     for k in range(HALF):
-        total = in_sum.total(k)
-        at = pl.ds(k * half, half)
-        d_query[at, :] = total[:, :q_width]
-        d_key[at, :] = total[:, q_width : q_width + HEAD_DIM]
-        d_value[at, :] = total[:, q_width + HEAD_DIM :]
+        d_in[pl.ds(k * half, half), :] = in_sum.total(k).astype(BF16)
     for op in (
+        grad_sum,
+        over_chips,
+        spread,
         mixed_sum,
         normed_sum,
         over_rows,
@@ -1400,9 +1467,8 @@
         op.sent()
 
 
-def back_call(gain_at, ep_count, tp_count, operands, w_in_all, w_out_all):
-    grad_moe, x = operands[0], operands[2]
-    rows, width = x.shape
+def back_call(gain_at, ep_count, tp_count, partial, mixed, w_in_all, w_out_all, operands):
+    rows, width = partial.shape
     share = width // tp_count
     in_width = w_in_all.shape[1]
     q_width = w_out_all.shape[1]
@@ -1416,22 +1482,27 @@
         return [pltpu.SemaphoreType.DMA((count,))] * 2
 
     return pl.pallas_call(
-        functools.partial(back_body, gain_at, ep_count, tp_count, rows, heads),
+        functools.partial(back_body, gain_at, ep_count, tp_count, rows, heads, len(operands)),
         out_shape=(
             shape((rows, share), BF16),
-            shape((rows, share), F32),
-            shape((rows, q_width), F32),
-            shape((rows, HEAD_DIM), F32),
-            shape((rows, HEAD_DIM), F32),
-            shape((rows, q_width), F32),
+            shape((rows, share), BF16),
+            shape((rows, in_width), BF16),
+            shape((rows, q_width), BF16),
             shape((8, sums_width), F32),
         ),
-        in_specs=[vmem_spec()] * len(operands) + [any_spec()] * 2,
-        out_specs=tuple([vmem_spec()] * 7),
-        scratch_shapes=[
+        in_specs=[vmem_spec()] + [any_spec()] * (3 + len(operands)),
+        out_specs=tuple([vmem_spec()] * 5),
+        scratch_shapes=[pltpu.VMEM(operand.shape, operand.dtype) for operand in operands]
+        + [
             pltpu.VMEM((everything, in_width), BF16),
             pltpu.VMEM((everything, q_width), BF16),
-            pltpu.VMEM((rows, width), F32),
+            pltpu.VMEM((4 * rows, width), BF16),
+            pltpu.VMEM((rows, width), BF16),
+            pltpu.VMEM((rows, width), BF16),
+            pltpu.VMEM((rows, width), BF16),
+            pltpu.VMEM((rows, width), BF16),
+            pltpu.VMEM((rows, width), BF16),
+            pltpu.VMEM((tp_count - 1, rows, share), BF16),
             pltpu.VMEM((rows, width), BF16),
             pltpu.VMEM((heads * rows, HEAD_DIM), BF16),
             pltpu.VMEM((heads * rows, HEAD_DIM), F32),
@@ -1455,10 +1526,17 @@
         + pair(ep_count - 1)
         + pair(tp_count - 1)
         + pair(ep_count - 1)
-        + [pltpu.SemaphoreType.DMA((2,))],
+        + [pltpu.SemaphoreType.DMA((3, HALF))] * 2
+        + pair(tp_count - 1)
+        + [
+            pltpu.SemaphoreType.DMA((4, tp_count - 1)),
+            pltpu.SemaphoreType.DMA((len(operands),)),
+            pltpu.SemaphoreType.DMA((4 * HALF,)),
+            pltpu.SemaphoreType.DMA((2,)),
+        ],
         compiler_params=comm_params(4),
         name="back",
-    )(*operands, w_in_all, w_out_all)
+    )(partial, mixed, w_in_all, w_out_all, *operands)
 
 
 def plain_layer(
@@ -1823,17 +1901,18 @@
     gate_matrix = w_gate.reshape(flat, model_width)
     up_matrix = w_up.reshape(flat, model_width)
     down_matrix = w_down.reshape(flat, model_width)
-    grad_partial, active, grad_w_gate, grad_w_up, grad_w_down = expert_call(
+    grad_partial, mixed_part, grad_w_gate, grad_w_up, grad_w_down = expert_call(
         moe_in, all_grad, small_all, pick, gate_matrix, up_matrix, down_matrix
     )
-    grad_moe_in, mixed_plane = mix_call(grad_partial, active, down_matrix, tp_count)
-    layer_out, layer_grad, d_query, d_key, d_value, d_out, sums = back_call(
+    layer_out, layer_grad, d_in, d_out, sums = back_call(
         gain_at,
         ep_count,
         tp_count,
+        grad_partial,
+        mixed_part,
+        w_in_all,
+        full_out,
         (
-            grad_moe_in,
-            mixed_plane,
             layer_full,
             hidden,
             grad_full,
@@ -1850,67 +1929,23 @@
             send,
             recv,
         ),
-        w_in_all,
-        full_out,
     )
     sums = jnp.sum(sums, axis=0)
     head_at = 2 * part + ep_index * head_part
     return (
         layer_out,
-        layer_grad,
-        d_query,
-        d_key,
-        d_value,
-        d_out,
+        layer_grad.astype(F32),
+        d_in[:, :q_width].astype(F32),
+        d_in[:, q_width : q_width + kv_width].astype(F32),
+        d_in[:, q_width + kv_width :].astype(F32),
+        d_out.astype(F32),
         sums[:part],
         sums[part : 2 * part],
         lax.dynamic_slice_in_dim(sums, head_at, head_part, 0),
         lax.dynamic_slice_in_dim(sums, head_at + HEAD_DIM, head_part, 0),
-        grad_w_gate.reshape(w_gate.shape),
-        grad_w_up.reshape(w_up.shape),
-        grad_w_down.reshape(w_down.shape),
-    )
-
-
-def solution(mesh):
-    return jax.shard_map(
-        on_device,
-        mesh=mesh,
-        in_specs=(
-            P("ep", "tp"),
-            P(),
-            P("ep", None),
-            P("ep", None),
-            P("ep", None),
-            P("ep", "tp"),
-            P("ep", "tp"),
-            P("ep", "tp"),
-            P("ep", "tp"),
-            P("ep"),
-            P("ep"),
-            P("ep"),
-            P("ep"),
-            P("ep", "tp", None),
-            P("ep", "tp", None),
-            P("ep", "tp", None),
-            P("ep", "tp"),
-        ),
-        out_specs=(
-            P("ep", "tp"),
-            P("ep", "tp"),
-            P("ep", "tp"),
-            P("ep", "tp"),
-            P("ep", "tp"),
-            P("ep", "tp"),
-            P("ep"),
-            P("ep"),
-            P("ep"),
-            P("ep"),
-            P("ep", "tp", None),
-            P("ep", "tp", None),
-            P("ep", "tp", None),
-        ),
-        check_vma=False,
+        grad_w_gate.astype(F32).reshape(w_gate.shape),
+        grad_w_up.astype(F32).reshape(w_up.shape),
+        grad_w_down.astype(F32).reshape(w_down.shape),
     )
 
 

time: 347 us -> 343 us (0.988)
  local copies, waits for them, and re-layouts: 18.9 us -> 5.03 us
  other arithmetic: 10.7 us -> 22.5 us
    pallas_call x1 -> x0, Pallas kernels: 50.1 us -> none  [mix_call(): pl.pallas_call(functools.partial(mix_body, tp_count, rows), out_shape=(wh...]
    pallas_call x1, Pallas kernels: 71.9 us -> 119 us  [back_call(): pl.pallas_call(functools.partial(back_body, gain_at, ep_count, tp_count,...]
    unnamed x23 -> x13, local copies, waits for them, and re-layouts: 14.6 us -> 0.73 us
    reshape x0 -> x3, other arithmetic: none -> 6.12 us  [the longest x1 2.04 us: plane_layer(): grad_w_gate.astype(F32).reshape(w_gate.shape)]
    convert_element_type x0 -> x4, other arithmetic: none -> 5.77 us  [the longest x1 2.13 us: plane_layer(): d_in[:, :q_width].astype(F32)]
where the time goes in v5:
time: 343 us
  Pallas kernels  312 us (91%)
  other arithmetic  22.5 us (7%)
  local copies, waits for them, and re-layouts  5.03 us (1%)
    pallas_call x1, Pallas kernels, back_call(): pl.pallas_call(functools.partial(back_body, gain_at, ep_count, tp_count,...  119 us
    pallas_call x1, Pallas kernels, front_call(): pl.pallas_call(functools.partial(front_body, gain_at, ep_count, tp_count,...  114 us
    pallas_call x1, Pallas kernels, expert_call(): pl.pallas_call(functools.partial(expert_body, flat, rows, parts), out_sha...  78.7 us

profile of v5, /device:TPU:0, one launch (start us, length us, event | category | flops | bytes accessed | tf_op | source)
XLA Modules:
  0.0 342.7 jit_solution(11195715204528904870)
XLA Ops:
  0.7 1.1 select_reduce_fusion
  1.8 0.9 reduce_window_sum.11
  2.6 0.7 sub.38
  3.3 0.1 copy.30
  3.4 0.1 fusion.20
  3.5 0.1 copy.31
  3.6 0.1 fusion.21
  3.7 0.2 convert_reduce_fusion.1
  3.9 0.7 broadcast_in_dim.46
  4.6 0.8 and_select_fusion.1
  5.4 0.2 convert_reduce_fusion
  5.5 0.8 multiply_add_fusion
  6.3 0.1 add.97
  6.4 0.7 reshape_dynamic-update-slice_fusion
  7.1 0.8 dynamic_update_slice.14
  7.8 0.8 dynamic_update_slice.15
  8.6 0.8 select_reduce_fusion.1
  9.4 0.7 compare_convert_fusion.pick_ref
  10.1 0.7 fusion.14.small_ref
  10.8 0.8 fusion.13.mask_ref
  11.5 0.8 fusion.3
  12.3 0.5 fusion.17
  12.8 0.8 pad_maximum_fusion
  13.7 2.1 convolution_convert_fusion.send_ref
  15.8 114.3 %front.1 = (bf16[256,2048]{1,0:T(8,128)(2,1)}, bf16[256,2048]{1,0:T(8,128)(2,1)}, f32[256,2048]{1,0:T(8,128)}, bf16[256,2048]{1,0:T(8,128)(2,1)}, f32[256,1280]{...) custom-call(bf16[256,1024]{1,0:T(8,128)(2,1)} %convolution_convert_f, ...), custom_call_target="tpu_custom_call" | custom-call | tf_op jit(solution)/shard_map/front/pallas_call | solution.py:1014
  130.1 78.7 %experts.1 = (bf16[256,2048]{1,0:T(8,128)(2,1)}, bf16[1024,2048]{1,0:T(8,128)(2,1)}, bf16[384,2048]{1,0:T(8,128)(2,1)}, bf16[384,2048]{1,0:T(8,128)(2,1)}, bf16[384,2048]{1,0:T(8,128)(2,1)}) custom-call(bf16[256,2048]{1,0:T(8,128)(2,1)} %get-tuple-element.38.own_hbm, bf16[2048,2048]{1,0:T(8,128)(2,1)} %get-tuple-element.39.grad_hbm, ...), custom_call_target="tpu_custom_call" | custom-call | tf_op jit(solution)/shard_map/experts/pallas_call | solution.py:548
  208.8 119.2 %back.1 = (bf16[256,512]{1,0:T(8,128)(2,1)}, bf16[256,512]{1,0:T(8,128)(2,1)}, bf16[256,1280]{1,0:T(8,128)(2,1)}, bf16[256,1024]{1,0:T(8,128)(2,1)}, f32[8,768]{1,0:T(8,128)}) custom-call(bf16[256,2048]{1,0:T(8,128)(2,1)} %get-tuple-element.41.partial_ref, bf16[1024,2048]{1,0:T(8,128)(2,1)} %get-tuple-element.42.mixed_hbm, ...), custom_call_target="tpu_custom_call" | custom-call | tf_op jit(solution)/shard_map/back/pallas_call | solution.py:1484
  328.1 0.0 copy-start.4
  328.1 0.0 copy-start.3
  328.1 0.8 reduce_sum.69
  328.9 0.6 fusion.23
  329.5 0.6 fusion.24
  330.1 0.0 copy-start.2
  330.1 1.7 slice_convert_fusion.1
  331.8 2.1 slice_convert_fusion
  333.9 0.0 copy-done.4
  333.9 0.9 convert_element_type.68
  334.8 0.0 copy-done.3
  334.8 1.1 convert_element_type.72
  335.9 0.0 copy-done.2
  335.9 0.0 copy-start.1
  335.9 2.0 convert.15
  337.9 0.0 copy-done.1
  337.9 2.0 convert.16
  339.9 0.0 copy-done
  339.9 2.0 convert.17
  342.0 0.0 copy-done.5
  342.0 0.7 copy.36
  (13 shorter events, 0.1 us)
Async XLA Ops:
  328.1 5.8 %copy-start.4 = (bf16[256,512]{1,0:T(8,128)(2,1)S(1)}, bf16[256,512]{1,0:T(8,128)(2,1)}, u32[]{:S(2)}) copy-start(bf16[256,512]{1,0:T(8,128)(2,1)} %get-tuple-element.56) | copy-start | bytes 786436
  328.1 6.7 %copy-start.3 = (bf16[256,1024]{1,0:T(8,128)(2,1)S(1)}, bf16[256,1024]{1,0:T(8,128)(2,1)}, u32[]{:S(2)}) copy-start(bf16[256,1024]{1,0:T(8,128)(2,1)} %get-tuple-element.58) | copy-start | bytes 1572868
  330.1 5.8 %copy-start.2 = (bf16[384,2048]{1,0:T(8,128)(2,1)S(1)}, bf16[384,2048]{1,0:T(8,128)(2,1)}, u32[]{:S(2)}) copy-start(bf16[384,2048]{1,0:T(8,128)(2,1)} %get-tuple-element.60) | copy-start | bytes 4718596
  335.9 2.0 copy-start.1
  337.9 2.0 copy-start
  339.9 2.0 copy-start.5

commit v6 on v5

--- a/solution.py
+++ b/solution.py
@@ -12,7 +12,7 @@
 F32 = jnp.float32
 BF16 = jnp.bfloat16
 SCALE_TERMS = 3
-VMEM_LIMIT = 66 * 1000 * 1000
+VMEM_LIMIT = 67 * 1000 * 1000
 
 epsilon = 1e-06
 rope_base = 1000000.0
@@ -113,6 +113,7 @@
 
 MESH_ID = pl.DeviceIdType.MESH
 HALF = 2
+LINE_CHUNKS = 16
 E0, E1, P0, P1, A0, B0, PA0, PB0, A1, B1, PA1, PB1, D0, PD0, D1, PD1 = range(16)
 SLOT_E, SLOT_P, SLOT_A, SLOT_B = (E0, E1), (P0, P1), (A0, A1), (B0, B1)
 SLOT_D, SLOT_PA, SLOT_PB, SLOT_PD = (D0, D1), (PA0, PA1), (PB0, PB1), (PD0, PD1)
@@ -586,7 +587,7 @@
 
 
 class LineSum:
-    def __init__(self, count, source, arrived, send, recv):
+    def __init__(self, count, source, arrived, send, recv, parts=1):
         self.count, self.source, self.arrived, self.send, self.recv = (
             count,
             source,
@@ -596,34 +597,127 @@
         )
         self.z = lax.axis_index("tp")
         self.share = source.shape[1] // count
+        self.parts, self.part = parts, source.shape[0] // parts
 
     def columns(self, z):
         return pl.ds(pl.multiple_of(z * self.share, self.share), self.share)
 
-    def copy(self, j):
+    def copy(self, j, k):
         target = (self.z + j) % self.count
+        rows = pl.ds(k * self.part, self.part)
         return send_to(
-            self.source.at[:, self.columns(target)],
-            self.arrived.at[j - 1],
-            self.send.at[j - 1],
-            self.recv.at[j - 1],
+            self.source.at[rows, self.columns(target)],
+            self.arrived.at[j - 1, rows],
+            self.send.at[k, j - 1],
+            self.recv.at[k, j - 1],
             tp=target,
         )
 
-    def begin(self):
+    def begin(self, k=0):
         for j in range(1, self.count):
-            self.copy(j).start()
+            self.copy(j, k).start()
 
     def total(self):
+        for k in range(self.parts):
+            for j in range(1, self.count):
+                self.copy(j, k).wait_recv()
         total = self.source[:, self.columns(self.z)].astype(F32)
         for j in range(1, self.count):
-            self.copy(j).wait_recv()
             total = total + self.arrived[j - 1].astype(F32)
         return total
 
     def sent(self):
-        for j in range(1, self.count):
-            self.copy(j).wait_send()
+        for k in range(self.parts):
+            for j in range(1, self.count):
+                self.copy(j, k).wait_send()
+
+
+class LineTotal:
+    def __init__(self, count, chunks, source, up_in, down_in, up_out, down_out, sems):
+        self.count, self.chunks, self.source = count, chunks, source
+        self.landed, self.onward, self.sems = (up_in, down_in), (up_out, down_out), sems
+        self.z = lax.axis_index("tp")
+        self.rows = source.shape[0] // chunks
+
+    def copy(self, way, chunk, buffer, device):
+        at = pl.ds(pl.multiple_of(chunk * self.rows, self.rows), self.rows)
+        return send_to(
+            buffer.at[at],
+            self.landed[way].at[at],
+            self.sems.at[way, 0, chunk],
+            self.sems.at[way, 1, chunk],
+            tp=device,
+        )
+
+    def is_first(self, way):
+        return self.z == (0, self.count - 1)[way]
+
+    def sends(self, way):
+        return self.z != (self.count - 1, 0)[way]
+
+    def begin(self):
+        for way, ahead in ((0, 1), (1, -1)):
+
+            @pl.when(self.is_first(way))
+            def _():
+                self.landed[way][...] = jnp.zeros_like(self.landed[way])
+
+                @pl.loop(0, self.chunks)
+                def _(chunk):
+                    self.copy(way, chunk, self.source, self.z + ahead).start()
+
+    def forward(self, way, chunk):
+        ahead = (1, -1)[way]
+        at = pl.ds(pl.multiple_of(chunk * self.rows, self.rows), self.rows)
+
+        @pl.when(jnp.logical_not(self.is_first(way)))
+        def _():
+            self.copy(way, chunk, self.onward[way], self.z - ahead).wait_recv()
+
+            @pl.when(self.sends(way))
+            def _():
+                self.onward[way][at, :] = (
+                    self.landed[way][at, :].astype(F32) + self.source[at, :].astype(F32)
+                ).astype(BF16)
+                self.copy(way, chunk, self.onward[way], self.z + ahead).start()
+
+    def run(self, beside):
+        lower = self.z < self.count // 2
+
+        @pl.loop(0, self.chunks + 1)
+        def _(step):
+            for ahead, is_here in ((0, lower), (1, jnp.logical_not(lower))):
+
+                @pl.when(is_here & (step < self.chunks))
+                def _():
+                    self.forward(ahead, step)
+
+                @pl.when(is_here & (step > 0))
+                def _():
+                    self.forward(1 - ahead, step - 1)
+
+            for at, action in beside:
+
+                @pl.when(step == at)
+                def _():
+                    action()
+
+    def total(self):
+        total = self.source[...].astype(F32) + self.landed[0][...].astype(F32)
+        return total + self.landed[1][...].astype(F32)
+
+    def sent(self):
+        for way, ahead in ((0, 1), (1, -1)):
+
+            @pl.when(self.sends(way))
+            def _():
+                @pl.loop(0, self.chunks)
+                def _(chunk):
+                    self.copy(way, chunk, self.source, self.z + ahead).wait_send()
+
+
+def line_total_scratch(rows, width):
+    return [pltpu.VMEM((rows, width), BF16)] * 4 + [pltpu.SemaphoreType.DMA((2, 2, LINE_CHUNKS))]
 
 
 class OrderedGather(PlaneGather):
@@ -809,9 +903,12 @@
     dealt,
     x_wire,
     grad_wire,
-    back_wire,
     attn,
-    line,
+    up_in,
+    down_in,
+    up_out,
+    down_out,
+    total_sems,
     deal_send,
     deal_recv,
     small_send,
@@ -824,9 +921,6 @@
     grad_recv,
     x_line,
     grad_line,
-    back_line,
-    line_send,
-    line_recv,
     local_sem,
 ):
     r = roles()
@@ -922,12 +1016,6 @@
     ).astype(BF16)
     values_ref[...] = proj_ref[:, q_width + HEAD_DIM :].astype(BF16)
 
-    grad_gather.step(3)
-    grad_ref[...] = dot_nn(recv_ref[...], grad_wire[...]).astype(BF16)
-    grad_here = pltpu.make_async_copy(grad_ref, all_grad.at[own], local_sem.at[4])
-    grad_here.start()
-    grad_here.wait()
-    gather_grad.begin()
 
     @pl.loop(0, heads)
     def _(head):
@@ -958,27 +1046,30 @@
                 head * micro_rows : (head + 1) * micro_rows
             ]
 
+    grad_gather.step(3)
+    grad_ref[...] = dot_nn(recv_ref[...], grad_wire[...]).astype(BF16)
+    grad_here = pltpu.make_async_copy(grad_ref, all_grad.at[own], local_sem.at[4])
+    grad_here.start()
+    grad_here.wait()
+    gather_grad.begin()
     gather_out.finish()
 
     attn[...] = dot_nt(context_ref[...], w_out[...]).astype(BF16)
-    over_line = LineSum(tp_count, attn, line, line_send, line_recv)
+    over_line = LineTotal(tp_count, LINE_CHUNKS, attn, up_in, down_in, up_out, down_out, total_sems)
     over_line.begin()
     w_in_out = pltpu.make_async_copy(w_in, w_in_hbm, local_sem.at[0])
     w_out_out = pltpu.make_async_copy(w_out, w_out_hbm, local_sem.at[1])
     w_in_out.start()
     w_out_out.start()
-    gather_grad.pass_near(0)
-    total = over_line.total()
-    back = LineGather(tp_count, back_wire, *[back_line.at[i] for i in range(4)])
-    back_wire[:, back.columns(z)] = total.astype(BF16)
-    back.begin()
-    back.step(1)
-    gather_grad.pass_near(1)
-    back.step(2)
+    over_line.run(
+        (
+            (LINE_CHUNKS * 5 // 8, lambda: gather_grad.pass_near(0)),
+            (LINE_CHUNKS, lambda: gather_grad.pass_near(1)),
+        )
+    )
+    hidden = x_ref[...].astype(F32) + over_line.total()
+    hidden_ref[...] = hidden
     gather_grad.pass_far(0)
-    back.step(3)
-    hidden = x_ref[...].astype(F32) + back_wire[...].astype(F32)
-    hidden_ref[...] = hidden
     unit_two = unit_of(hidden)
     for place in range(ep_count):
         at = slice(place * rows, (place + 1) * rows)
@@ -989,7 +1080,6 @@
         deal(j, e, (e + j) % ep_count).wait_send()
     x_gather.sent()
     grad_gather.sent()
-    back.sent()
     over_line.sent()
     for gather in (gather_small, gather_in, gather_out, gather_grad):
         gather.sent()
@@ -1039,14 +1129,11 @@
             pltpu.VMEM((rows, width), BF16),
             pltpu.VMEM((rows, width), BF16),
             pltpu.VMEM((rows, width), BF16),
-            pltpu.VMEM((rows, width), BF16),
-            pltpu.VMEM((tp_count - 1, rows, share), BF16),
-            pltpu.SemaphoreType.DMA((ep_count - 1,)),
-            pltpu.SemaphoreType.DMA((ep_count - 1,)),
         ]
+        + line_total_scratch(rows, width)
+        + [pltpu.SemaphoreType.DMA((ep_count - 1,))] * 2
         + [gather_sems] * 8
-        + [line_sems] * 3
-        + [pltpu.SemaphoreType.DMA((tp_count - 1,))] * 2
+        + [line_sems] * 2
         + [pltpu.SemaphoreType.DMA((5,))],
         compiler_params=comm_params(3),
         name="front",
@@ -1144,8 +1231,11 @@
     mixed_first,
     mixed_second,
     mixed_ref,
-    grad_moe_ref,
-    grad_line,
+    up_in,
+    down_in,
+    up_out,
+    down_out,
+    total_sems,
     grad_attn,
     stacked_grad,
     grad_turned,
@@ -1191,11 +1281,7 @@
         rest[24:26],
         rest[26:28],
     )
-    far_sems, grad_sems, gather_sem, operand_sem, mixed_sem, local_sem = (
-        rest[28:30],
-        rest[30:32],
-        *rest[32:36],
-    )
+    far_sems, operand_sem, mixed_sem, local_sem = (rest[28:30], *rest[30:33])
     r = roles()
     e = r["e"]
     z = lax.axis_index("tp")
@@ -1218,7 +1304,7 @@
         )
         for index in range(4 * HALF)
     ]
-    for index in (6, 7, 4, 5, 2, 3, 0, 1):
+    for index in (6, 4, 7, 5, 2, 3, 0, 1):
         blocks[index].start()
     operand_loads = [
         pltpu.make_async_copy(source, target, operand_sem.at[index])
@@ -1228,26 +1314,32 @@
         load.start()
     greet([(e + j) % ep_count for j in range(1, ep_count)], line_peers(tp_count))
 
-    grad_sum = LineSum(tp_count, partial_ref, grad_line, *grad_sems)
+    grad_sum = LineTotal(
+        tp_count, LINE_CHUNKS, partial_ref, up_in, down_in, up_out, down_out, total_sems
+    )
     grad_sum.begin()
     over_chips = FarSum(r, mixed_part, mixed_far, mixed_first, mixed_second, half, *far_sems)
-    for kind, block in ((0, 6), (2, 4)):
-        for k in range(HALF):
+    for k in range(HALF):
+        for kind, block in ((0, 6), (2, 4)):
             blocks[block + k].wait()
             over_chips.copy(kind, k).start()
     for index in range(4):
         blocks[index].wait()
+    mixed_sum = LineSum(tp_count, mixed_ref, mixed_line, *mixed_sems, HALF)
+
+    def mixed_half(k):
+        mixed_ref[pl.ds(k * half, half), :] = over_chips.total(k).astype(BF16)
+        mixed_sum.begin(k)
+
+    grad_sum.run(
+        (
+            (LINE_CHUNKS // 4, lambda: over_chips.pass_first(0)),
+            (LINE_CHUNKS * 5 // 8, lambda: over_chips.pass_first(1)),
+        )
+    )
+    mixed_half(0)
     for load in operand_loads:
         load.wait()
-    spread = LineGather(tp_count, grad_moe_ref, *[gather_sem.at[i] for i in range(4)])
-    grad_moe_ref[:, spread.columns(z)] = grad_sum.total().astype(BF16)
-    spread.begin()
-    spread.step(1)
-    over_chips.pass_first(0)
-    spread.step(2)
-    over_chips.pass_first(1)
-    spread.step(3)
-    mixed_sum = LineSum(tp_count, mixed_ref, mixed_line, *mixed_sems)
     out_sum = PlaneSum(r, out_part, *out_bufs, half, out_sems)
     in_sum = PlaneSum(r, in_part, *in_bufs, half, in_sems)
 
@@ -1258,7 +1350,7 @@
     hidden = hidden_ref[...]
     inverse_two = lax.rsqrt(jnp.mean(hidden * hidden, axis=-1, keepdims=True) + epsilon)
     unit_two = hidden * inverse_two
-    grad_moe = grad_moe_ref[...].astype(F32)
+    grad_moe = grad_sum.total()
     moe_sums = fold(grad_moe * unit_two)
     gain_moe = jnp.concatenate([gain_row(place, rows, rows) for place in range(ep_count)], axis=1)
     scaled = grad_moe * gain_moe
@@ -1307,6 +1399,7 @@
         out_sum.pass_far(k)
     for k in range(HALF):
         out_sum.pass_second(k)
+    mixed_half(1)
 
     cosine, sine_table = cosine_ref[...], -sine_ref[...]
     column = 2 * rows
@@ -1341,9 +1434,6 @@
     grad_proj[:, q_width : q_width + HEAD_DIM] = grad_key
     for k in range(HALF):
         out_sum.pass_first(k)
-    for k in range(HALF):
-        mixed_ref[pl.ds(k * half, half), :] = over_chips.total(k).astype(BF16)
-    mixed_sum.begin()
 
     def one_head(head, total):
         lanes = pl.ds(pl.multiple_of(head * HEAD_DIM, HEAD_DIM), HEAD_DIM)
@@ -1454,7 +1544,6 @@
     for op in (
         grad_sum,
         over_chips,
-        spread,
         mixed_sum,
         normed_sum,
         over_rows,
@@ -1501,8 +1590,9 @@
             pltpu.VMEM((rows, width), BF16),
             pltpu.VMEM((rows, width), BF16),
             pltpu.VMEM((rows, width), BF16),
-            pltpu.VMEM((rows, width), BF16),
-            pltpu.VMEM((tp_count - 1, rows, share), BF16),
+        ]
+        + line_total_scratch(rows, width)
+        + [
             pltpu.VMEM((rows, width), BF16),
             pltpu.VMEM((heads * rows, HEAD_DIM), BF16),
             pltpu.VMEM((heads * rows, HEAD_DIM), F32),
@@ -1522,14 +1612,14 @@
         ]
         + plane_sum_scratch(half, q_width)
         + plane_sum_scratch(half, in_width)
-        + pair(tp_count - 1) * 3
+        + [pltpu.SemaphoreType.DMA((HALF, tp_count - 1))] * 2
+        + [pltpu.SemaphoreType.DMA((1, tp_count - 1))] * 2
+        + pair(tp_count - 1)
         + pair(ep_count - 1)
         + pair(tp_count - 1)
         + pair(ep_count - 1)
         + [pltpu.SemaphoreType.DMA((3, HALF))] * 2
-        + pair(tp_count - 1)
         + [
-            pltpu.SemaphoreType.DMA((4, tp_count - 1)),
             pltpu.SemaphoreType.DMA((len(operands),)),
             pltpu.SemaphoreType.DMA((4 * HALF,)),
             pltpu.SemaphoreType.DMA((2,)),

time: 343 us -> 337 us (0.983)
  Pallas kernels: 312 us -> 306 us
    pallas_call x1, Pallas kernels: 119 us -> 113 us  [back_call(): pl.pallas_call(functools.partial(back_body, gain_at, ep_count, tp_count,...]
where the time goes in v6:
time: 337 us; the launch traced here: 336 us
  Pallas kernels  306 us (91%)
  other arithmetic  22.5 us (7%)
  local copies, waits for them, and re-layouts  5.03 us (1%)
    pallas_call x1, Pallas kernels, front_call(): pl.pallas_call(functools.partial(front_body, gain_at, ep_count, tp_count,...  114 us
    pallas_call x1, Pallas kernels, back_call(): pl.pallas_call(functools.partial(back_body, gain_at, ep_count, tp_count,...  113 us
    pallas_call x1, Pallas kernels, expert_call(): pl.pallas_call(functools.partial(expert_body, flat, rows, parts), out_sha...  79 us

profile of v6, /device:TPU:0, one launch (start us, length us, event | category | flops | bytes accessed | tf_op | source)
XLA Modules:
  0.0 336.2 jit_solution(16115628805279053960)
XLA Ops:
  0.7 1.1 select_reduce_fusion
  1.8 0.9 reduce_window_sum.11
  2.6 0.7 sub.38
  3.3 0.1 copy.30
  3.4 0.1 fusion.20
  3.5 0.1 copy.31
  3.6 0.1 fusion.21
  3.7 0.2 convert_reduce_fusion.1
  3.9 0.7 broadcast_in_dim.46
  4.6 0.8 and_select_fusion.1
  5.4 0.2 convert_reduce_fusion
  5.5 0.8 multiply_add_fusion
  6.3 0.1 add.97
  6.4 0.7 reshape_dynamic-update-slice_fusion
  7.1 0.8 dynamic_update_slice.14
  7.8 0.8 dynamic_update_slice.15
  8.6 0.8 select_reduce_fusion.1
  9.4 0.7 compare_convert_fusion.pick_ref
  10.1 0.7 fusion.14.small_ref
  10.8 0.8 fusion.13.mask_ref
  11.5 0.8 fusion.3
  12.3 0.5 fusion.17
  12.8 0.8 pad_maximum_fusion
  13.7 2.1 convolution_convert_fusion.send_ref
  15.8 114.1 %front.1 = (bf16[256,2048]{1,0:T(8,128)(2,1)}, bf16[256,2048]{1,0:T(8,128)(2,1)}, f32[256,2048]{1,0:T(8,128)}, bf16[256,2048]{1,0:T(8,128)(2,1)}, f32[256,1280]{...) custom-call(bf16[256,1024]{1,0:T(8,128)(2,1)} %convolution_convert_f, ...), custom_call_target="tpu_custom_call" | custom-call | tf_op jit(solution)/shard_map/front/pallas_call | solution.py:1104
  129.9 79.0 %experts.1 = (bf16[256,2048]{1,0:T(8,128)(2,1)}, bf16[1024,2048]{1,0:T(8,128)(2,1)}, bf16[384,2048]{1,0:T(8,128)(2,1)}, bf16[384,2048]{1,0:T(8,128)(2,1)}, bf16[384,2048]{1,0:T(8,128)(2,1)}) custom-call(bf16[256,2048]{1,0:T(8,128)(2,1)} %get-tuple-element.38.own_hbm, bf16[2048,2048]{1,0:T(8,128)(2,1)} %get-tuple-element.39.grad_hbm, ...), custom_call_target="tpu_custom_call" | custom-call | tf_op jit(solution)/shard_map/experts/pallas_call | solution.py:549
  209.0 112.6 %back.1 = (bf16[256,512]{1,0:T(8,128)(2,1)}, bf16[256,512]{1,0:T(8,128)(2,1)}, bf16[256,1280]{1,0:T(8,128)(2,1)}, bf16[256,1024]{1,0:T(8,128)(2,1)}, f32[8,768]{1,0:T(8,128)}) custom-call(bf16[256,2048]{1,0:T(8,128)(2,1)} %get-tuple-element.41.partial_ref, bf16[1024,2048]{1,0:T(8,128)(2,1)} %get-tuple-element.42.mixed_hbm, ...), custom_call_target="tpu_custom_call" | custom-call | tf_op jit(solution)/shard_map/back/pallas_call | solution.py:1573
  321.5 0.0 copy-start.4
  321.6 0.0 copy-start.3
  321.6 0.8 reduce_sum.69
  322.4 0.6 fusion.23
  323.0 0.6 fusion.24
  323.6 0.0 copy-start.2
  323.6 1.7 slice_convert_fusion.1
  325.3 2.1 slice_convert_fusion
  327.4 0.0 copy-done.4
  327.4 0.9 convert_element_type.68
  328.2 0.0 copy-done.3
  328.3 1.1 convert_element_type.72
  329.3 0.0 copy-done.2
  329.3 0.0 copy-start.1
  329.3 2.0 convert.15
  331.4 0.0 copy-done.1
  331.4 2.0 convert.16
  333.4 0.0 copy-done
  333.4 2.0 convert.17
  335.5 0.0 copy-done.5
  335.5 0.7 copy.36
  (13 shorter events, 0.1 us)
Async XLA Ops:
  321.5 5.8 %copy-start.4 = (bf16[256,512]{1,0:T(8,128)(2,1)S(1)}, bf16[256,512]{1,0:T(8,128)(2,1)}, u32[]{:S(2)}) copy-start(bf16[256,512]{1,0:T(8,128)(2,1)} %get-tuple-element.56) | copy-start | bytes 786436
  321.6 6.7 %copy-start.3 = (bf16[256,1024]{1,0:T(8,128)(2,1)S(1)}, bf16[256,1024]{1,0:T(8,128)(2,1)}, u32[]{:S(2)}) copy-start(bf16[256,1024]{1,0:T(8,128)(2,1)} %get-tuple-element.58) | copy-start | bytes 1572868
  323.6 5.8 %copy-start.2 = (bf16[384,2048]{1,0:T(8,128)(2,1)S(1)}, bf16[384,2048]{1,0:T(8,128)(2,1)}, u32[]{:S(2)}) copy-start(bf16[384,2048]{1,0:T(8,128)(2,1)} %get-tuple-element.60) | copy-start | bytes 4718596
  329.3 2.0 copy-start.1
  331.4 2.0 copy-start
  333.4 2.0 copy-start.5
